TPU v7x, 32 devices: a whole 2x2x4 slice. The times are simulated.
32 devices in a mesh: grp: 4 (over z), dev: 8 (over y, x, core).
Axes of the slice: x: 2, y: 2, z: 4, core: 2. Of those that a mesh axis runs over, the one named last changes fastest.
Arguments:
- positions: float32 [3, 128, 544], P(None, ('grp', 'dev')), may hold values from -2 to 20, as said below
- rest_shape: float32 [3, 544], replicated, may hold values from -3 to 3
- stiffness: float32 [544, 544], replicated, may hold values from -0.25 to 0.25
- up_map: float32 [544, 152], replicated, may hold values from -0.25 to 0.25
- down_map: float32 [152, 544], replicated, may hold values from -0.5 to 0.5
- m2m: float32 [152, 152], replicated, may hold values from -0.5 to 0.5
- box_template: float32 [3, 152], replicated, may hold values from -1 to 1
- near_target: int32 [32, 2], P(('grp', 'dev')), may hold values from 0 to 3
- near_owner: int32 [32, 2], P(('grp', 'dev')), may hold values from 0 to 7, as said below
- near_cell: int32 [32, 2], P(('grp', 'dev')), may hold values from 0 to 3, as said below
- near_count: int32 [32], P(('grp', 'dev')), may hold values from 1 to 2, as said below
Outputs:
- new_positions: float32 [3, 128, 544], P(None, ('grp', 'dev'))
- velocity: float32 [3, 128, 544], P(None, ('grp', 'dev'))
Inputs may be any that keep to these rules, and one draw needn't show every extreme that they name: `positions`: each cell's points lie within about 1.2 of the cell's center; devices of one group sit on a grid of spacing 2.5, groups are 6 apart. `near_owner`: device e's slots name devices of e's own group other than e itself; at most 2 used slots of one device name the same owner, and device 0 uses all 2 slots with exactly 2 on each owner it names. `near_cell`: the source cells named by one device's used slots are distinct. `near_count`: the used slots come first; device 0 uses all of them.
All inputs are finite; a program needn't handle non-finite values.
Results may differ from a plain program's by a relative error of at most 0.0003.
Values sent between devices are 32-bit elements; how exact they have to be, the bound alone decides.
No kernel may reach another device: no remote copies, remote signals or barrier semaphores. Data moves between devices by JAX's collectives and lax.ppermute only.
A program may use at most 64 MiB of HBM per device.

v0:
```python
import jax
import jax.numpy as jnp
from jax import lax
from jax.sharding import PartitionSpec as P

NEAR = 2
STEPS = 2


EPSILON_SQ = 0.25
VISCOSITY = 0.039788735772973836
TIME_STEP = 0.1
SKALAK_HARDEN = 2.0
CHECK_RADIUS = 1.0
DEVICE_RADIUS = 1.5
GROUP_RADIUS = 6.0


def stokes(targets, sources, forces):
    delta_x = targets[0][:, None] - sources[0][None, :]
    delta_y = targets[1][:, None] - sources[1][None, :]
    delta_z = targets[2][:, None] - sources[2][None, :]
    square = delta_x * delta_x + delta_y * delta_y + delta_z * delta_z
    inverse = 1.0 / ((square + EPSILON_SQ) * jnp.sqrt(square + EPSILON_SQ))
    direct = (square + 2.0 * EPSILON_SQ) * inverse
    projected = (
        delta_x * forces[0][None, :] + delta_y * forces[1][None, :] + delta_z * forces[2][None, :]
    ) * inverse
    result = jnp.einsum("ts,ks->kt", direct, forces, precision=lax.Precision.HIGHEST)
    extra = jnp.stack(
        [
            jnp.sum(delta_x * projected, axis=1),
            jnp.sum(delta_y * projected, axis=1),
            jnp.sum(delta_z * projected, axis=1),
        ]
    )
    return VISCOSITY * (result + extra)


def membrane(points, rest_shape, stiffness):
    centroid = jnp.mean(points, axis=2, keepdims=True)
    strain = points - centroid - rest_shape[:, None, :]
    linear = jnp.dot(
        strain.reshape(-1, strain.shape[2]), stiffness, precision=lax.Precision.HIGHEST
    ).reshape(strain.shape)
    stretch = jnp.sum(linear * linear, axis=0)
    return -linear * (1.0 + SKALAK_HARDEN * stretch / (1.0 + stretch))


def box_far(checks, equivalents, centers, radius, weights, box_template):
    sources = centers[:, :, None] + radius * box_template[None]
    forces = equivalents * weights.astype(equivalents.dtype)[:, None, None]
    source_count = equivalents.shape[0] * equivalents.shape[2]
    flat_sources = jnp.transpose(sources, (1, 0, 2)).reshape(3, source_count)
    flat_forces = jnp.transpose(forces, (1, 0, 2)).reshape(3, source_count)
    return stokes(checks, flat_sources, flat_forces)


def body(
    positions,
    rest_shape,
    stiffness,
    up_map,
    down_map,
    m2m,
    box_template,
    near_target,
    near_owner,
    near_cell,
    near_count,
):
    own_device = lax.axis_index("dev")
    own_group = lax.axis_index("grp")
    dev_count = lax.axis_size("dev")
    cell_count = positions.shape[1]
    slot_ids = jnp.arange(NEAR, dtype=jnp.int32)
    owners = near_owner[0]
    cell_ids = near_cell[0]
    targets = near_target[0]
    in_use = slot_ids < near_count[0]
    onehot = (
        (targets[:, None] == jnp.arange(cell_count, dtype=jnp.int32)[None, :]) & in_use[:, None]
    ).astype(jnp.float32)
    source_rows = owners * cell_count + cell_ids
    points = positions
    velocity = jnp.zeros_like(positions)
    for step_index in range(STEPS):
        forces = membrane(points, rest_shape, stiffness)
        stacked = jnp.concatenate([points, forces], axis=0)
        source_pool = lax.all_gather(stacked, "dev", axis=1, tiled=True)
        sources = jnp.take(source_pool, source_rows, axis=1)
        receivers = jnp.take(points, targets, axis=1)
        near_tiles = jax.vmap(stokes, in_axes=(1, 1, 1), out_axes=1)(
            receivers, sources[:3], sources[3:]
        )
        near_velocity = jnp.einsum(
            "ksp,sc->kcp", near_tiles, onehot, precision=lax.Precision.HIGHEST
        )
        equivalent = jnp.dot(jnp.sum(forces, axis=1), up_map, precision=lax.Precision.HIGHEST)
        center = jnp.mean(points, axis=(1, 2))
        checks = center[:, None] + CHECK_RADIUS * box_template
        box_forces = lax.all_gather(equivalent[None], "dev", axis=0, tiled=True)
        places = lax.all_gather(center[None], "dev", axis=0, tiled=True)
        indices = jnp.arange(box_forces.shape[0], dtype=jnp.int32)
        added = box_far(
            checks, box_forces, places, DEVICE_RADIUS, indices != own_device, box_template
        )
        equivalent_sum = jnp.sum(box_forces, axis=0)
        center_sum = jnp.sum(places, axis=0)
        group_eq = jnp.dot(equivalent_sum, m2m, precision=lax.Precision.HIGHEST)
        group_center = center_sum / dev_count
        outer_box_forces = lax.all_gather(group_eq[None], "grp", axis=0, tiled=True)
        outer_places = lax.all_gather(group_center[None], "grp", axis=0, tiled=True)
        outer_indices = jnp.arange(outer_box_forces.shape[0], dtype=jnp.int32)
        outer_far = box_far(
            checks,
            outer_box_forces,
            outer_places,
            GROUP_RADIUS,
            outer_indices != own_group,
            box_template,
        )
        far_checks = added + outer_far
        far_surface = jnp.dot(far_checks, down_map, precision=lax.Precision.HIGHEST)
        velocity = far_surface[:, None, :] + near_velocity
        points = points + TIME_STEP * velocity
    return (points, velocity)


def solution(mesh):
    return jax.shard_map(
        body,
        mesh=mesh,
        in_specs=(
            P(None, ("grp", "dev"), None),
            P(),
            P(),
            P(),
            P(),
            P(),
            P(),
            P(("grp", "dev"), None),
            P(("grp", "dev"), None),
            P(("grp", "dev"), None),
            P(("grp", "dev")),
        ),
        out_specs=(P(None, ("grp", "dev"), None), P(None, ("grp", "dev"), None)),
        check_vma=False,
    )
```

profile of v0, /device:TPU:0, one launch (start us, length us, event | category | flops | bytes accessed | tf_op | source)
XLA Modules:
  0.0 156.4 jit_solution(3233264386179120395)
XLA Ops:
  0.7 1.4 dynamic-slice
  2.7 0.9 fusion.199
  3.6 0.1 broadcast_multiply_fusion.5
  3.7 0.8 broadcast_multiply_fusion
  4.4 15.1 %all-reduce = f32[24]{0:T(128)S(1)} all-reduce(f32[24]{0:T(128)S(1)} %get-tuple-element.90), channel_id=3, replica_groups=mesh['grp'=4,'dev'=8] {'dev'}, use_global_device_ids=true, to_apply=%add | all-reduce | flops 24 | bytes 192
  19.5 0.1 reshape.238
  19.6 0.1 copy.42
  19.8 0.1 sub.330
  19.9 0.1 sub.335
  20.1 1.6 %multiply_reduce_fusion.1 = (f32[4,544]{1,0:T(4,128)S(1)}, f32[3,4,544]{2,1,0:T(4,128)S(1)}) fusion(f32[544,544]{1,0:T(8,128)S(1)} %copy-done, f32[3,4,544]{2,1,0:T(4,128)} %param.15, f32[3,544]{1,0:T(4,128)} %param.16, f32[3,4]{1,0:T(4,128)S(1)} %broadcast_multiply_fusion.3), kind=kOutput, calls=%fused_computation.219 | convolution fusion | flops 42638720 | bytes 1251248 | tf_op jit(solution)/shard_map/dot_general | solution.py:43
  21.8 0.5 convolution_bitcast_fusion.1
  22.3 8.1 %all-gather.8 = f32[8,3,152]{2,1,0:T(4,128)S(1)} all-gather(f32[1,3,152]{2,1,0:T(4,128)S(1)} %convolution_bitcast_fusion.1), channel_id=2, replica_groups=mesh['grp'=4,'dev'=8] {'dev'}, dimensions={0}, use_global_device_ids=true | all-gather | bytes 16416 | tf_op jit(solution)/shard_map/all_gather | solution.py:102
  30.4 0.1 fusion.205
  30.6 0.1 mul.464
  30.8 1.1 fusion.81
  31.9 0.1 reshape.201
  32.0 1.3 convolution_add_fusion.5
  33.4 0.6 dynamic-slice.1
  34.6 0.1 multiply_dynamic-update-slice_fusion.1
  34.7 11.9 %all-reduce.1 = f32[12]{0:T(128)S(1)} all-reduce(f32[12]{0:T(128)S(1)} %multiply_dynamic-update-slice_fusion.1), channel_id=5, replica_groups=mesh['grp'=4,'dev'=8] {'grp'}, use_global_device_ids=true, to_apply=%add.1 | all-reduce | flops 12 | bytes 96
  46.6 0.1 reshape.240
  46.7 0.1 copy.44
  46.9 0.1 sub.344
  47.1 0.2 convolution_bitcast_fusion.3
  47.3 13.2 %all-gather.9 = f32[4,3,152]{2,1,0:T(4,128)S(1)} all-gather(f32[1,3,152]{2,1,0:T(4,128)S(1)} %convolution_bitcast_fusion.3), channel_id=4, replica_groups=mesh['grp'=4,'dev'=8] {'grp'}, dimensions={0}, use_global_device_ids=true | all-gather | bytes 9120 | tf_op jit(solution)/shard_map/all_gather | solution.py:112
  60.9 0.7 fusion.107
  61.7 0.1 reshape.202
  61.8 0.8 fusion.73
  62.6 0.3 fusion.213
  63.0 10.3 %all_gather.34 = f32[6,32,544]{2,0,1:T(8,128)S(1)} all-gather(f32[6,4,544]{2,0,1:T(8,128)S(1)} %copy.45), channel_id=1, replica_groups=mesh['grp'=4,'dev'=8] {'dev'}, dimensions={1}, use_global_device_ids=true | all-gather | bytes 470016 | tf_op jit(solution)/shard_map/all_gather | solution.py:90
  73.3 0.6 gather_fusion
  74.1 0.6 gather_fusion.1
  74.8 4.4 %fusion.7 = (f32[2,544]{1,0:T(2,128)S(1)}, f32[2,544]{1,0:T(2,128)S(1)}, f32[2,544]{1,0:T(2,128)S(1)}) fusion(f32[2,544]{1,0:T(2,128)S(1)} %get-tuple-element.103, f32[2,544]{1,0:T(2,128)S(1)} %get-tuple-element.69, f32[2,544]{1,0:T(2,128)S(1)} %get-tuple-element.98, f32[2,544]{1,0:T(2,128)S(1)} %get-tuple-element.101, f32[2,544]{1,0:T(2,128)S(1)} %get-tuple-element.70, ...), kind=kLoop, calls=%fused_computation.31 | loop fusion | flops 13609792 | bytes 52224 | tf_op jit(solution)/shard_map/vmap()/reduce_sum | solution.py:32
  79.2 4.6 %fusion.67 = f32[3,2,544]{2,0,1:T(4,128)S(1)} fusion(f32[2,544]{1,0:T(2,128)S(1)} %get-tuple-element.101, f32[2,544]{1,0:T(2,128)S(1)} %get-tuple-element.70, f32[2,544]{1,0:T(2,128)S(1)} %get-tuple-element.102, f32[2,544]{1,0:T(2,128)S(1)} %get-tuple-element.71, f32[2,544]{1,0:T(2,128)S(1)} %get-tuple-element.103, f32[2,544]{1,0:T(2,128)S(1)} %get-tuple-element.69, ...), kind=kOutput, calls=%fused_computation.99 | convolution fusion | flops 29014784 | bytes 79616 | tf_op jit(solution)/shard_map/vmap(ts,ks->kt)/dot_general | solution.py:29
  84.5 0.4 fusion.198
  84.9 0.9 multiply_reduce_fusion
  85.9 0.5 convolution_bitcast_fusion
  86.3 8.1 %all-gather.10 = f32[8,3,152]{2,1,0:T(4,128)S(1)} all-gather(f32[1,3,152]{2,1,0:T(4,128)S(1)} %convolution_bitcast_fusion), channel_id=6, replica_groups=mesh['grp'=4,'dev'=8] {'dev'}, dimensions={0}, use_global_device_ids=true | all-gather | bytes 16416 | tf_op jit(solution)/shard_map/all_gather | solution.py:102
  94.5 0.2 convolution_bitcast_fusion.2
  94.7 13.2 %all-gather.11 = f32[4,3,152]{2,1,0:T(4,128)S(1)} all-gather(f32[1,3,152]{2,1,0:T(4,128)S(1)} %convolution_bitcast_fusion.2), channel_id=8, replica_groups=mesh['grp'=4,'dev'=8] {'grp'}, dimensions={0}, use_global_device_ids=true | all-gather | bytes 9120 | tf_op jit(solution)/shard_map/all_gather | solution.py:112
  108.3 0.1 broadcast_multiply_fusion.4
  108.4 11.8 %all-reduce.2 = f32[24]{0:T(128)S(1)} all-reduce(f32[24]{0:T(128)S(1)} %get-tuple-element.88), channel_id=7, replica_groups=mesh['grp'=4,'dev'=8] {'dev'}, use_global_device_ids=true, to_apply=%add.2 | all-reduce | flops 24 | bytes 192
  120.1 0.1 reshape.242
  120.3 0.1 multiply_dynamic-update-slice_fusion
  120.4 8.6 %all-reduce.3 = f32[12]{0:T(128)S(1)} all-reduce(f32[12]{0:T(128)S(1)} %multiply_dynamic-update-slice_fusion), channel_id=9, replica_groups=mesh['grp'=4,'dev'=8] {'grp'}, use_global_device_ids=true, to_apply=%add.3 | all-reduce | flops 12 | bytes 96
  128.9 0.1 reshape.244
  129.0 0.1 copy.50
  129.2 0.1 sub.389
  129.5 0.7 fusion.118
  130.3 0.1 mul.529
  130.6 0.1 copy.48
  130.8 0.1 sub.375
  131.0 1.1 fusion.92
  132.1 0.1 reshape.203
  132.2 1.3 convolution_add_fusion.4
  133.5 0.1 reshape.204
  133.6 0.8 fusion.71
  134.4 0.3 fusion.214
  134.8 10.1 %all_gather.39 = f32[6,32,544]{2,0,1:T(8,128)S(1)} all-gather(f32[6,4,544]{2,0,1:T(8,128)S(1)} %copy.51), channel_id=1, replica_groups=mesh['grp'=4,'dev'=8] {'dev'}, dimensions={1}, use_global_device_ids=true | all-gather | bytes 470016 | tf_op jit(solution)/shard_map/all_gather | solution.py:90
  145.0 0.5 gather_fusion.2
  145.7 0.6 gather_fusion.3
  146.4 4.4 %fusion.18 = (f32[2,544]{1,0:T(2,128)S(1)}, f32[2,544]{1,0:T(2,128)S(1)}, f32[2,544]{1,0:T(2,128)S(1)}) fusion(f32[2,544]{1,0:T(2,128)S(1)} %bitcast.162, f32[2,544]{1,0:T(2,128)S(1)} %bitcast.171, f32[2,544]{1,0:T(2,128)S(1)} %bitcast.164, f32[2,544]{1,0:T(2,128)S(1)} %bitcast.158, f32[2,544]{1,0:T(2,128)S(1)} %bitcast.167, f32[2,544]{1,0:T(2,128)S(1)} %bitcast.165, ...), kind=kLoop, calls=%fused_computation.42 | loop fusion | flops 13609792 | bytes 52224 | tf_op jit(solution)/shard_map/vmap()/reduce_sum | solution.py:32
  150.9 4.6 %fusion.61 = f32[3,2,544]{2,0,1:T(4,128)S(1)} fusion(f32[2,544]{1,0:T(2,128)S(1)} %bitcast.159, f32[2,544]{1,0:T(2,128)S(1)} %bitcast.168, f32[2,544]{1,0:T(2,128)S(1)} %bitcast.161, f32[2,544]{1,0:T(2,128)S(1)} %bitcast.170, f32[2,544]{1,0:T(2,128)S(1)} %bitcast.163, f32[2,544]{1,0:T(2,128)S(1)} %bitcast.172, f32[6,2,544]{2,0,1:T(8,128)S(1)} %select_bitcast_fusion, ...), kind=kOutput, calls=%fused_computation.97 | convolution fusion | flops 29014784 | bytes 79616 | tf_op jit(solution)/shard_map/vmap(ts,ks->kt)/dot_general | solution.py:29
  155.4 0.9 multiply_add_fusion
  (112 shorter events, 3.1 us)
Async XLA Ops:
  0.6 19.5 %copy-start = (f32[544,544]{1,0:T(8,128)S(1)}, f32[544,544]{1,0:T(8,128)}, u32[]{:S(2)}) copy-start(f32[544,544]{1,0:T(8,128)} %param.17) | copy-start | bytes 3551236
  0.6 21.1 %copy-start.1 = (f32[544,152]{0,1:T(8,128)S(1)}, f32[544,152]{0,1:T(8,128)}, u32[]{:S(2)}) copy-start(f32[544,152]{0,1:T(8,128)} %param.18) | copy-start | bytes 992260
  32.0 1.3 copy-start.10
  32.0 15.1 %copy-start.4 = (f32[152,152]{1,0:T(8,128)S(1)}, f32[152,152]{1,0:T(8,128)}, u32[]{:S(2)}) copy-start(f32[152,152]{1,0:T(8,128)} %param.20) | copy-start | bytes 277252
  60.9 1.7 %copy-start.2 = (f32[152,544]{1,0:T(8,128)S(1)}, f32[152,544]{1,0:T(8,128)}, u32[]{:S(2)}) copy-start(f32[152,544]{1,0:T(8,128)} %param.19) | copy-start | bytes 992260
  61.7 1.2 copy-start.3
  61.8 11.6 %copy-start.7 = (s32[1,2]{1,0:T(1,128)S(1)}, s32[1,2]{1,0:T(1,128)}, u32[]{:S(2)}) copy-start(s32[1,2]{1,0:T(1,128)} %param.24) | copy-start | bytes 28
  61.8 11.5 %copy-start.8 = (s32[1,2]{1,0:T(1,128)S(1)}, s32[1,2]{1,0:T(1,128)}, u32[]{:S(2)}) copy-start(s32[1,2]{1,0:T(1,128)} %param.23) | copy-start | bytes 28
  62.6 11.4 %copy-start.9 = (s32[1,2]{1,0:T(1,128)S(1)}, s32[1,2]{1,0:T(1,128)}, u32[]{:S(2)}) copy-start(s32[1,2]{1,0:T(1,128)} %param.22) | copy-start | bytes 28
  79.2 5.7 %copy-start.5 = (f32[3,544]{1,0:T(4,128)S(1)}, f32[3,544]{1,0:T(4,128)}, u32[]{:S(2)}) copy-start(f32[3,544]{1,0:T(4,128)} %param.16) | copy-start | bytes 19588
  83.8 45.6 %copy-start.6 = (f32[3,152]{1,0:T(4,128)S(1)}, f32[3,152]{1,0:T(4,128)}, u32[]{:S(2)}) copy-start(f32[3,152]{1,0:T(4,128)} %param.21) | copy-start | bytes 5476
where the time goes:
time: 157 us; the launch traced here: 156 us
  blocking collectives  111 us (71%)
  matrix products  19.1 us (12%)
  other arithmetic  15.7 us (10%)
  local copies, waits for them, and re-layouts  7.79 us (5%)
  between operations  3.27 us (2%)
    unnamed x4, blocking collectives  47.4 us
    all_gather x2, blocking collectives, body(): outer_box_forces = lax.all_gather(group_eq[None], 'grp', axis=0, tiled=True)  26.5 us
    all_gather x2, blocking collectives, body(): source_pool = lax.all_gather(stacked, 'dev', axis=1, tiled=True)  20.4 us
    all_gather x2, blocking collectives, body(): box_forces = lax.all_gather(equivalent[None], 'dev', axis=0, tiled=True)  16.2 us
    dot_general x6, matrix products, stokes(): jnp.einsum('ts,ks->kt', direct, forces, precision=lax.Precision.HIGHEST)  13.4 us
    reduce_sum x6, other arithmetic, stokes(): jnp.sum(delta_x * projected, axis=1)  12.5 us

commit v1 on v0

--- a/solution.py
+++ b/solution.py
@@ -81,41 +81,50 @@
     onehot = (
         (targets[:, None] == jnp.arange(cell_count, dtype=jnp.int32)[None, :]) & in_use[:, None]
     ).astype(jnp.float32)
-    source_rows = owners * cell_count + cell_ids
     points = positions
     velocity = jnp.zeros_like(positions)
+    groups = lax.axis_size("grp")
+    q = up_map.shape[1]
     for step_index in range(STEPS):
-        forces = membrane(points, rest_shape, stiffness)
-        stacked = jnp.concatenate([points, forces], axis=0)
-        source_pool = lax.all_gather(stacked, "dev", axis=1, tiled=True)
-        sources = jnp.take(source_pool, source_rows, axis=1)
+        pool = lax.all_to_all(
+            jnp.broadcast_to(points[None], (dev_count,) + points.shape), "dev", 0, 0
+        )
+        sources = pool[owners, :, cell_ids]
+        source_points = jnp.transpose(sources, (1, 0, 2))
+        source_forces = membrane(source_points, rest_shape, stiffness)
         receivers = jnp.take(points, targets, axis=1)
         near_tiles = jax.vmap(stokes, in_axes=(1, 1, 1), out_axes=1)(
-            receivers, sources[:3], sources[3:]
+            receivers, source_points, source_forces
         )
         near_velocity = jnp.einsum(
             "ksp,sc->kcp", near_tiles, onehot, precision=lax.Precision.HIGHEST
         )
+        forces = membrane(points, rest_shape, stiffness)
         equivalent = jnp.dot(jnp.sum(forces, axis=1), up_map, precision=lax.Precision.HIGHEST)
         center = jnp.mean(points, axis=(1, 2))
         checks = center[:, None] + CHECK_RADIUS * box_template
-        box_forces = lax.all_gather(equivalent[None], "dev", axis=0, tiled=True)
-        places = lax.all_gather(center[None], "dev", axis=0, tiled=True)
-        indices = jnp.arange(box_forces.shape[0], dtype=jnp.int32)
+        message = jnp.concatenate([equivalent.reshape(-1), center])
+        size = -(-message.shape[0] // 512) * 512
+        message = jnp.pad(message, (0, size - message.shape[0]))
+        told = lax.all_to_all(
+            jnp.broadcast_to(message[None], (groups * dev_count, size)), ("grp", "dev"), 0, 0
+        )
+        all_forces = told[:, : 3 * q].reshape(groups, dev_count, 3, q)
+        all_places = told[:, 3 * q : 3 * q + 3].reshape(groups, dev_count, 3)
+        box_forces = all_forces[own_group]
+        places = all_places[own_group]
+        indices = jnp.arange(dev_count, dtype=jnp.int32)
         added = box_far(
             checks, box_forces, places, DEVICE_RADIUS, indices != own_device, box_template
         )
-        equivalent_sum = jnp.sum(box_forces, axis=0)
-        center_sum = jnp.sum(places, axis=0)
-        group_eq = jnp.dot(equivalent_sum, m2m, precision=lax.Precision.HIGHEST)
-        group_center = center_sum / dev_count
-        outer_box_forces = lax.all_gather(group_eq[None], "grp", axis=0, tiled=True)
-        outer_places = lax.all_gather(group_center[None], "grp", axis=0, tiled=True)
-        outer_indices = jnp.arange(outer_box_forces.shape[0], dtype=jnp.int32)
+        group_eq = jnp.dot(
+            jnp.sum(all_forces, axis=1).reshape(groups * 3, q), m2m, precision=lax.Precision.HIGHEST
+        ).reshape(groups, 3, q)
+        outer_indices = jnp.arange(groups, dtype=jnp.int32)
         outer_far = box_far(
             checks,
-            outer_box_forces,
-            outer_places,
+            group_eq,
+            jnp.mean(all_places, axis=1),
             GROUP_RADIUS,
             outer_indices != own_group,
             box_template,

time: 157 us -> 78.4 us (0.50)
  blocking collectives: 111 us -> 0 us
  starting transfers between devices: 0 us -> 17.7 us
  waiting for transfers between devices: 0 us -> 12.7 us
  matrix products: 19.1 us -> 20.9 us
    all_gather x6 -> x0, blocking collectives: 63.1 us -> none  [the longest x2 26.5 us: body(): outer_box_forces = lax.all_gather(group_eq[None], 'grp', axis=0, tiled=True)]
    unnamed x4 -> x0, blocking collectives: 47.4 us -> none
    all_to_all x0 -> x4, starting transfers between devices: none -> 17.7 us  [the longest x2 10.7 us: body(): lax.all_to_all(jnp.broadcast_to(message[None], (groups * dev_count, size)...]
    all_to_all x0 -> x4, waiting for transfers between devices: none -> 12.7 us  [the longest x2 12.5 us: body(): lax.all_to_all(jnp.broadcast_to(message[None], (groups * dev_count, size)...]
    broadcast_in_dim x0 -> x4, local copies, waits for them, and re-layouts: none -> 2.76 us  [the longest x2 1.43 us: body(): jnp.broadcast_to(points[None], (dev_count,) + points.shape)]
    dot_general x2 -> x4, matrix products: 2.51 us -> 4.22 us  [membrane(): jnp.dot(strain.reshape(-1, strain.shape[2]), stiffness, precision=lax.Pre...]
  transfers between devices with their start and end apart: 0 -> 4, of which waited for: 0 -> 3; matrix products, arithmetic and copies ran while one was open for 0% -> 18% of each run, Pallas kernels for 0% -> 0%
where the time goes in v1:
time: 78.4 us; the launch traced here: 77.8 us
  matrix products  20.9 us (27%)
  starting transfers between devices  17.7 us (23%)
  other arithmetic  15.2 us (19%)
  waiting for transfers between devices  12.7 us (16%)
  local copies, waits for them, and re-layouts  9.27 us (12%)
  between operations  2.05 us (3%)
    dot_general x6, matrix products, stokes(): jnp.einsum('ts,ks->kt', direct, forces, precision=lax.Precision.HIGHEST)  13.4 us
    reduce_sum x6, other arithmetic, stokes(): jnp.sum(delta_x * projected, axis=1)  12.7 us
    all_to_all x2, waiting for transfers between devices, body(): lax.all_to_all(jnp.broadcast_to(message[None], (groups * dev_count, size)...  12.5 us
    all_to_all x2, starting transfers between devices, body(): lax.all_to_all(jnp.broadcast_to(message[None], (groups * dev_count, size)...  10.7 us
    all_to_all x2, starting transfers between devices, body(): lax.all_to_all(jnp.broadcast_to(points[None], (dev_count,) + points.shape...  7.03 us
    dot_general x4, matrix products, membrane(): jnp.dot(strain.reshape(-1, strain.shape[2]), stiffness, precision=lax.Pre...  4.22 us
  transfers between devices with their start and end apart: 4, of which 3 were waited for; matrix products, arithmetic and copies ran while one was open for 18% of the time, Pallas kernels for 0%

profile of v1, /device:TPU:0, one launch (start us, length us, event | category | flops | bytes accessed | tf_op | source)
XLA Modules:
  0.0 77.8 jit_solution(397613314308246547)
XLA Ops:
  0.7 1.0 %fusion.227 = (f32[3,4]{1,0:T(4,128)S(1)}, f32[3]{0:T(128)S(1)}) fusion(f32[3,4,544]{2,1,0:T(4,128)} %param.13), kind=kLoop, calls=%fused_computation.348 | loop fusion | flops 13041 | bytes 26172 | tf_op jit(solution)/shard_map/reduce_sum | solution.py:41
  1.7 0.5 copy-done
  2.1 1.6 %multiply_reduce_fusion.3 = (f32[4,544]{1,0:T(4,128)S(1)}, f32[3,4,544]{2,1,0:T(4,128)S(1)}) fusion(f32[544,544]{1,0:T(8,128)S(1)} %copy-done, f32[3,4,544]{2,1,0:T(4,128)} %param.13, f32[3,544]{1,0:T(4,128)} %param.14, f32[3,4]{1,0:T(4,128)S(1)} %broadcast_multiply_fusion.3), kind=kOutput, calls=%fused_computation.222 | convolution fusion | flops 42638720 | bytes 1251248 | tf_op jit(solution)/shard_map/dot_general | solution.py:43
  3.9 0.5 fusion.243
  4.3 0.1 reshape.285
  4.4 0.1 select_maximum_fusion.1
  4.5 0.7 broadcast_in_dim.17
  5.2 7.3 %all-to-all-start = ((f32[32,1,512]{2,1,0:T(1,128)}), f32[32,1,512]{2,1,0:T(1,128)S(1)}, u32[]{:S(2)}, u32[]{:S(2)}) async-start(f32[32,1,512]{2,1,0:T(1,128)} %broadcast_in_dim.17), calls=%async_computation | async-start | bytes 131072 | tf_op jit(solution)/shard_map/all_to_all | solution.py:109
  12.7 0.6 gather_fusion.2
  14.1 5.9 %all-to-all-done = f32[32,1,512]{2,1,0:T(1,128)S(1)} async-done(((f32[32,1,512]{2,1,0:T(1,128)}), f32[32,1,512]{2,1,0:T(1,128)S(1)}, u32[]{:S(2)}, u32[]{:S(2)}) %all-to-all-start) | async-done | bytes 65568 | tf_op jit(solution)/shard_map/all_to_all | solution.py:109
  19.9 0.7 broadcast_in_dim.18
  20.6 3.4 %all-to-all-start.1 = ((f32[8,3,4,544]{3,2,1,0:T(4,128)}), f32[8,3,4,544]{3,2,1,0:T(4,128)S(1)}, u32[]{:S(2)}, u32[]{:S(2)}) async-start(f32[8,3,4,544]{3,2,1,0:T(4,128)} %broadcast_in_dim.18), calls=%async_computation.1 | async-start | bytes 491520 | tf_op jit(solution)/shard_map/all_to_all | solution.py:89
  24.1 0.1 reshape.286
  24.4 0.1 reshape.287
  24.5 0.1 fusion.224
  24.6 0.2 fusion.75
  24.8 0.1 reshape.289
  24.9 0.1 copy.58
  25.1 0.1 sub.360
  25.8 0.1 copy.76
  26.0 0.1 sub.374
  26.2 1.1 %fusion.87 = (f32[152]{0:T(256)S(1)}, f32[152]{0:T(256)S(1)}, f32[152]{0:T(256)S(1)}) fusion(f32[1216]{0:T(1024)S(1)} %sub.360, f32[152]{0:T(256)S(1)} %bitcast.234, f32[1216]{0:T(1024)S(1)} %mul.507, f32[1216]{0:T(1024)S(1)} %sub.370, f32[152]{0:T(256)S(1)} %bitcast.238, f32[1216]{0:T(1024)S(1)} %mul.504, f32[1216]{0:T(1024)S(1)} %sub.365, ...), kind=kLoop, calls=%fused_computation.123 | loop fusion | flops 4250680 | bytes 32832 | tf_op jit(solution)/shard_map/reduce_sum | solution.py:32
  27.4 1.3 %convolution_add_fusion.5 = f32[3,152]{1,0:T(4,128)S(1)} fusion(f32[3,1216]{1,0:T(4,128)S(1)} %reshape.287, f32[1216]{0:T(1024)S(1)} %sub.370, f32[152]{0:T(256)S(1)} %bitcast.239, f32[1216]{0:T(1024)S(1)} %sub.365, f32[152]{0:T(256)S(1)} %bitcast.243, f32[1216]{0:T(1024)S(1)} %sub.360, f32[152]{0:T(256)S(1)} %bitcast.235, f32[1,152]{1,0:T(1,128)S(1)} %bitcast.267, ...), kind=kOutput, calls=%fused_computation.115 | convolution fusion | flops 9058136 | bytes 34656 | tf_op jit(solution)/shard_map/ts,ks->kt/dot_general | solution.py:29
  28.6 0.8 fusion.113
  29.4 0.8 %fusion.79 = f32[3,152]{1,0:T(4,128)S(1)} fusion(f32[3,152]{1,0:T(4,128)S(1)} %convolution_add_fusion.5, f32[3,608]{1,0:T(4,128)S(1)} %reshape.289, f32[608]{0:T(1024)S(1)} %sub.382, f32[152]{0:T(256)S(1)} %bitcast.241, f32[608]{0:T(1024)S(1)} %sub.378, f32[152]{0:T(256)S(1)} %bitcast.245, f32[608]{0:T(1024)S(1)} %sub.374, f32[152]{0:T(256)S(1)} %bitcast.237, ...), kind=kOutput, calls=%fused_computation.113 | convolution fusion | flops 4530664 | bytes 21888 | tf_op jit(solution)/shard_map/ts,ks->kt/dot_general | solution.py:29
  30.2 0.3 fusion.244
  30.6 0.1 all-to-all-done.1
  30.7 0.1 copy.47
  30.8 0.6 gather_fusion
  31.4 0.1 bitcast_reduce_fusion.1
  31.5 0.9 %multiply_reduce_fusion.5 = (f32[2,544]{1,0:T(2,128)S(1)}, f32[3,2,544]{2,0,1:T(4,128)S(1)}) fusion(f32[544,544]{1,0:T(8,128)S(1)} %copy-done, f32[3,544]{1,0:T(4,128)S(1)} %copy-done.5, f32[3,2]{0,1:T(2,128)S(1)} %broadcast_multiply_fusion.5, f32[2,3,544]{2,1,0:T(4,128)S(1)} %gather_fusion), kind=kOutput, calls=%fused_computation.234 | convolution fusion | flops 21319360 | bytes 1220760 | tf_op jit(solution)/shard_map/dot_general | solution.py:43
  32.5 4.6 %fusion.7 = (f32[2,544]{1,0:T(2,128)S(1)}, f32[2,544]{1,0:T(2,128)S(1)}, f32[2,544]{1,0:T(2,128)S(1)}) fusion(f32[2,544]{1,0:T(2,128)S(1)} %bitcast.223, f32[2,544]{1,0:T(2,128)S(1)} %get-tuple-element.52, f32[2,544]{1,0:T(2,128)S(1)} %get-tuple-element.89, f32[2,544]{1,0:T(2,128)S(1)} %get-tuple-element.87, f32[2,544]{1,0:T(2,128)S(1)} %get-tuple-element.53, ...), kind=kLoop, calls=%fused_computation.31 | loop fusion | flops 13609792 | bytes 52224 | tf_op jit(solution)/shard_map/vmap()/reduce_sum | solution.py:32
  37.1 4.6 %fusion.71 = f32[3,2,544]{2,0,1:T(4,128)S(1)} fusion(f32[3,2,544]{2,0,1:T(4,128)S(1)} %negate_multiply_fusion.1, f32[2,544]{1,0:T(2,128)S(1)} %get-tuple-element.87, f32[2,544]{1,0:T(2,128)S(1)} %get-tuple-element.53, f32[2,544]{1,0:T(2,128)S(1)} %get-tuple-element.88, f32[2,544]{1,0:T(2,128)S(1)} %get-tuple-element.54, f32[2,544]{1,0:T(2,128)S(1)} %bitcast.224, ...), kind=kOutput, calls=%fused_computation.103 | convolution fusion | flops 29014784 | bytes 65280 | tf_op jit(solution)/shard_map/vmap(ts,ks->kt)/dot_general | solution.py:29
  41.7 0.4 fusion.226
  42.1 0.9 %multiply_reduce_fusion.1 = (f32[4,544]{1,0:T(4,128)S(1)}, f32[3,4,544]{2,1,0:T(4,128)S(1)}) fusion(f32[544,544]{1,0:T(8,128)S(1)} %copy-done, f32[3,4,544]{2,1,0:T(4,128)S(1)} %get-tuple-element.82, f32[3,4]{1,0:T(4,128)S(1)} %broadcast_multiply_fusion.2, f32[3,544]{1,0:T(4,128)S(1)} %copy-done.5), kind=kOutput, calls=%fused_computation.218 | convolution fusion | flops 42638720 | bytes 1251248 | tf_op jit(solution)/shard_map/dot_general | solution.py:43
  43.0 0.5 fusion.245
  43.5 0.1 reshape.290
  43.8 0.7 broadcast_in_dim.19
  44.4 3.4 %all-to-all-start.2 = ((f32[32,1,512]{2,1,0:T(1,128)}), f32[32,1,512]{2,1,0:T(1,128)S(1)}, u32[]{:S(2)}, u32[]{:S(2)}) async-start(f32[32,1,512]{2,1,0:T(1,128)} %broadcast_in_dim.19), calls=%async_computation.2 | async-start | bytes 131072 | tf_op jit(solution)/shard_map/all_to_all | solution.py:109
  47.8 0.6 gather_fusion.3
  48.5 6.7 %all-to-all-done.2 = f32[32,1,512]{2,1,0:T(1,128)S(1)} async-done(((f32[32,1,512]{2,1,0:T(1,128)}), f32[32,1,512]{2,1,0:T(1,128)S(1)}, u32[]{:S(2)}, u32[]{:S(2)}) %all-to-all-start.2) | async-done | bytes 65568 | tf_op jit(solution)/shard_map/all_to_all | solution.py:109
  55.2 0.7 broadcast_in_dim.20
  55.9 3.6 %all-to-all-start.3 = ((f32[8,3,4,544]{3,2,1,0:T(4,128)}), f32[8,3,4,544]{3,2,1,0:T(4,128)S(1)}, u32[]{:S(2)}, u32[]{:S(2)}) async-start(f32[8,3,4,544]{3,2,1,0:T(4,128)} %broadcast_in_dim.20), calls=%async_computation.3 | async-start | bytes 491520 | tf_op jit(solution)/shard_map/all_to_all | solution.py:89
  59.6 0.1 fusion.225
  59.7 0.1 reshape.291
  60.0 0.1 reshape.292
  60.1 0.2 fusion.74
  60.3 0.1 reshape.294
  60.7 0.1 copy.77
  60.8 0.1 sub.423
  61.1 0.1 mul.573
  61.5 0.1 sub.409
  61.8 1.1 %fusion.98 = (f32[152]{0:T(256)S(1)}, f32[152]{0:T(256)S(1)}, f32[152]{0:T(256)S(1)}) fusion(f32[1216]{0:T(1024)S(1)} %sub.409, f32[152]{0:T(256)S(1)} %bitcast.246, f32[1216]{0:T(1024)S(1)} %mul.579, f32[1216]{0:T(1024)S(1)} %sub.419, f32[152]{0:T(256)S(1)} %bitcast.250, f32[1216]{0:T(1024)S(1)} %mul.576, f32[1216]{0:T(1024)S(1)} %sub.414, ...), kind=kLoop, calls=%fused_computation.134 | loop fusion | flops 4250680 | bytes 32832 | tf_op jit(solution)/shard_map/reduce_sum | solution.py:32
  62.9 1.3 %convolution_add_fusion.4 = f32[3,152]{1,0:T(4,128)S(1)} fusion(f32[3,1216]{1,0:T(4,128)S(1)} %reshape.292, f32[1216]{0:T(1024)S(1)} %sub.419, f32[152]{0:T(256)S(1)} %bitcast.251, f32[1216]{0:T(1024)S(1)} %sub.414, f32[152]{0:T(256)S(1)} %bitcast.255, f32[1216]{0:T(1024)S(1)} %sub.409, f32[152]{0:T(256)S(1)} %bitcast.247, f32[1,152]{1,0:T(1,128)S(1)} %bitcast.270, ...), kind=kOutput, calls=%fused_computation.114 | convolution fusion | flops 9058136 | bytes 34656 | tf_op jit(solution)/shard_map/ts,ks->kt/dot_general | solution.py:29
  64.2 0.8 fusion.124
  64.9 0.8 %fusion.77 = f32[3,152]{1,0:T(4,128)S(1)} fusion(f32[3,152]{1,0:T(4,128)S(1)} %convolution_add_fusion.4, f32[3,608]{1,0:T(4,128)S(1)} %reshape.294, f32[608]{0:T(1024)S(1)} %sub.431, f32[152]{0:T(256)S(1)} %bitcast.253, f32[608]{0:T(1024)S(1)} %sub.427, f32[152]{0:T(256)S(1)} %bitcast.257, f32[608]{0:T(1024)S(1)} %sub.423, f32[152]{0:T(256)S(1)} %bitcast.249, ...), kind=kOutput, calls=%fused_computation.110 | convolution fusion | flops 4530664 | bytes 21888 | tf_op jit(solution)/shard_map/ts,ks->kt/dot_general | solution.py:29
  65.8 0.3 fusion.246
  66.1 0.1 copy.52
  66.2 0.6 gather_fusion.1
  66.8 0.1 bitcast_reduce_fusion
  66.9 0.9 %multiply_reduce_fusion.4 = (f32[2,544]{1,0:T(2,128)S(1)}, f32[3,2,544]{2,0,1:T(4,128)S(1)}) fusion(f32[544,544]{1,0:T(8,128)S(1)} %copy-done, f32[3,2]{0,1:T(2,128)S(1)} %broadcast_multiply_fusion.4, f32[3,544]{1,0:T(4,128)S(1)} %copy-done.5, f32[2,3,544]{2,1,0:T(4,128)S(1)} %gather_fusion.1), kind=kOutput, calls=%fused_computation.230 | convolution fusion | flops 21319360 | bytes 1220760 | tf_op jit(solution)/shard_map/dot_general | solution.py:43
  67.9 4.4 %fusion.18 = (f32[2,544]{1,0:T(2,128)S(1)}, f32[2,544]{1,0:T(2,128)S(1)}, f32[2,544]{1,0:T(2,128)S(1)}) fusion(f32[2,544]{1,0:T(2,128)S(1)} %bitcast.230, f32[2,544]{1,0:T(2,128)S(1)} %bitcast.221, f32[2,544]{1,0:T(2,128)S(1)} %bitcast.229, f32[2,544]{1,0:T(2,128)S(1)} %bitcast.225, f32[2,544]{1,0:T(2,128)S(1)} %bitcast.217, f32[2,544]{1,0:T(2,128)S(1)} %bitcast.232, ...), kind=kLoop, calls=%fused_computation.42 | loop fusion | flops 13609792 | bytes 52224 | tf_op jit(solution)/shard_map/vmap()/reduce_sum | solution.py:32
  72.3 4.6 %fusion.65 = f32[3,2,544]{2,0,1:T(4,128)S(1)} fusion(f32[3,2,544]{2,0,1:T(4,128)S(1)} %negate_multiply_fusion, f32[2,544]{1,0:T(2,128)S(1)} %bitcast.226, f32[2,544]{1,0:T(2,128)S(1)} %bitcast.218, f32[2,544]{1,0:T(2,128)S(1)} %bitcast.228, f32[2,544]{1,0:T(2,128)S(1)} %bitcast.220, f32[2,544]{1,0:T(2,128)S(1)} %bitcast.231, f32[2,544]{1,0:T(2,128)S(1)} %bitcast.222, ...), kind=kOutput, calls=%fused_computation.101 | convolution fusion | flops 29014784 | bytes 65280 | tf_op jit(solution)/shard_map/vmap(ts,ks->kt)/dot_general | solution.py:29
  76.9 0.9 %multiply_add_fusion = (f32[3,4,544]{2,1,0:T(4,128)}, f32[3,4,544]{2,1,0:T(4,128)}) fusion(f32[3,4,544]{2,1,0:T(4,128)S(1)} %get-tuple-element.82, f32[3,2,544]{2,0,1:T(4,128)S(1)} %fusion.65, pred[2]{0:T(512)(128)(4,1)S(1)} %iota_compare_fusion.1, s32[2]{0:T(128)S(1)} %bitcast.259, f32[3,544]{1,0:T(4,128)S(1)} %fusion.246), kind=kOutput, calls=%fused_computation.216 | convolution fusion | flops 176272 | bytes 97930 | tf_op jit(solution)/shard_map/ksp,sc->kcp/dot_general | solution.py:99
  (119 shorter events, 3.2 us)
Async XLA Ops:
  0.6 1.5 %copy-start = (f32[544,544]{1,0:T(8,128)S(1)}, f32[544,544]{1,0:T(8,128)}, u32[]{:S(2)}) copy-start(f32[544,544]{1,0:T(8,128)} %param.15) | copy-start | bytes 3551236
  0.6 12.0 %copy-start.3 = (f32[3,4,544]{2,1,0:T(4,128)S(1)}, f32[3,4,544]{2,1,0:T(4,128)}, u32[]{:S(2)}) copy-start(f32[3,4,544]{2,1,0:T(4,128)} %param.13) | copy-start | bytes 78340
  0.7 3.2 %copy-start.1 = (f32[544,152]{0,1:T(8,128)S(1)}, f32[544,152]{0,1:T(8,128)}, u32[]{:S(2)}) copy-start(f32[544,152]{0,1:T(8,128)} %param.16) | copy-start | bytes 992260
  0.7 11.8 %copy-start.9 = (s32[1,2]{1,0:T(1,128)S(1)}, s32[1,2]{1,0:T(1,128)}, u32[]{:S(2)}) copy-start(s32[1,2]{1,0:T(1,128)} %param.20) | copy-start | bytes 28
  0.7 11.9 %copy-start.6 = (f32[3,152]{1,0:T(4,128)S(1)}, f32[3,152]{1,0:T(4,128)}, u32[]{:S(2)}) copy-start(f32[3,152]{1,0:T(4,128)} %param.19) | copy-start | bytes 5476
  0.7 12.6 %copy-start.8 = (s32[1,2]{1,0:T(1,128)S(1)}, s32[1,2]{1,0:T(1,128)}, u32[]{:S(2)}) copy-start(s32[1,2]{1,0:T(1,128)} %param.21) | copy-start | bytes 28
  0.7 12.6 %copy-start.7 = (s32[1,2]{1,0:T(1,128)S(1)}, s32[1,2]{1,0:T(1,128)}, u32[]{:S(2)}) copy-start(s32[1,2]{1,0:T(1,128)} %param.22) | copy-start | bytes 28
  3.8 20.8 %copy-start.4 = (f32[152,152]{1,0:T(8,128)S(1)}, f32[152,152]{1,0:T(8,128)}, u32[]{:S(2)}) copy-start(f32[152,152]{1,0:T(8,128)} %param.18) | copy-start | bytes 277252
  5.2 14.7 %all-to-all-start = ((f32[32,1,512]{2,1,0:T(1,128)}), f32[32,1,512]{2,1,0:T(1,128)S(1)}, u32[]{:S(2)}, u32[]{:S(2)}) async-start(f32[32,1,512]{2,1,0:T(1,128)} %broadcast_in_dim.17), calls=%async_computation | async-start | bytes 131072 | tf_op jit(solution)/shard_map/all_to_all | solution.py:109
  20.6 10.1 %all-to-all-start.1 = ((f32[8,3,4,544]{3,2,1,0:T(4,128)}), f32[8,3,4,544]{3,2,1,0:T(4,128)S(1)}, u32[]{:S(2)}, u32[]{:S(2)}) async-start(f32[8,3,4,544]{3,2,1,0:T(4,128)} %broadcast_in_dim.18), calls=%async_computation.1 | async-start | bytes 491520 | tf_op jit(solution)/shard_map/all_to_all | solution.py:89
  28.6 1.6 %copy-start.2 = (f32[152,544]{1,0:T(8,128)S(1)}, f32[152,544]{1,0:T(8,128)}, u32[]{:S(2)}) copy-start(f32[152,544]{1,0:T(8,128)} %param.17) | copy-start | bytes 992260
  29.4 2.1 %copy-start.5 = (f32[3,544]{1,0:T(4,128)S(1)}, f32[3,544]{1,0:T(4,128)}, u32[]{:S(2)}) copy-start(f32[3,544]{1,0:T(4,128)} %param.14) | copy-start | bytes 19588
  44.4 10.8 %all-to-all-start.2 = ((f32[32,1,512]{2,1,0:T(1,128)}), f32[32,1,512]{2,1,0:T(1,128)S(1)}, u32[]{:S(2)}, u32[]{:S(2)}) async-start(f32[32,1,512]{2,1,0:T(1,128)} %broadcast_in_dim.19), calls=%async_computation.2 | async-start | bytes 131072 | tf_op jit(solution)/shard_map/all_to_all | solution.py:109
  55.9 10.1 %all-to-all-start.3 = ((f32[8,3,4,544]{3,2,1,0:T(4,128)}), f32[8,3,4,544]{3,2,1,0:T(4,128)S(1)}, u32[]{:S(2)}, u32[]{:S(2)}) async-start(f32[8,3,4,544]{3,2,1,0:T(4,128)} %broadcast_in_dim.20), calls=%async_computation.3 | async-start | bytes 491520 | tf_op jit(solution)/shard_map/all_to_all | solution.py:89

commit v2 on v0

v2 whole, which is shorter than its diff:
```python
import functools

import jax
import jax.numpy as jnp
from jax import lax
from jax.experimental import pallas as pl
from jax.experimental.pallas import tpu as pltpu
from jax.sharding import PartitionSpec as P

STEPS = 2
NEAR = 2

EPSILON_SQ = 0.25
VISCOSITY = 0.039788735772973836
TIME_STEP = 0.1
SKALAK_HARDEN = 2.0
CHECK_RADIUS = 1.0
DEVICE_RADIUS = 1.5
GROUP_RADIUS = 6.0

LANES = 128
SUB = 8


def up8(n):
    return -(-n // SUB) * SUB


def split(a):
    high = a.astype(jnp.bfloat16)
    low = (a - high.astype(jnp.float32)).astype(jnp.bfloat16)
    return high, low


def dot3(a, b):
    a_high, a_low = split(a)
    b_high, b_low = split(b)
    dot = functools.partial(jnp.dot, preferred_element_type=jnp.float32)
    return dot(a_high, b_high) + (dot(a_low, b_high) + dot(a_high, b_low))


def harden(linear, stretch):
    return -linear * (1.0 + SKALAK_HARDEN * stretch / (1.0 + stretch))


def add_pair(acc, delta, force):
    square = delta[0] * delta[0] + delta[1] * delta[1] + delta[2] * delta[2]
    root = lax.rsqrt(square + EPSILON_SQ)
    inverse = root * root * root
    direct = root + EPSILON_SQ * inverse
    along = (delta[0] * force[0] + delta[1] * force[1] + delta[2] * force[2]) * inverse
    return [acc[k] + (direct * force[k] + along * delta[k]) for k in range(3)]


def membrane_kernel(points_ref, rest_ref, stiffness_ref, up_ref, out_ref, rows_ref, flat_ref):
    cells, size = points_ref.shape[1:]
    q = up_ref.shape[1]
    tail = q - LANES
    rows_ref[...] = jnp.zeros_like(rows_ref)
    centers = []
    for k in range(3):
        own = points_ref[k]
        mean = jnp.mean(own, axis=1, keepdims=True)
        rows_ref[SUB * k : SUB * k + cells, :] = own - mean - rest_ref[k : k + 1, :]
        centers.append(jnp.mean(mean, axis=0, keepdims=True))
    linear = dot3(rows_ref[...], stiffness_ref[...])
    parts = [linear[SUB * k : SUB * (k + 1)] for k in range(3)]
    stretch = parts[0] * parts[0] + parts[1] * parts[1] + parts[2] * parts[2]
    sums = [jnp.sum(harden(part, stretch), axis=0, keepdims=True) for part in parts]
    summed = jnp.concatenate(sums + [jnp.zeros((SUB - 3, size), jnp.float32)], axis=0)
    flat_ref[...] = jnp.zeros_like(flat_ref)
    flat_ref[:, :q] = dot3(summed, up_ref[...])
    ends = flat_ref[:, LANES:]
    last = ends[0:1]
    lane = lax.broadcasted_iota(jnp.int32, (1, LANES), 1)
    for k in range(1, 3):
        last = last + pltpu.roll(ends[k : k + 1], tail * k, axis=1)
    for k in range(3):
        last = jnp.where(lane == 3 * tail + k, centers[k], last)
    message = jnp.concatenate([flat_ref[0:3, :LANES], last], axis=0)
    out_ref[...] = jnp.broadcast_to(message[None], out_ref.shape)


def pick(block, row):
    rows = lax.broadcasted_iota(jnp.int32, (block.shape[0], 1), 0)
    return jnp.sum(jnp.where(rows == row, block, 0.0), axis=0, keepdims=True)


def near_kernel(
    target_ref,
    owner_ref,
    cell_ref,
    count_ref,
    own_ref,
    *refs,
    spread,
):
    pool_refs, (rest_ref, stiffness_ref, out_ref, rows_ref, cols_ref, aim_ref, move_ref) = (
        refs[:-7],
        refs[-7:],
    )
    size = own_ref.shape[2]
    chunks = aim_ref.shape[1] // LANES
    me = lax.axis_index("dev")
    out_ref[...] = jnp.zeros_like(out_ref)
    rows_ref[...] = jnp.zeros_like(rows_ref)
    move_ref[...] = jnp.zeros_like(move_ref)
    for slot in range(NEAR):
        cell = cell_ref[0, slot]
        owner = owner_ref[0, slot]
        if spread:
            for mask, pool_ref in enumerate(pool_refs):

                @pl.when((owner ^ me) == mask)
                def _(pool_ref=pool_ref):
                    for k in range(3):
                        rows_ref[SUB * slot + k : SUB * slot + k + 1, :] = pick(pool_ref[k], cell)
        else:
            for k in range(3):
                rows_ref[SUB * slot + k : SUB * slot + k + 1, :] = pick(
                    pool_refs[0][owner, k], cell
                )
    sources = rows_ref[...]
    for slot in range(NEAR):
        own = sources[SUB * slot : SUB * slot + 3]
        mean = jnp.mean(own, axis=1, keepdims=True)
        move_ref[SUB * slot : SUB * slot + 3, :] = own - mean - rest_ref[...]
    linear = dot3(move_ref[...], stiffness_ref[...])
    square = linear * linear
    for slot in range(NEAR):
        part = linear[SUB * slot : SUB * slot + 3]
        stretch = jnp.sum(square[SUB * slot : SUB * slot + 3], axis=0, keepdims=True)
        rows_ref[SUB * slot + 3 : SUB * slot + 6, :] = harden(part, stretch)
    aim_ref[...] = jnp.zeros_like(aim_ref)
    for slot in range(NEAR):

        @pl.when(slot < count_ref[0])
        def _(slot=slot):
            target = target_ref[0, slot]
            cols_ref[...] = jnp.transpose(rows_ref[SUB * slot : SUB * slot + SUB, :])
            for k in range(3):
                aim_ref[k : k + 1, :size] = pick(own_ref[k], target)
            aims = [
                [
                    jnp.broadcast_to(aim_ref[k : k + 1, LANES * c : LANES * (c + 1)], (SUB, LANES))
                    for k in range(3)
                ]
                for c in range(chunks)
            ]

            def group(i, acc):
                block = cols_ref[pl.ds(pl.multiple_of(i * SUB, SUB), SUB), :]
                place = [jnp.broadcast_to(block[:, k : k + 1], (SUB, LANES)) for k in range(3)]
                force = [jnp.broadcast_to(block[:, k : k + 1], (SUB, LANES)) for k in range(3, 6)]
                return tuple(
                    tuple(
                        add_pair(acc[c], [aims[c][k] - place[k] for k in range(3)], force)
                    )
                    for c in range(chunks)
                )

            zero = jnp.zeros((SUB, LANES), jnp.float32)
            acc = lax.fori_loop(
                0, size // SUB, group, tuple((zero,) * 3 for _ in range(chunks)), unroll=2
            )
            for c in range(chunks):
                for k in range(3):
                    part = VISCOSITY * jnp.sum(acc[c][k], axis=0, keepdims=True)
                    aim_ref[k : k + 1, LANES * c : LANES * (c + 1)] = part
            for k in range(3):
                old = out_ref[k]
                chosen = lax.broadcasted_iota(jnp.int32, (old.shape[0], 1), 0) == target
                out_ref[k] = old + jnp.where(chosen, aim_ref[k : k + 1, :size], 0.0)


def boxes(main, ends, center, template, radius, per_row):
    count = main[0].shape[0]
    tail_lanes = template[2]
    rows = []
    for k in range(3):
        place_main = center[k] + radius * template[0][k : k + 1]
        place_ends = jnp.where(tail_lanes, center[k] + radius * template[1][k : k + 1], 0.0)
        rows.append((place_main, place_ends))
    for k in range(3):
        rows.append((main[k], ends[k]))
    packed = []
    for whole, part in rows:
        turn = lax.broadcasted_iota(jnp.int32, (count, 1), 0) % per_row[0]
        shifted = jnp.where(turn == 0, part, 0.0)
        for i in range(1, per_row[0]):
            shifted += jnp.where(turn == i, pltpu.roll(part, per_row[1] * i, axis=1), 0.0)
        packed.append(
            [whole]
            + [
                jnp.sum(shifted[a : min(a + per_row[0], count)], axis=0, keepdims=True)
                for a in range(0, count, per_row[0])
            ]
        )
    return packed


def far_kernel(
    told_ref,
    points_ref,
    near_ref,
    m2m_ref,
    template_ref,
    down_ref,
    points_out_ref,
    velocity_ref,
    wide_ref,
    sums_ref,
    group_ref,
    source_ref,
    check_ref,
    result_ref,
    *,
    groups,
    devs,
):
    q = template_ref.shape[1]
    tail = q - LANES
    per_row = (LANES // tail, tail)
    group = lax.axis_index("grp")
    dev = lax.axis_index("dev")
    lane = lax.broadcasted_iota(jnp.int32, (1, LANES), 1)
    tail_lanes = lane < tail

    def ends_of(row, k):
        moved = pltpu.roll(row, LANES - tail * k, axis=1) if k else row
        return jnp.where(tail_lanes, moved, 0.0)

    wide_ref[...] = jnp.zeros_like(wide_ref)
    wide_ref[0:3, :q] = template_ref[...]
    template = (wide_ref[:, :LANES], wide_ref[:, LANES:], tail_lanes)

    first = group * devs
    own_rows = [told_ref[pl.ds(first, devs), k, :] for k in range(4)]
    others = lax.broadcasted_iota(jnp.int32, (devs, 1), 0) != dev
    inner = boxes(
        [jnp.where(others, own_rows[k], 0.0) for k in range(3)],
        [jnp.where(others, ends_of(own_rows[3], k), 0.0) for k in range(3)],
        [own_rows[3][:, 3 * tail + k : 3 * tail + k + 1] for k in range(3)],
        template,
        DEVICE_RADIUS,
        per_row,
    )

    span = up8(groups)
    sums_ref[...] = jnp.zeros_like(sums_ref)
    for h in range(groups):
        sums_ref[h] = jnp.sum(told_ref[h * devs : (h + 1) * devs], axis=0)
    sum_rows = [sums_ref[:, k, :] for k in range(4)]
    for k in range(3):
        group_ref[span * k : span * (k + 1), :LANES] = sum_rows[k]
        group_ref[span * k : span * (k + 1), LANES:] = ends_of(sum_rows[3], k)
    shifted = dot3(group_ref[:, :q], m2m_ref[...])
    group_ref[:, :q] = shifted
    other_groups = lax.broadcasted_iota(jnp.int32, (span, 1), 0) != group
    outer = boxes(
        [
            jnp.where(other_groups, group_ref[span * k : span * (k + 1), :LANES], 0.0)
            for k in range(3)
        ],
        [
            jnp.where(other_groups, group_ref[span * k : span * (k + 1), LANES:], 0.0)
            for k in range(3)
        ],
        [sum_rows[3][:, 3 * tail + k : 3 * tail + k + 1] / devs for k in range(3)],
        template,
        GROUP_RADIUS,
        per_row,
    )
    rows = 0
    for part, count in ((inner, devs), (outer, groups)):
        ends = -(-count // per_row[0])
        for index in range(6):
            source_ref[index, rows : rows + count, :] = part[index][0][:count]
            for j in range(ends):
                source_ref[index, rows + count + j : rows + count + j + 1, :] = part[index][1 + j]
        rows += count + ends

    center_row = told_ref[pl.ds(first + dev, 1), 3, :]
    for k in range(3):
        center = center_row[:, 3 * tail + k : 3 * tail + k + 1]
        wide_ref[k : k + 1, :] = center + CHECK_RADIUS * wide_ref[k : k + 1, :]
    check_ref[...] = jnp.transpose(wide_ref[...])

    @pl.loop(0, q // SUB)
    def _(i):
        at = pl.ds(pl.multiple_of(i * SUB, SUB), SUB)
        block = check_ref[at, :]
        check = [jnp.broadcast_to(block[:, k : k + 1], (SUB, LANES)) for k in range(3)]
        acc = [jnp.zeros((SUB, LANES), jnp.float32)] * 3
        for row in range(rows):
            source = [
                jnp.broadcast_to(source_ref[index, row : row + 1, :], (SUB, LANES))
                for index in range(6)
            ]
            acc = add_pair(acc, [check[k] - source[k] for k in range(3)], source[3:])
        total = [VISCOSITY * jnp.sum(acc[k], axis=1, keepdims=True) for k in range(3)]
        result_ref[at, :] = jnp.where(
            lane == 0, total[0], jnp.where(lane == 1, total[1], total[2])
        )

    checks = jnp.transpose(result_ref[...])[:SUB]
    surface = dot3(checks, down_ref[...])
    for k in range(3):
        velocity = surface[k : k + 1] + near_ref[k]
        velocity_ref[k] = velocity
        points_out_ref[k] = points_ref[k] + TIME_STEP * velocity


VMEM = pl.BlockSpec(memory_space=pltpu.VMEM)
SMEM = pl.BlockSpec(memory_space=pltpu.SMEM)


def float32(*shape):
    return jax.ShapeDtypeStruct(shape, jnp.float32)


def body(
    positions,
    rest_shape,
    stiffness,
    up_map,
    down_map,
    m2m,
    box_template,
    near_target,
    near_owner,
    near_cell,
    near_count,
):
    devs = lax.axis_size("dev")
    groups = lax.axis_size("grp")
    cells, size = positions.shape[1:]
    q = up_map.shape[1]
    wide = -(-size // LANES) * LANES
    spread = devs == 8
    span = up8(groups)
    tail_boxes = LANES // (q - LANES)
    source_rows = devs + groups + -(-devs // tail_boxes) + -(-groups // tail_boxes)

    membrane = pl.pallas_call(
        membrane_kernel,
        out_shape=float32(groups * devs, 4, LANES),
        in_specs=[VMEM] * 4,
        out_specs=VMEM,
        scratch_shapes=[
            pltpu.VMEM((3 * SUB, size), jnp.float32),
            pltpu.VMEM((SUB, 2 * LANES), jnp.float32),
        ],
        name="membrane",
        cost_estimate=pl.CostEstimate(flops=10**9, bytes_accessed=10**6, transcendentals=0),
    )
    pools = 8 if spread else 1
    near = pl.pallas_call(
        functools.partial(near_kernel, spread=spread),
        out_shape=float32(3, cells, size),
        in_specs=[SMEM] * 4 + [VMEM] * (1 + pools + 2),
        out_specs=VMEM,
        scratch_shapes=[
            pltpu.VMEM((NEAR * SUB, size), jnp.float32),
            pltpu.VMEM((size, SUB), jnp.float32),
            pltpu.VMEM((SUB, wide), jnp.float32),
            pltpu.VMEM((NEAR * SUB, size), jnp.float32),
        ],
        name="near",
        cost_estimate=pl.CostEstimate(flops=4 * 10**9, bytes_accessed=10**6, transcendentals=0),
    )
    far = pl.pallas_call(
        functools.partial(far_kernel, groups=groups, devs=devs),
        out_shape=(float32(3, cells, size), float32(3, cells, size)),
        in_specs=[VMEM] * 6,
        out_specs=(VMEM, VMEM),
        scratch_shapes=[
            pltpu.VMEM((SUB, 2 * LANES), jnp.float32),
            pltpu.VMEM((span, 4, LANES), jnp.float32),
            pltpu.VMEM((3 * span, 2 * LANES), jnp.float32),
            pltpu.VMEM((6, up8(source_rows), LANES), jnp.float32),
            pltpu.VMEM((2 * LANES, SUB), jnp.float32),
            pltpu.VMEM((q, LANES), jnp.float32),
        ],
        name="far",
        cost_estimate=pl.CostEstimate(flops=2 * 10**9, bytes_accessed=10**6, transcendentals=0),
    )

    def to(array, mask):
        return lax.ppermute(array, "dev", [(j, j ^ mask) for j in range(devs)])

    points = positions
    velocity = None
    for _ in range(STEPS):
        message = membrane(points, rest_shape, stiffness, up_map)
        told = lax.all_to_all(message, ("grp", "dev"), 0, 0)
        if spread:
            pool = [points] + [to(points, mask) for mask in (2, 4, 6)]
            pool += [to(array, 1) for array in pool]
            pool = [pool[mask // 2 + 4 * (mask % 2)] for mask in range(8)]
        else:
            copies = jnp.broadcast_to(points[None], (devs,) + points.shape)
            pool = [lax.all_to_all(copies, "dev", 0, 0)]
        close = near(
            near_target,
            near_owner,
            near_cell,
            near_count,
            points,
            *pool,
            rest_shape,
            stiffness,
        )
        points, velocity = far(told, points, close, m2m, box_template, down_map)
    return (points, velocity)


def solution(mesh):
    both = ("grp", "dev")
    return jax.shard_map(
        body,
        mesh=mesh,
        in_specs=(P(None, both, None),) + (P(),) * 6 + (P(both, None),) * 3 + (P(both),),
        out_specs=(P(None, both, None), P(None, both, None)),
        check_vma=False,
    )
```

time: 157 us -> 73.5 us (0.47)
  blocking collectives: 111 us -> 0 us
  Pallas kernels: 0 us -> 42 us
  matrix products: 19.1 us -> 0 us
  starting transfers between devices: 0 us -> 18.8 us
  other arithmetic: 15.7 us -> 0 us
  waiting for transfers between devices: 0 us -> 5.14 us
  local copies, waits for them, and re-layouts: 7.79 us -> 5.69 us
  between operations: 3.27 us -> 1.44 us
    all_gather x6 -> x0, blocking collectives: 63.1 us -> none  [the longest x2 26.5 us: body(): outer_box_forces = lax.all_gather(group_eq[None], 'grp', axis=0, tiled=True)]
    unnamed x4 -> x0, blocking collectives: 47.4 us -> none
    pallas_call x0 -> x6, Pallas kernels: none -> 42 us  [the longest x2 22.4 us: body(): near(near_target, near_owner, near_cell, near_count, points, *pool, rest_...]
    dot_general x16 -> x0, matrix products: 19.1 us -> none  [the longest x6 13.4 us: stokes(): jnp.einsum('ts,ks->kt', direct, forces, precision=lax.Precision.HIGHEST)]
    reduce_sum x13 -> x0, other arithmetic: 13.6 us -> none  [the longest x6 12.5 us: stokes(): jnp.sum(delta_x * projected, axis=1)]
    all_to_all x0 -> x2, starting transfers between devices: none -> 10 us  [body(): told = lax.all_to_all(message, ('grp', 'dev'), 0, 0)]
    ppermute x0 -> x14, starting transfers between devices: none -> 8.79 us  [to(): return lax.ppermute(array, 'dev', [(j, j ^ mask) for j in range(devs)])]
    ppermute x0 -> x14, waiting for transfers between devices: none -> 5.14 us  [to(): return lax.ppermute(array, 'dev', [(j, j ^ mask) for j in range(devs)])]
  transfers between devices with their start and end apart: 0 -> 16, of which waited for: 0 -> 5; matrix products, arithmetic and copies ran while one was open for 0% -> 3% of each run, Pallas kernels for 0% -> 39%
where the time goes in v2:
time: 73.5 us; the launch traced here: 73.1 us
  Pallas kernels  42 us (57%)
  starting transfers between devices  18.8 us (26%)
  local copies, waits for them, and re-layouts  5.69 us (8%)
  waiting for transfers between devices  5.14 us (7%)
  between operations  1.44 us (2%)
    pallas_call x2, Pallas kernels, body(): near(near_target, near_owner, near_cell, near_count, points, *pool, rest_...  22.4 us
    pallas_call x2, Pallas kernels, body(): points, velocity = far(told, points, close, m2m, box_template, down_map)  13.3 us
    all_to_all x2, starting transfers between devices, body(): told = lax.all_to_all(message, ('grp', 'dev'), 0, 0)  10 us
    ppermute x14, starting transfers between devices, to(): return lax.ppermute(array, 'dev', [(j, j ^ mask) for j in range(devs)])  8.79 us
    pallas_call x2, Pallas kernels, body(): message = membrane(points, rest_shape, stiffness, up_map)  6.3 us
    unnamed x33, local copies, waits for them, and re-layouts  5.69 us
    ppermute x14, waiting for transfers between devices, to(): return lax.ppermute(array, 'dev', [(j, j ^ mask) for j in range(devs)])  5.14 us
  transfers between devices with their start and end apart: 16, of which 5 were waited for; matrix products, arithmetic and copies ran while one was open for 3% of the time, Pallas kernels for 39%

profile of v2, /device:TPU:0, one launch (start us, length us, event | category | flops | bytes accessed | tf_op | source)
XLA Modules:
  0.0 73.1 jit_solution(13729005178001488550)
XLA Ops:
  0.6 4.0 %collective-permute-start.5 = (f32[3,4,544]{2,1,0:T(4,128)}, f32[3,4,544]{2,1,0:T(4,128)S(1)}, u32[]{:S(2)}, u32[]{:S(2)}) collective-permute-start(f32[3,4,544]{2,1,0:T(4,128)} %points_ref.3), channel_id=1, source_target_pairs={{0,6},{1,7},{2,4},{3,5},{4,2},{5,3},{6,0},{7,1},{8,14},{9,15},{10,... | collective-permute-start | bytes 78344 | tf_op jit(solution)/shard_map/ppermute | solution.py:390
  4.6 0.5 collective-permute-start.3
  5.1 0.1 collective-permute-start.1
  5.3 0.0 collective-permute-start
  5.3 2.0 %copy.13.up_ref = f32[544,152]{1,0:T(8,128)} copy(f32[544,152]{0,1:T(8,128)} %param.14) | data formatting | bytes 661504 | tf_op args[3]
  7.3 0.0 collective-permute-done.5.refs_6_
  7.3 0.0 copy-start.2
  7.3 0.5 collective-permute-start.6
  7.8 0.9 %collective-permute-done.3.refs_4_ = f32[3,4,544]{2,1,0:T(4,128)S(1)} collective-permute-done((f32[3,4,544]{2,1,0:T(4,128)}, f32[3,4,544]{2,1,0:T(4,128)S(1)}, u32[]{:S(2)}, u32[]{:S(2)}) %collective-permute-start.3) | collective-permute-done | bytes 26144 | tf_op jit(solution)/shard_map/ppermute | solution.py:390
  8.7 0.0 copy-start.4
  8.7 0.0 collective-permute-start.4
  8.7 0.5 collective-permute-done.1.refs_2_
  9.2 0.0 copy-start.6
  9.2 0.0 collective-permute-start.2
  9.2 3.1 %membrane.2 = f32[32,4,128]{2,1,0:T(4,128)} custom-call(f32[3,4,544]{2,1,0:T(4,128)} %points_ref.3, f32[3,544]{1,0:T(4,128)} %refs_8_.3, f32[544,544]{1,0:T(8,128)} %refs_9_.3, f32[544,152]{1,0:T(8,128)} %copy.13.up_ref), custom_call_target="tpu_custom_call" | custom-call | flops 1000000000 | bytes 1000000 | tf_op jit(solution)/shard_map/membrane/pallas_call | solution.py:395
  12.4 0.0 copy-done.2
  12.4 0.0 copy-done.4
  12.4 0.0 copy-done.6
  12.4 5.3 %all-to-all-start = ((f32[32,4,128]{2,1,0:T(4,128)}), f32[32,4,128]{2,1,0:T(4,128)S(1)}, u32[]{:S(2)}, u32[]{:S(2)}) async-start(f32[32,4,128]{2,1,0:T(4,128)} %membrane.2), calls=%async_computation | async-start | bytes 131072 | tf_op jit(solution)/shard_map/all_to_all | solution.py:396
  18.4 0.0 collective-permute-done.refs_1_
  18.4 0.0 copy-start.8
  18.4 0.0 collective-permute-done.6.refs_7_
  18.4 0.0 copy-start.11
  18.4 0.0 collective-permute-done.4.refs_5_
  18.4 0.0 copy-start.13
  18.4 0.0 collective-permute-done.2.refs_3_
  18.5 0.5 copy-done.8
  19.0 0.0 copy-done.11
  19.0 0.0 copy-done.13
  19.0 0.6 copy-done.15
  19.6 11.2 %near.2.near_ref = f32[3,4,544]{2,1,0:T(4,128)} custom-call(s32[1,2]{1,0:T(1,128)} %target_ref.3, s32[1,2]{1,0:T(1,128)} %owner_ref.3, s32[1,2]{1,0:T(1,128)} %cell_ref.3, s32[1]{0:T(128)S(6)} %copy.15.count_ref, f32[3,4,544]{2,1,0:T(4,128)} %points_ref.3, f32[3,4,544]{2,1,0:T(4,128)} %points_ref.3, f32[3,4,544]{2,1,0:T(4,128)} %copy-done.8, ...), custom_call_target="tpu_custom_call" | custom-call | flops 4000000000 | bytes 1000000 | tf_op jit(solution)/shard_map/near/pallas_call | solution.py:404
  30.8 0.0 all-to-all-done.told_ref
  30.8 0.6 copy-done.1
  31.4 6.7 %far.2 = (f32[3,4,544]{2,1,0:T(4,128)}, f32[3,4,544]{2,1,0:T(4,128)}) custom-call(f32[32,4,128]{2,1,0:T(4,128)} %copy-done.1, f32[3,4,544]{2,1,0:T(4,128)} %points_ref.3, f32[3,4,544]{2,1,0:T(4,128)} %near.2.near_ref, f32[152,152]{1,0:T(8,128)} %m2m_ref.3, f32[3,152]{1,0:T(4,128)} %template_ref.3, f32[152,544]{1,0:T(8,128)} %down_ref.3), custom_call_target="tpu_custom_call" | custom-call | flops 2000000000 | bytes 1000000 | tf_op jit(solution)/shard_map/far/pallas_call | solution.py:414
  38.1 0.0 collective-permute-start.12
  38.1 3.2 %collective-permute-start.10 = (f32[3,4,544]{2,1,0:T(4,128)}, f32[3,4,544]{2,1,0:T(4,128)S(1)}, u32[]{:S(2)}, u32[]{:S(2)}) collective-permute-start(f32[3,4,544]{2,1,0:T(4,128)} %get-tuple-element.3.points_ref.own_ref.refs_0_), channel_id=1, source_target_pairs={{0,4},{1,5},{2,6},{3,7},{4,0},{5,1},{6,2},{7,3},{8,12},{9,13},{10,... | collective-permute-start | bytes 78344 | tf_op jit(solution)/shard_map/ppermute | solution.py:390
  41.3 0.3 collective-permute-start.8
  41.6 0.0 collective-permute-start.7
  41.6 1.5 %collective-permute-done.12.refs_6_ = f32[3,4,544]{2,1,0:T(4,128)S(1)} collective-permute-done((f32[3,4,544]{2,1,0:T(4,128)}, f32[3,4,544]{2,1,0:T(4,128)S(1)}, u32[]{:S(2)}, u32[]{:S(2)}) %collective-permute-start.12) | collective-permute-done | bytes 26144 | tf_op jit(solution)/shard_map/ppermute | solution.py:390
  43.1 0.0 collective-permute-start.13
  43.1 0.4 collective-permute-done.10.refs_4_
  43.5 0.1 collective-permute-start.11
  43.6 1.8 %collective-permute-done.8.refs_2_ = f32[3,4,544]{2,1,0:T(4,128)S(1)} collective-permute-done((f32[3,4,544]{2,1,0:T(4,128)}, f32[3,4,544]{2,1,0:T(4,128)S(1)}, u32[]{:S(2)}, u32[]{:S(2)}) %collective-permute-start.8) | collective-permute-done | bytes 26144 | tf_op jit(solution)/shard_map/ppermute | solution.py:390
  45.4 0.0 collective-permute-start.9
  45.4 3.2 %membrane.3 = f32[32,4,128]{2,1,0:T(4,128)} custom-call(f32[3,4,544]{2,1,0:T(4,128)} %get-tuple-element.3.points_ref.own_ref.refs_0_, f32[3,544]{1,0:T(4,128)} %refs_8_.3, f32[544,544]{1,0:T(8,128)} %refs_9_.3, f32[544,152]{1,0:T(8,128)} %copy.13.up_ref), custom_call_target="tpu_custom_call" | custom-call | flops 1000000000 | bytes 1000000 | tf_op jit(solution)/shard_map/membrane/pallas_call | solution.py:395
  48.6 0.0 copy-done.3
  48.6 0.0 copy-done.5
  48.6 0.0 copy-done.7
  48.6 4.7 %all-to-all-start.1 = ((f32[32,4,128]{2,1,0:T(4,128)}), f32[32,4,128]{2,1,0:T(4,128)S(1)}, u32[]{:S(2)}, u32[]{:S(2)}) async-start(f32[32,4,128]{2,1,0:T(4,128)} %membrane.3), calls=%async_computation.1 | async-start | bytes 131072 | tf_op jit(solution)/shard_map/all_to_all | solution.py:396
  53.3 0.0 collective-permute-done.7.refs_1_
  53.3 0.0 copy-start.9
  53.4 0.0 collective-permute-done.13.refs_7_
  53.4 0.0 copy-start.10
  53.4 0.0 collective-permute-done.11.refs_5_
  53.4 0.0 copy-start.12
  53.4 0.0 collective-permute-done.9.refs_3_
  53.4 0.5 copy-done.9
  54.0 0.0 copy-done.10
  54.0 0.0 copy-done.12
  54.0 0.6 copy-done.14
  54.6 11.2 %near.3.near_ref = f32[3,4,544]{2,1,0:T(4,128)} custom-call(s32[1,2]{1,0:T(1,128)} %target_ref.3, s32[1,2]{1,0:T(1,128)} %owner_ref.3, s32[1,2]{1,0:T(1,128)} %cell_ref.3, s32[1]{0:T(128)S(6)} %copy.15.count_ref, f32[3,4,544]{2,1,0:T(4,128)} %get-tuple-element.3.points_ref.own_ref.refs_0_, f32[3,4,544]{2,1,0:T(4,128)} %get-tuple-element.3.points_ref.own_ref.refs_0_, ...), custom_call_target="tpu_custom_call" | custom-call | flops 4000000000 | bytes 1000000 | tf_op jit(solution)/shard_map/near/pallas_call | solution.py:404
  65.8 0.0 all-to-all-done.1.told_ref
  65.8 0.6 copy-done
  66.4 6.7 %far.3 = (f32[3,4,544]{2,1,0:T(4,128)}, f32[3,4,544]{2,1,0:T(4,128)}) custom-call(f32[32,4,128]{2,1,0:T(4,128)} %copy-done, f32[3,4,544]{2,1,0:T(4,128)} %get-tuple-element.3.points_ref.own_ref.refs_0_, f32[3,4,544]{2,1,0:T(4,128)} %near.3.near_ref, f32[152,152]{1,0:T(8,128)} %m2m_ref.3, f32[3,152]{1,0:T(4,128)} %template_ref.3, f32[152,544]{1,0:T(8,128)} %down_ref.3), custom_call_target="tpu_custom_call" | custom-call | flops 2000000000 | bytes 1000000 | tf_op jit(solution)/shard_map/far/pallas_call | solution.py:414
  (7 shorter events, 0.0 us)
Async XLA Ops:
  0.6 6.7 %collective-permute-start.5 = (f32[3,4,544]{2,1,0:T(4,128)}, f32[3,4,544]{2,1,0:T(4,128)S(1)}, u32[]{:S(2)}, u32[]{:S(2)}) collective-permute-start(f32[3,4,544]{2,1,0:T(4,128)} %points_ref.3), channel_id=1, source_target_pairs={{0,6},{1,7},{2,4},{3,5},{4,2},{5,3},{6,0},{7,1},{8,14},{9,15},{10,... | collective-permute-start | bytes 78344 | tf_op jit(solution)/shard_map/ppermute | solution.py:390
  4.6 4.1 %collective-permute-start.3 = (f32[3,4,544]{2,1,0:T(4,128)}, f32[3,4,544]{2,1,0:T(4,128)S(1)}, u32[]{:S(2)}, u32[]{:S(2)}) collective-permute-start(f32[3,4,544]{2,1,0:T(4,128)} %points_ref.3), channel_id=1, source_target_pairs={{0,4},{1,5},{2,6},{3,7},{4,0},{5,1},{6,2},{7,3},{8,12},{9,13},{10,... | collective-permute-start | bytes 78344 | tf_op jit(solution)/shard_map/ppermute | solution.py:390
  5.1 4.1 %collective-permute-start.1 = (f32[3,4,544]{2,1,0:T(4,128)}, f32[3,4,544]{2,1,0:T(4,128)S(1)}, u32[]{:S(2)}, u32[]{:S(2)}) collective-permute-start(f32[3,4,544]{2,1,0:T(4,128)} %points_ref.3), channel_id=1, source_target_pairs={{0,2},{1,3},{2,0},{3,1},{4,6},{5,7},{6,4},{7,5},{8,10},{9,11},{10,... | collective-permute-start | bytes 78344 | tf_op jit(solution)/shard_map/ppermute | solution.py:390
  5.3 13.1 %collective-permute-start = (f32[3,4,544]{2,1,0:T(4,128)}, f32[3,4,544]{2,1,0:T(4,128)S(1)}, u32[]{:S(2)}, u32[]{:S(2)}) collective-permute-start(f32[3,4,544]{2,1,0:T(4,128)} %points_ref.3), channel_id=1, source_target_pairs={{0,1},{1,0},{2,3},{3,2},{4,5},{5,4},{6,7},{7,6},{8,9},{9,8},{10,11... | collective-permute-start | bytes 78344 | tf_op jit(solution)/shard_map/ppermute | solution.py:390
  7.3 5.1 %copy-start.2 = (f32[3,4,544]{2,1,0:T(4,128)}, f32[3,4,544]{2,1,0:T(4,128)S(1)}, u32[]{:S(2)}) copy-start(f32[3,4,544]{2,1,0:T(4,128)S(1)} %collective-permute-done.5.refs_6_) | copy-start | bytes 78340
  7.3 11.1 %collective-permute-start.6 = (f32[3,4,544]{2,1,0:T(4,128)S(1)}, f32[3,4,544]{2,1,0:T(4,128)S(1)}, u32[]{:S(2)}, u32[]{:S(2)}) collective-permute-start(f32[3,4,544]{2,1,0:T(4,128)S(1)} %collective-permute-done.5.refs_6_), channel_id=1, source_target_pairs={{0,1},{1,0},{2,3},{3,2},{4,5},{5,4},{6,7},{7,6},{8,9},{9,8},{10,11... | collective-permute-start | bytes 78344 | tf_op jit(solution)/shard_map/ppermute | solution.py:390
  8.7 3.7 %copy-start.4 = (f32[3,4,544]{2,1,0:T(4,128)}, f32[3,4,544]{2,1,0:T(4,128)S(1)}, u32[]{:S(2)}) copy-start(f32[3,4,544]{2,1,0:T(4,128)S(1)} %collective-permute-done.3.refs_4_) | copy-start | bytes 78340
  8.7 9.7 %collective-permute-start.4 = (f32[3,4,544]{2,1,0:T(4,128)S(1)}, f32[3,4,544]{2,1,0:T(4,128)S(1)}, u32[]{:S(2)}, u32[]{:S(2)}) collective-permute-start(f32[3,4,544]{2,1,0:T(4,128)S(1)} %collective-permute-done.3.refs_4_), channel_id=1, source_target_pairs={{0,1},{1,0},{2,3},{3,2},{4,5},{5,4},{6,7},{7,6},{8,9},{9,8},{10,11... | collective-permute-start | bytes 78344 | tf_op jit(solution)/shard_map/ppermute | solution.py:390
  9.2 3.2 %copy-start.6 = (f32[3,4,544]{2,1,0:T(4,128)}, f32[3,4,544]{2,1,0:T(4,128)S(1)}, u32[]{:S(2)}) copy-start(f32[3,4,544]{2,1,0:T(4,128)S(1)} %collective-permute-done.1.refs_2_) | copy-start | bytes 78340
  9.2 9.2 %collective-permute-start.2 = (f32[3,4,544]{2,1,0:T(4,128)S(1)}, f32[3,4,544]{2,1,0:T(4,128)S(1)}, u32[]{:S(2)}, u32[]{:S(2)}) collective-permute-start(f32[3,4,544]{2,1,0:T(4,128)S(1)} %collective-permute-done.1.refs_2_), channel_id=1, source_target_pairs={{0,1},{1,0},{2,3},{3,2},{4,5},{5,4},{6,7},{7,6},{8,9},{9,8},{10,11... | collective-permute-start | bytes 78344 | tf_op jit(solution)/shard_map/ppermute | solution.py:390
  12.4 18.4 %all-to-all-start = ((f32[32,4,128]{2,1,0:T(4,128)}), f32[32,4,128]{2,1,0:T(4,128)S(1)}, u32[]{:S(2)}, u32[]{:S(2)}) async-start(f32[32,4,128]{2,1,0:T(4,128)} %membrane.2), calls=%async_computation | async-start | bytes 131072 | tf_op jit(solution)/shard_map/all_to_all | solution.py:396
  18.4 0.6 copy-start.8
  18.4 0.6 copy-start.11
  18.4 0.6 copy-start.13
  19.0 0.6 copy-start.15
  30.8 0.6 copy-start.1
  38.1 5.0 %collective-permute-start.12 = (f32[3,4,544]{2,1,0:T(4,128)}, f32[3,4,544]{2,1,0:T(4,128)S(1)}, u32[]{:S(2)}, u32[]{:S(2)}) collective-permute-start(f32[3,4,544]{2,1,0:T(4,128)} %get-tuple-element.3.points_ref.own_ref.refs_0_), channel_id=1, source_target_pairs={{0,6},{1,7},{2,4},{3,5},{4,2},{5,3},{6,0},{7,1},{8,14},{9,15},{10,... | collective-permute-start | bytes 78344 | tf_op jit(solution)/shard_map/ppermute | solution.py:390
  38.1 5.4 %collective-permute-start.10 = (f32[3,4,544]{2,1,0:T(4,128)}, f32[3,4,544]{2,1,0:T(4,128)S(1)}, u32[]{:S(2)}, u32[]{:S(2)}) collective-permute-start(f32[3,4,544]{2,1,0:T(4,128)} %get-tuple-element.3.points_ref.own_ref.refs_0_), channel_id=1, source_target_pairs={{0,4},{1,5},{2,6},{3,7},{4,0},{5,1},{6,2},{7,3},{8,12},{9,13},{10,... | collective-permute-start | bytes 78344 | tf_op jit(solution)/shard_map/ppermute | solution.py:390
  41.3 4.1 %collective-permute-start.8 = (f32[3,4,544]{2,1,0:T(4,128)}, f32[3,4,544]{2,1,0:T(4,128)S(1)}, u32[]{:S(2)}, u32[]{:S(2)}) collective-permute-start(f32[3,4,544]{2,1,0:T(4,128)} %get-tuple-element.3.points_ref.own_ref.refs_0_), channel_id=1, source_target_pairs={{0,2},{1,3},{2,0},{3,1},{4,6},{5,7},{6,4},{7,5},{8,10},{9,11},{10,... | collective-permute-start | bytes 78344 | tf_op jit(solution)/shard_map/ppermute | solution.py:390
  41.6 11.7 %collective-permute-start.7 = (f32[3,4,544]{2,1,0:T(4,128)}, f32[3,4,544]{2,1,0:T(4,128)S(1)}, u32[]{:S(2)}, u32[]{:S(2)}) collective-permute-start(f32[3,4,544]{2,1,0:T(4,128)} %get-tuple-element.3.points_ref.own_ref.refs_0_), channel_id=1, source_target_pairs={{0,1},{1,0},{2,3},{3,2},{4,5},{5,4},{6,7},{7,6},{8,9},{9,8},{10,11... | collective-permute-start | bytes 78344 | tf_op jit(solution)/shard_map/ppermute | solution.py:390
  43.1 5.5 %copy-start.3 = (f32[3,4,544]{2,1,0:T(4,128)}, f32[3,4,544]{2,1,0:T(4,128)S(1)}, u32[]{:S(2)}) copy-start(f32[3,4,544]{2,1,0:T(4,128)S(1)} %collective-permute-done.12.refs_6_) | copy-start | bytes 78340
  43.1 10.3 %collective-permute-start.13 = (f32[3,4,544]{2,1,0:T(4,128)S(1)}, f32[3,4,544]{2,1,0:T(4,128)S(1)}, u32[]{:S(2)}, u32[]{:S(2)}) collective-permute-start(f32[3,4,544]{2,1,0:T(4,128)S(1)} %collective-permute-done.12.refs_6_), channel_id=1, source_target_pairs={{0,1},{1,0},{2,3},{3,2},{4,5},{5,4},{6,7},{7,6},{8,9},{9,8},{10,11... | collective-permute-start | bytes 78344 | tf_op jit(solution)/shard_map/ppermute | solution.py:390
  43.5 5.1 %copy-start.5 = (f32[3,4,544]{2,1,0:T(4,128)}, f32[3,4,544]{2,1,0:T(4,128)S(1)}, u32[]{:S(2)}) copy-start(f32[3,4,544]{2,1,0:T(4,128)S(1)} %collective-permute-done.10.refs_4_) | copy-start | bytes 78340
  43.5 9.9 %collective-permute-start.11 = (f32[3,4,544]{2,1,0:T(4,128)S(1)}, f32[3,4,544]{2,1,0:T(4,128)S(1)}, u32[]{:S(2)}, u32[]{:S(2)}) collective-permute-start(f32[3,4,544]{2,1,0:T(4,128)S(1)} %collective-permute-done.10.refs_4_), channel_id=1, source_target_pairs={{0,1},{1,0},{2,3},{3,2},{4,5},{5,4},{6,7},{7,6},{8,9},{9,8},{10,11... | collective-permute-start | bytes 78344 | tf_op jit(solution)/shard_map/ppermute | solution.py:390
  45.4 3.2 %copy-start.7 = (f32[3,4,544]{2,1,0:T(4,128)}, f32[3,4,544]{2,1,0:T(4,128)S(1)}, u32[]{:S(2)}) copy-start(f32[3,4,544]{2,1,0:T(4,128)S(1)} %collective-permute-done.8.refs_2_) | copy-start | bytes 78340
  45.4 8.0 %collective-permute-start.9 = (f32[3,4,544]{2,1,0:T(4,128)S(1)}, f32[3,4,544]{2,1,0:T(4,128)S(1)}, u32[]{:S(2)}, u32[]{:S(2)}) collective-permute-start(f32[3,4,544]{2,1,0:T(4,128)S(1)} %collective-permute-done.8.refs_2_), channel_id=1, source_target_pairs={{0,1},{1,0},{2,3},{3,2},{4,5},{5,4},{6,7},{7,6},{8,9},{9,8},{10,11... | collective-permute-start | bytes 78344 | tf_op jit(solution)/shard_map/ppermute | solution.py:390
  48.6 17.2 %all-to-all-start.1 = ((f32[32,4,128]{2,1,0:T(4,128)}), f32[32,4,128]{2,1,0:T(4,128)S(1)}, u32[]{:S(2)}, u32[]{:S(2)}) async-start(f32[32,4,128]{2,1,0:T(4,128)} %membrane.3), calls=%async_computation.1 | async-start | bytes 131072 | tf_op jit(solution)/shard_map/all_to_all | solution.py:396
  53.3 0.6 copy-start.9
  53.4 0.6 copy-start.10
  53.4 0.6 copy-start.12
  54.0 0.6 copy-start.14
  65.8 0.6 copy-start

commit v3 on v2

v3 whole, which is shorter than its diff:
```python
import functools

import jax
import jax.numpy as jnp
from jax import lax
from jax.experimental import pallas as pl
from jax.experimental.pallas import tpu as pltpu
from jax.sharding import PartitionSpec as P


STEPS = 2
NEAR = 2

EPSILON_SQ = 0.25
VISCOSITY = 0.039788735772973836
TIME_STEP = 0.1
SKALAK_HARDEN = 2.0
CHECK_RADIUS = 1.0
DEVICE_RADIUS = 1.5
GROUP_RADIUS = 6.0

LANES = 128
SUB = 8
CHUNK = 544
BATCH = 3


def up8(n):
    return -(-n // SUB) * SUB


def split(a):
    high = a.astype(jnp.bfloat16)
    low = (a - high.astype(jnp.float32)).astype(jnp.bfloat16)
    return high, low


NN = (((1,), (0,)), ((), ()))
NT = (((1,), (1,)), ((), ()))


def dot3(a, b_parts, dims=NN):
    dot = functools.partial(
        lax.dot_general, dimension_numbers=dims, preferred_element_type=jnp.float32
    )
    rows = a.shape[0]
    first = a.astype(jnp.bfloat16).astype(jnp.float32)
    both = jnp.concatenate([first, a - first], axis=0).astype(jnp.bfloat16)
    high = dot(both, b_parts[0])
    return high[:rows] + (high[rows:] + dot(first.astype(jnp.bfloat16), b_parts[1]))


def harden(linear, stretch):
    return -linear * (1.0 + SKALAK_HARDEN * stretch / (1.0 + stretch))


def parts3(a):
    first = a.astype(jnp.bfloat16).astype(jnp.float32)
    rest = a - first
    second = rest.astype(jnp.bfloat16).astype(jnp.float32)
    return first, second, rest - second


def stack_left(a):
    first, second, third = parts3(a)
    return jnp.concatenate([first, first, first, second, second, third], axis=0)


def stack_right(a):
    first, second, third = parts3(a)
    return jnp.concatenate([first, second, third, first, second, first], axis=0)


def stack_pair(a):
    first, second, _ = parts3(a)
    return jnp.concatenate([first, second], axis=0).astype(jnp.bfloat16)


def rows8(rows):
    size = rows[0].shape[1]
    count = sum(row.shape[0] for row in rows)
    return jnp.concatenate(rows + [jnp.zeros((SUB - count, size), jnp.float32)], axis=0)


def square_of(place):
    return jnp.sum(place * place, axis=0, keepdims=True)


def target_rows(place):
    return rows8([place, square_of(place), jnp.ones_like(place[:1])])


def source_rows(place, force):
    near = rows8(
        [-2.0 * place, jnp.ones_like(place[:1]), square_of(place) + EPSILON_SQ]
    )
    along = rows8(
        [
            force,
            jnp.zeros_like(place[:1]),
            -jnp.sum(place * force, axis=0, keepdims=True),
        ]
    )
    return near, along


def weights(shifted, along):
    root = lax.rsqrt(jnp.maximum(shifted, EPSILON_SQ))
    inverse = root * root * root
    return split(root + EPSILON_SQ * inverse) + split(along * inverse)


def twice(a):
    return jnp.concatenate([a, a], axis=1)


def finish(place, direct, moment):
    direct = direct[:SUB] + direct[SUB:]
    moment = moment[:SUB] + moment[SUB:]
    return VISCOSITY * (direct[0:3] + place * moment[3:4] - moment[0:3])


def membrane_kernel(points_ref, rest_ref, up_ref, *refs, fresh):
    count = 1 if fresh else 2
    stiffness_refs, out_ref = refs[:count], refs[count]
    split_refs, (rows_ref, flat_ref) = refs[count + 1 : -2], refs[-2:]
    cells, size = points_ref.shape[1:]
    q = up_ref.shape[0]
    tail = q - LANES
    rows_ref[...] = jnp.zeros_like(rows_ref)
    centers = []
    for k in range(3):
        own = points_ref[k]
        mean = jnp.mean(own, axis=1, keepdims=True)
        rows_ref[SUB * k : SUB * k + cells, :] = own - mean - rest_ref[k : k + 1, :]
        centers.append(jnp.mean(mean, axis=0, keepdims=True))
    if len(stiffness_refs) == 1:
        stiffness = split(stiffness_refs[0][...])
        for ref, part in zip(split_refs, stiffness):
            ref[...] = part
    else:
        stiffness = [ref[...] for ref in stiffness_refs]
    linear = dot3(rows_ref[...], stiffness)
    parts = [linear[SUB * k : SUB * (k + 1)] for k in range(3)]
    stretch = parts[0] * parts[0] + parts[1] * parts[1] + parts[2] * parts[2]
    sums = [jnp.sum(harden(part, stretch), axis=0, keepdims=True) for part in parts]
    summed = jnp.concatenate(sums + [jnp.zeros((SUB - 3, size), jnp.float32)], axis=0)
    flat_ref[...] = jnp.zeros_like(flat_ref)
    flat_ref[:, :q] = dot3(summed, split(up_ref[...]), NT)
    ends = flat_ref[:, LANES:]
    last = ends[0:1]
    lane = lax.broadcasted_iota(jnp.int32, (1, LANES), 1)
    for k in range(1, 3):
        last = last + pltpu.roll(ends[k : k + 1], tail * k, axis=1)
    for k in range(3):
        last = jnp.where(lane == 3 * tail + k, centers[k], last)
    message = jnp.concatenate([flat_ref[0:3, :LANES], last], axis=0)
    out_ref[...] = jnp.broadcast_to(message[None], out_ref.shape)


def pick(block, row):
    rows = lax.broadcasted_iota(jnp.int32, (block.shape[0], 1), 0)
    return jnp.sum(jnp.where(rows == row, block, 0.0), axis=0, keepdims=True)


def near_kernel(
    target_ref,
    owner_ref,
    cell_ref,
    count_ref,
    own_ref,
    *refs,
    spread,
):
    pool_refs, (rest_ref, high_ref, low_ref, out_ref, rows_ref, move_ref) = (
        refs[:-6],
        refs[-6:],
    )
    size = own_ref.shape[2]
    me = lax.axis_index("dev")
    rows_ref[...] = jnp.zeros_like(rows_ref)
    move_ref[...] = jnp.zeros_like(move_ref)
    for slot in range(NEAR):
        cell = cell_ref[0, slot]
        owner = owner_ref[0, slot]
        if spread:
            for mask, pool_ref in enumerate(pool_refs):

                @pl.when((owner ^ me) == mask)
                def _(pool_ref=pool_ref):
                    for k in range(3):
                        rows_ref[SUB * slot + k : SUB * slot + k + 1, :] = pick(pool_ref[k], cell)
        else:
            for k in range(3):
                rows_ref[SUB * slot + k : SUB * slot + k + 1, :] = pick(
                    pool_refs[0][owner, k], cell
                )
    sources = rows_ref[...]
    for slot in range(NEAR):
        own = sources[SUB * slot : SUB * slot + 3]
        mean = jnp.mean(own, axis=1, keepdims=True)
        move_ref[SUB * slot : SUB * slot + 3, :] = own - mean - rest_ref[...]
    linear = dot3(move_ref[...], (high_ref[...], low_ref[...]))
    square = linear * linear
    for slot in range(NEAR):
        part = linear[SUB * slot : SUB * slot + 3]
        stretch = jnp.sum(square[SUB * slot : SUB * slot + 3], axis=0, keepdims=True)
        rows_ref[SUB * slot + 3 : SUB * slot + 6, :] = harden(part, stretch)
    dot = functools.partial(jnp.dot, preferred_element_type=jnp.float32)
    results = []
    for slot in range(NEAR):
        aim = jnp.concatenate([pick(own_ref[k], target_ref[0, slot]) for k in range(3)], axis=0)
        center = jnp.mean(aim, axis=1, keepdims=True)
        aim = aim - center
        place = rows_ref[SUB * slot : SUB * slot + 3, :] - center
        force = rows_ref[SUB * slot + 3 : SUB * slot + 6, :]
        near, along = source_rows(place, force)
        near = jnp.transpose(stack_left(near)).astype(jnp.bfloat16)
        along = jnp.transpose(stack_left(along)).astype(jnp.bfloat16)
        right = stack_right(target_rows(aim)).astype(jnp.bfloat16)
        forces = stack_pair(rows8([force]))
        places = stack_pair(rows8([place, jnp.ones_like(place[:1])]))
        direct = jnp.zeros((2 * SUB, size), jnp.float32)
        moment = direct
        for row in range(0, size, CHUNK):
            part = slice(row, min(row + CHUNK, size))
            both = weights(dot(near[part], right), dot(along[part], right))
            direct += dot(twice(forces[:, part]), jnp.concatenate(both[:2], axis=0))
            moment += dot(twice(places[:, part]), jnp.concatenate(both[2:], axis=0))
        results.append(jnp.where(slot < count_ref[0], finish(aim, direct, moment), 0.0))
    cells = lax.broadcasted_iota(jnp.int32, (out_ref.shape[1], 1), 0)
    for k in range(3):
        out_ref[k] = sum(
            jnp.where(cells == target_ref[0, slot], results[slot][k : k + 1], 0.0)
            for slot in range(NEAR)
        )


def boxes(main, ends, center, template, radius, per_row):
    count = main[0].shape[0]
    tail_lanes = template[2]
    rows = []
    for k in range(3):
        place_main = center[k] + radius * template[0][k : k + 1]
        place_ends = jnp.where(tail_lanes, center[k] + radius * template[1][k : k + 1], 0.0)
        rows.append((place_main, place_ends))
    for k in range(3):
        rows.append((main[k], ends[k]))
    packed = []
    for whole, part in rows:
        turn = lax.broadcasted_iota(jnp.int32, (count, 1), 0) % per_row[0]
        shifted = jnp.where(turn == 0, part, 0.0)
        for i in range(1, per_row[0]):
            shifted += jnp.where(turn == i, pltpu.roll(part, per_row[1] * i, axis=1), 0.0)
        packed.append(
            [whole]
            + [
                jnp.sum(shifted[a : min(a + per_row[0], count)], axis=0, keepdims=True)
                for a in range(0, count, per_row[0])
            ]
        )
    return packed


def far_kernel(
    told_ref,
    points_ref,
    near_ref,
    m2m_ref,
    template_ref,
    down_ref,
    points_out_ref,
    velocity_ref,
    wide_ref,
    sums_ref,
    group_ref,
    source_ref,
    *,
    groups,
    devs,
):
    q = template_ref.shape[1]
    tail = q - LANES
    per_row = (LANES // tail, tail)
    group = lax.axis_index("grp")
    dev = lax.axis_index("dev")
    lane = lax.broadcasted_iota(jnp.int32, (1, LANES), 1)
    tail_lanes = lane < tail

    def ends_of(row, k):
        moved = pltpu.roll(row, LANES - tail * k, axis=1) if k else row
        return jnp.where(tail_lanes, moved, 0.0)

    wide_ref[...] = jnp.zeros_like(wide_ref)
    wide_ref[0:3, :q] = template_ref[...]
    template = (wide_ref[:, :LANES], wide_ref[:, LANES:], tail_lanes)

    first = group * devs
    own_rows = [told_ref[pl.ds(first, devs), k, :] for k in range(4)]
    others = lax.broadcasted_iota(jnp.int32, (devs, 1), 0) != dev
    inner = boxes(
        [jnp.where(others, own_rows[k], 0.0) for k in range(3)],
        [jnp.where(others, ends_of(own_rows[3], k), 0.0) for k in range(3)],
        [own_rows[3][:, 3 * tail + k : 3 * tail + k + 1] for k in range(3)],
        template,
        DEVICE_RADIUS,
        per_row,
    )

    span = up8(groups)
    sums_ref[...] = jnp.zeros_like(sums_ref)
    for h in range(groups):
        sums_ref[h] = jnp.sum(told_ref[h * devs : (h + 1) * devs], axis=0)
    sum_rows = [sums_ref[:, k, :] for k in range(4)]
    for k in range(3):
        group_ref[span * k : span * (k + 1), :LANES] = sum_rows[k]
        group_ref[span * k : span * (k + 1), LANES:] = ends_of(sum_rows[3], k)
    shifted = dot3(group_ref[:, :q], split(m2m_ref[...]))
    group_ref[:, :q] = shifted
    other_groups = lax.broadcasted_iota(jnp.int32, (span, 1), 0) != group
    outer = boxes(
        [
            jnp.where(other_groups, group_ref[span * k : span * (k + 1), :LANES], 0.0)
            for k in range(3)
        ],
        [
            jnp.where(other_groups, group_ref[span * k : span * (k + 1), LANES:], 0.0)
            for k in range(3)
        ],
        [sum_rows[3][:, 3 * tail + k : 3 * tail + k + 1] / devs for k in range(3)],
        template,
        GROUP_RADIUS,
        per_row,
    )
    source_ref[...] = jnp.zeros_like(source_ref)
    rows = 0
    center_row = told_ref[pl.ds(first + dev, 1), 3, :]
    centers = [center_row[:, 3 * tail + k : 3 * tail + k + 1] for k in range(3)]
    for part, count in ((inner, devs), (outer, groups)):
        ends = -(-count // per_row[0])
        for index in range(6):
            shift = centers[index] if index < 3 else 0.0
            source_ref[rows : rows + count, index, :] = part[index][0][:count] - shift
            for j in range(ends):
                at = rows + count + j
                source_ref[at : at + 1, index, :] = part[index][1 + j] - shift
        rows += count + ends
    tall = up8(up8(q) // 2) * 2
    targets = CHECK_RADIUS * wide_ref[0:3, :]
    left = jnp.transpose(stack_left(target_rows(targets)))[:tall].astype(jnp.bfloat16)
    targets = targets[:, :tall]
    contract = functools.partial(
        lax.dot_general,
        dimension_numbers=NT,
        preferred_element_type=jnp.float32,
    )
    dot = functools.partial(jnp.dot, preferred_element_type=jnp.float32)
    direct = jnp.zeros((2 * SUB, tall), jnp.float32)
    moment = jnp.zeros((2 * SUB, tall), jnp.float32)
    for row in range(0, source_ref.shape[0], BATCH):
        block = jnp.concatenate([source_ref[row + i] for i in range(BATCH)], axis=1)
        place = block[0:3]
        force = block[3:6]
        near, along = source_rows(place, force)
        both = weights(
            dot(left, stack_right(near).astype(jnp.bfloat16)),
            dot(left, stack_right(along).astype(jnp.bfloat16)),
        )
        forces = stack_pair(rows8([force]))
        places = stack_pair(rows8([place, jnp.ones_like(place[:1])]))
        direct += contract(twice(forces), jnp.concatenate(both[:2], axis=1))
        moment += contract(twice(places), jnp.concatenate(both[2:], axis=1))
    checks = jnp.concatenate(
        [finish(targets, direct, moment)[:, :q], jnp.zeros((SUB - 3, q), jnp.float32)], axis=0
    )
    surface = dot3(checks, split(down_ref[...]))
    for k in range(3):
        velocity = surface[k : k + 1] + near_ref[k]
        velocity_ref[k] = velocity
        points_out_ref[k] = points_ref[k] + TIME_STEP * velocity


PARAMS = pltpu.CompilerParams(vmem_limit_bytes=20 * 2**20)
VMEM = pl.BlockSpec(memory_space=pltpu.VMEM)
SMEM = pl.BlockSpec(memory_space=pltpu.SMEM)


def float32(*shape):
    return jax.ShapeDtypeStruct(shape, jnp.float32)


def body(
    positions,
    rest_shape,
    stiffness,
    up_map,
    down_map,
    m2m,
    box_template,
    near_target,
    near_owner,
    near_cell,
    near_count,
):
    devs = lax.axis_size("dev")
    groups = lax.axis_size("grp")
    cells, size = positions.shape[1:]
    q = up_map.shape[1]
    spread = devs == 8
    span = up8(groups)
    tail_boxes = LANES // (q - LANES)
    source_count = devs + groups + -(-devs // tail_boxes) + -(-groups // tail_boxes)

    def membrane(*args):
        fresh = len(args) == 4
        told = float32(groups * devs, 4, LANES)
        part = jax.ShapeDtypeStruct((size, size), jnp.bfloat16)
        return pl.pallas_call(
            functools.partial(membrane_kernel, fresh=fresh),
            out_shape=(told, part, part) if fresh else (told,),
            in_specs=[VMEM] * len(args),
            out_specs=(VMEM,) * (3 if fresh else 1),
            scratch_shapes=[
                pltpu.VMEM((3 * SUB, size), jnp.float32),
                pltpu.VMEM((SUB, 2 * LANES), jnp.float32),
            ],
            name="membrane",
            compiler_params=PARAMS,
            cost_estimate=pl.CostEstimate(flops=10**9, bytes_accessed=10**6, transcendentals=0),
        )(*args)

    pools = 8 if spread else 1
    near = pl.pallas_call(
        functools.partial(near_kernel, spread=spread),
        out_shape=float32(3, cells, size),
        in_specs=[SMEM] * 4 + [VMEM] * (1 + pools + 3),
        out_specs=VMEM,
        scratch_shapes=[
            pltpu.VMEM((NEAR * SUB, size), jnp.float32),
            pltpu.VMEM((NEAR * SUB, size), jnp.float32),
        ],
        name="near",
        compiler_params=PARAMS,
        cost_estimate=pl.CostEstimate(flops=4 * 10**9, bytes_accessed=10**6, transcendentals=0),
    )
    far = pl.pallas_call(
        functools.partial(far_kernel, groups=groups, devs=devs),
        out_shape=(float32(3, cells, size), float32(3, cells, size)),
        in_specs=[VMEM] * 6,
        out_specs=(VMEM, VMEM),
        scratch_shapes=[
            pltpu.VMEM((SUB, 2 * LANES), jnp.float32),
            pltpu.VMEM((span, 4, LANES), jnp.float32),
            pltpu.VMEM((3 * span, 2 * LANES), jnp.float32),
            pltpu.VMEM((-(-source_count // BATCH) * BATCH, SUB, LANES), jnp.float32),
        ],
        name="far",
        compiler_params=PARAMS,
        cost_estimate=pl.CostEstimate(flops=2 * 10**9, bytes_accessed=10**6, transcendentals=0),
    )

    def to(array, mask):
        return lax.ppermute(array, "dev", [(j, j ^ mask) for j in range(devs)])

    points = positions
    velocity = None
    parts = [stiffness]
    for _ in range(STEPS):
        message, *fresh = membrane(points, rest_shape, up_map.T, *parts)
        parts = fresh or parts
        told = lax.all_to_all(message, ("grp", "dev"), 0, 0)
        if spread:
            pool = [to(points, 6)]
            pool = [points] + [to(points, mask) for mask in (2, 4)] + pool
            twins = [to(points, 1)]
            twins += [to(array, 1) for array in pool[1:]]
            pool = [(pool, twins)[mask % 2][mask // 2] for mask in range(8)]
        else:
            copies = jnp.broadcast_to(points[None], (devs,) + points.shape)
            pool = [lax.all_to_all(copies, "dev", 0, 0)]
        close = near(
            near_target,
            near_owner,
            near_cell,
            near_count,
            points,
            *pool,
            rest_shape,
            *parts,
        )
        points, velocity = far(told, points, close, m2m, box_template, down_map)
    return (points, velocity)


def solution(mesh):
    both = ("grp", "dev")
    return jax.shard_map(
        body,
        mesh=mesh,
        in_specs=(P(None, both, None),) + (P(),) * 6 + (P(both, None),) * 3 + (P(both),),
        out_specs=(P(None, both, None), P(None, both, None)),
        check_vma=False,
    )
```

time: 73.5 us -> 49.6 us (0.67)
  Pallas kernels: 42 us -> 14 us
  waiting for transfers between devices: 5.14 us -> 13.6 us
  starting transfers between devices: 18.8 us -> 16.3 us
  local copies, waits for them, and re-layouts: 5.69 us -> 3.84 us
    pallas_call x2, Pallas kernels: 22.4 us -> 6.16 us  [body(): near(near_target, near_owner, near_cell, near_count, points, *pool, rest_...]
    pallas_call x2, Pallas kernels: 13.3 us -> 4.99 us  [body(): points, velocity = far(told, points, close, m2m, box_template, down_map)]
    all_to_all x2, waiting for transfers between devices: 0.01 us -> 7.82 us  [body(): told = lax.all_to_all(message, ('grp', 'dev'), 0, 0)]
    pallas_call x2, Pallas kernels: 6.3 us -> 2.87 us  [membrane(): pl.pallas_call(functools.partial(membrane_kernel, fresh=fresh), out_shape...]
    all_to_all x2, starting transfers between devices: 10 us -> 7.61 us  [body(): told = lax.all_to_all(message, ('grp', 'dev'), 0, 0)]
    unnamed x33 -> x26, local copies, waits for them, and re-layouts: 5.69 us -> 3.84 us
  transfers between devices with their start and end apart: 16 -> 16, of which waited for: 5 -> 7; matrix products, arithmetic and copies ran while one was open for 3% -> 0% of each run, Pallas kernels for 39% -> 18%
where the time goes in v3:
time: 49.6 us; the launch traced here: 49.2 us
  starting transfers between devices  16.3 us (33%)
  Pallas kernels  14 us (28%)
  waiting for transfers between devices  13.6 us (27%)
  local copies, waits for them, and re-layouts  3.84 us (8%)
  between operations  1.47 us (3%)
    ppermute x14, starting transfers between devices, to(): return lax.ppermute(array, 'dev', [(j, j ^ mask) for j in range(devs)])  8.65 us
    all_to_all x2, waiting for transfers between devices, body(): told = lax.all_to_all(message, ('grp', 'dev'), 0, 0)  7.82 us
    all_to_all x2, starting transfers between devices, body(): told = lax.all_to_all(message, ('grp', 'dev'), 0, 0)  7.61 us
    pallas_call x2, Pallas kernels, body(): near(near_target, near_owner, near_cell, near_count, points, *pool, rest_...  6.16 us
    ppermute x14, waiting for transfers between devices, to(): return lax.ppermute(array, 'dev', [(j, j ^ mask) for j in range(devs)])  5.76 us
    pallas_call x2, Pallas kernels, body(): points, velocity = far(told, points, close, m2m, box_template, down_map)  4.99 us
    unnamed x26, local copies, waits for them, and re-layouts  3.84 us
    pallas_call x2, Pallas kernels, membrane(): pl.pallas_call(functools.partial(membrane_kernel, fresh=fresh), out_shape...  2.87 us
  transfers between devices with their start and end apart: 16, of which 7 were waited for; matrix products, arithmetic and copies ran while one was open for 0% of the time, Pallas kernels for 18%

profile of v3, /device:TPU:0, one launch (start us, length us, event | category | flops | bytes accessed | tf_op | source)
XLA Modules:
  0.0 49.2 jit_solution(7256628693141472455)
XLA Ops:
  0.6 4.0 %collective-permute-start.5 = (f32[3,4,544]{2,1,0:T(4,128)}, f32[3,4,544]{2,1,0:T(4,128)S(1)}, u32[]{:S(2)}, u32[]{:S(2)}) collective-permute-start(f32[3,4,544]{2,1,0:T(4,128)} %points_ref.3), channel_id=1, source_target_pairs={{0,6},{1,7},{2,4},{3,5},{4,2},{5,3},{6,0},{7,1},{8,14},{9,15},{10,... | collective-permute-start | bytes 78344 | tf_op jit(solution)/shard_map/ppermute | solution.py:463
  4.6 0.5 %collective-permute-start.3 = (f32[3,4,544]{2,1,0:T(4,128)}, f32[3,4,544]{2,1,0:T(4,128)S(1)}, u32[]{:S(2)}, u32[]{:S(2)}) collective-permute-start(f32[3,4,544]{2,1,0:T(4,128)} %points_ref.3), channel_id=1, source_target_pairs={{0,4},{1,5},{2,6},{3,7},{4,0},{5,1},{6,2},{7,3},{8,12},{9,13},{10,... | collective-permute-start | bytes 78344 | tf_op jit(solution)/shard_map/ppermute | solution.py:463
  5.1 0.1 collective-permute-start.1
  5.3 0.0 collective-permute-start
  5.3 1.4 %collective-permute-done.5.refs_6_ = f32[3,4,544]{2,1,0:T(4,128)S(1)} collective-permute-done((f32[3,4,544]{2,1,0:T(4,128)}, f32[3,4,544]{2,1,0:T(4,128)S(1)}, u32[]{:S(2)}, u32[]{:S(2)}) %collective-permute-start.5) | collective-permute-done | bytes 26144 | tf_op jit(solution)/shard_map/ppermute | solution.py:463
  6.7 0.0 collective-permute-start.6
  6.7 2.0 %collective-permute-done.3.refs_4_ = f32[3,4,544]{2,1,0:T(4,128)S(1)} collective-permute-done((f32[3,4,544]{2,1,0:T(4,128)}, f32[3,4,544]{2,1,0:T(4,128)S(1)}, u32[]{:S(2)}, u32[]{:S(2)}) %collective-permute-start.3) | collective-permute-done | bytes 26144 | tf_op jit(solution)/shard_map/ppermute | solution.py:463
  8.7 0.0 collective-permute-start.4
  8.7 0.5 %collective-permute-done.1.refs_2_ = f32[3,4,544]{2,1,0:T(4,128)S(1)} collective-permute-done((f32[3,4,544]{2,1,0:T(4,128)}, f32[3,4,544]{2,1,0:T(4,128)S(1)}, u32[]{:S(2)}, u32[]{:S(2)}) %collective-permute-start.1) | collective-permute-done | bytes 26144 | tf_op jit(solution)/shard_map/ppermute | solution.py:463
  9.2 0.0 collective-permute-start.2
  9.2 0.0 copy-start
  9.2 1.3 %copy-done = f32[544,544]{1,0:T(8,128)S(1)} copy-done((f32[544,544]{1,0:T(8,128)S(1)}, f32[544,544]{1,0:T(8,128)}, u32[]{:S(2)}) %copy-start) | copy-done | bytes 1183768
  10.6 0.0 copy-start.1
  10.6 1.0 %copy-done.1 = f32[544,152]{0,1:T(8,128)S(1)} copy-done((f32[544,152]{0,1:T(8,128)S(1)}, f32[544,152]{0,1:T(8,128)}, u32[]{:S(2)}) %copy-start.1) | copy-done | bytes 330776
  11.6 0.0 copy-start.5
  11.6 0.8 %copy-done.5 = f32[3,4,544]{2,1,0:T(4,128)S(1)} copy-done((f32[3,4,544]{2,1,0:T(4,128)S(1)}, f32[3,4,544]{2,1,0:T(4,128)}, u32[]{:S(2)}) %copy-start.5) | copy-done | bytes 26136
  12.3 0.0 copy-start.7
  12.3 0.7 %copy-done.7 = f32[3,544]{1,0:T(4,128)S(1)} copy-done((f32[3,544]{1,0:T(4,128)S(1)}, f32[3,544]{1,0:T(4,128)}, u32[]{:S(2)}) %copy-start.7) | copy-done | bytes 6552
  13.0 0.0 copy-start.6
  13.0 0.0 copy-start.8
  13.0 0.0 copy-start.10
  13.0 0.0 copy-start.11
  13.0 0.0 copy-start.12
  13.1 1.5 %membrane.2 = (f32[32,4,128]{2,1,0:T(4,128)}, bf16[544,544]{1,0:T(8,128)(2,1)S(1)}, bf16[544,544]{1,0:T(8,128)(2,1)S(1)}) custom-call(f32[3,4,544]{2,1,0:T(4,128)S(1)} %copy-done.5, f32[3,544]{1,0:T(4,128)S(1)} %copy-done.7, f32[152,544]{1,0:T(8,128)S(1)} %bitcast.1, f32[544,544]{1,0:T(8,128)S(1)} %copy-done), custom_call_target="tpu_custom_call" | custom-call | flops 1000000000 | bytes 1000000 | tf_op jit(solution)/shard_map/membrane/pallas_call | solution.py:418
  14.6 5.0 %all-to-all-start = ((f32[32,4,128]{2,1,0:T(4,128)}), f32[32,4,128]{2,1,0:T(4,128)S(1)}, u32[]{:S(2)}, u32[]{:S(2)}) async-start(f32[32,4,128]{2,1,0:T(4,128)} %get-tuple-element.6), calls=%async_computation | async-start | bytes 131072 | tf_op jit(solution)/shard_map/all_to_all | solution.py:471
  20.3 0.0 collective-permute-done.refs_1_
  20.3 0.0 collective-permute-done.6.refs_7_
  20.3 0.0 collective-permute-done.4.refs_5_
  20.3 0.0 collective-permute-done.2.refs_3_
  20.3 0.0 copy-done.6
  20.3 0.0 copy-done.8
  20.3 0.0 copy-done.10
  20.3 0.0 copy-done.11
  20.3 0.0 copy-done.12
  20.3 0.0 copy-start.3
  20.4 0.0 copy-start.4
  20.4 0.0 copy-start.9
  20.4 3.1 %near.2.near_ref = f32[3,4,544]{2,1,0:T(4,128)S(1)} custom-call(s32[1,2]{1,0:T(1,128)S(1)} %copy-done.10, s32[1,2]{1,0:T(1,128)S(1)} %copy-done.11, s32[1,2]{1,0:T(1,128)S(1)} %copy-done.12, s32[1]{0:T(128)S(6)} %copy.13.count_ref, f32[3,4,544]{2,1,0:T(4,128)S(1)} %copy-done.6, f32[3,4,544]{2,1,0:T(4,128)S(1)} %copy-done.6, ...), custom_call_target="tpu_custom_call" | custom-call | flops 4000000000 | bytes 1000000 | tf_op jit(solution)/shard_map/near/pallas_call | solution.py:481
  23.5 0.0 copy-start.2
  23.5 3.5 %all-to-all-done.told_ref = f32[32,4,128]{2,1,0:T(4,128)S(1)} async-done(((f32[32,4,128]{2,1,0:T(4,128)}), f32[32,4,128]{2,1,0:T(4,128)S(1)}, u32[]{:S(2)}, u32[]{:S(2)}) %all-to-all-start) | async-done | bytes 65568 | tf_op jit(solution)/shard_map/all_to_all | solution.py:471
  27.0 0.0 copy-done.3
  27.0 0.0 copy-done.4
  27.0 0.0 copy-done.9
  27.0 2.5 %far.2 = (f32[3,4,544]{2,1,0:T(4,128)S(1)}, f32[3,4,544]{2,1,0:T(4,128)}) custom-call(f32[32,4,128]{2,1,0:T(4,128)S(1)} %all-to-all-done.told_ref, f32[3,4,544]{2,1,0:T(4,128)S(1)} %copy-done.6, f32[3,4,544]{2,1,0:T(4,128)S(1)} %near.2.near_ref, f32[152,152]{1,0:T(8,128)S(1)} %copy-done.4, f32[3,152]{1,0:T(4,128)S(1)} %copy-done.9, f32[152,544]{1,0:T(8,128)S(1)} %copy-done.3), custom_call_target="tpu_custom_call" | custom-call | flops 2000000000 | bytes 1000000 | tf_op jit(solution)/shard_map/far/pallas_call | solution.py:491
  29.5 0.7 %collective-permute-start.12 = (f32[3,4,544]{2,1,0:T(4,128)S(1)}, f32[3,4,544]{2,1,0:T(4,128)S(1)}, u32[]{:S(2)}, u32[]{:S(2)}) collective-permute-start(f32[3,4,544]{2,1,0:T(4,128)S(1)} %get-tuple-element.9.points_ref.own_ref.refs_0_), channel_id=1, source_target_pairs={{0,6},{1,7},{2,4},{3,5},{4,2},{5,3},{6,0},{7,1},{8,14},{9,15},{10,... | collective-permute-start | bytes 78344 | tf_op jit(solution)/shard_map/ppermute | solution.py:463
  30.2 1.2 %collective-permute-start.10 = (f32[3,4,544]{2,1,0:T(4,128)S(1)}, f32[3,4,544]{2,1,0:T(4,128)S(1)}, u32[]{:S(2)}, u32[]{:S(2)}) collective-permute-start(f32[3,4,544]{2,1,0:T(4,128)S(1)} %get-tuple-element.9.points_ref.own_ref.refs_0_), channel_id=1, source_target_pairs={{0,4},{1,5},{2,6},{3,7},{4,0},{5,1},{6,2},{7,3},{8,12},{9,13},{10,... | collective-permute-start | bytes 78344 | tf_op jit(solution)/shard_map/ppermute | solution.py:463
  31.4 1.6 %collective-permute-start.8 = (f32[3,4,544]{2,1,0:T(4,128)S(1)}, f32[3,4,544]{2,1,0:T(4,128)S(1)}, u32[]{:S(2)}, u32[]{:S(2)}) collective-permute-start(f32[3,4,544]{2,1,0:T(4,128)S(1)} %get-tuple-element.9.points_ref.own_ref.refs_0_), channel_id=1, source_target_pairs={{0,2},{1,3},{2,0},{3,1},{4,6},{5,7},{6,4},{7,5},{8,10},{9,11},{10,... | collective-permute-start | bytes 78344 | tf_op jit(solution)/shard_map/ppermute | solution.py:463
  33.0 0.0 collective-permute-start.7
  33.0 1.4 %collective-permute-done.12.refs_6_ = f32[3,4,544]{2,1,0:T(4,128)S(1)} collective-permute-done((f32[3,4,544]{2,1,0:T(4,128)S(1)}, f32[3,4,544]{2,1,0:T(4,128)S(1)}, u32[]{:S(2)}, u32[]{:S(2)}) %collective-permute-start.12) | collective-permute-done | bytes 26144 | tf_op jit(solution)/shard_map/ppermute | solution.py:463
  34.5 0.0 collective-permute-start.13
  34.5 0.0 collective-permute-done.10.refs_4_
  34.5 0.5 %collective-permute-start.11 = (f32[3,4,544]{2,1,0:T(4,128)S(1)}, f32[3,4,544]{2,1,0:T(4,128)S(1)}, u32[]{:S(2)}, u32[]{:S(2)}) collective-permute-start(f32[3,4,544]{2,1,0:T(4,128)S(1)} %collective-permute-done.10.refs_4_), channel_id=1, source_target_pairs={{0,1},{1,0},{2,3},{3,2},{4,5},{5,4},{6,7},{7,6},{8,9},{9,8},{10,11... | collective-permute-start | bytes 78344 | tf_op jit(solution)/shard_map/ppermute | solution.py:463
  35.0 0.3 collective-permute-done.8.refs_2_
  35.3 0.0 collective-permute-start.9
  35.3 0.0 copy-done.2
  35.3 1.4 %membrane.3 = f32[32,4,128]{2,1,0:T(4,128)} custom-call(f32[3,4,544]{2,1,0:T(4,128)S(1)} %get-tuple-element.9.points_ref.own_ref.refs_0_, f32[3,544]{1,0:T(4,128)S(1)} %copy-done.8, f32[152,544]{1,0:T(8,128)S(1)} %bitcast.2, bf16[544,544]{1,0:T(8,128)(2,1)S(1)} %get-tuple-element.7.refs_9_.refs_0_, bf16[544,544]{1,0:T(8,128)(2,1)S(1)} %get-tuple-element.8.refs_10_.refs_1_), custom_call_target="tpu_custom_call" | custom-call | flops 1000000000 | bytes 1000000 | tf_op jit(solution)/shard_map/membrane/pallas_call | solution.py:418
  36.7 2.6 %all-to-all-start.1 = ((f32[32,4,128]{2,1,0:T(4,128)}), f32[32,4,128]{2,1,0:T(4,128)S(1)}, u32[]{:S(2)}, u32[]{:S(2)}) async-start(f32[32,4,128]{2,1,0:T(4,128)} %membrane.3), calls=%async_computation.1 | async-start | bytes 131072 | tf_op jit(solution)/shard_map/all_to_all | solution.py:471
  39.3 0.0 collective-permute-done.7.refs_1_
  39.3 0.0 collective-permute-done.13.refs_7_
  39.3 0.0 collective-permute-done.11.refs_5_
  39.3 0.0 collective-permute-done.9.refs_3_
  39.3 3.1 %near.3.near_ref = f32[3,4,544]{2,1,0:T(4,128)S(1)} custom-call(s32[1,2]{1,0:T(1,128)S(1)} %copy-done.10, s32[1,2]{1,0:T(1,128)S(1)} %copy-done.11, s32[1,2]{1,0:T(1,128)S(1)} %copy-done.12, s32[1]{0:T(128)S(6)} %copy.13.count_ref, f32[3,4,544]{2,1,0:T(4,128)S(1)} %get-tuple-element.9.points_ref.own_ref.refs_0_, ...), custom_call_target="tpu_custom_call" | custom-call | flops 4000000000 | bytes 1000000 | tf_op jit(solution)/shard_map/near/pallas_call | solution.py:481
  42.4 4.3 %all-to-all-done.1.told_ref = f32[32,4,128]{2,1,0:T(4,128)S(1)} async-done(((f32[32,4,128]{2,1,0:T(4,128)}), f32[32,4,128]{2,1,0:T(4,128)S(1)}, u32[]{:S(2)}, u32[]{:S(2)}) %all-to-all-start.1) | async-done | bytes 65568 | tf_op jit(solution)/shard_map/all_to_all | solution.py:471
  46.7 2.5 %far.3 = (f32[3,4,544]{2,1,0:T(4,128)}, f32[3,4,544]{2,1,0:T(4,128)}) custom-call(f32[32,4,128]{2,1,0:T(4,128)S(1)} %all-to-all-done.1.told_ref, f32[3,4,544]{2,1,0:T(4,128)S(1)} %get-tuple-element.9.points_ref.own_ref.refs_0_, f32[3,4,544]{2,1,0:T(4,128)S(1)} %near.3.near_ref, f32[152,152]{1,0:T(8,128)S(1)} %copy-done.4, f32[3,152]{1,0:T(4,128)S(1)} %copy-done.9, ...), custom_call_target="tpu_custom_call" | custom-call | flops 2000000000 | bytes 1000000 | tf_op jit(solution)/shard_map/far/pallas_call | solution.py:491
Async XLA Ops:
  0.6 6.1 %collective-permute-start.5 = (f32[3,4,544]{2,1,0:T(4,128)}, f32[3,4,544]{2,1,0:T(4,128)S(1)}, u32[]{:S(2)}, u32[]{:S(2)}) collective-permute-start(f32[3,4,544]{2,1,0:T(4,128)} %points_ref.3), channel_id=1, source_target_pairs={{0,6},{1,7},{2,4},{3,5},{4,2},{5,3},{6,0},{7,1},{8,14},{9,15},{10,... | collective-permute-start | bytes 78344 | tf_op jit(solution)/shard_map/ppermute | solution.py:463
  4.6 4.1 %collective-permute-start.3 = (f32[3,4,544]{2,1,0:T(4,128)}, f32[3,4,544]{2,1,0:T(4,128)S(1)}, u32[]{:S(2)}, u32[]{:S(2)}) collective-permute-start(f32[3,4,544]{2,1,0:T(4,128)} %points_ref.3), channel_id=1, source_target_pairs={{0,4},{1,5},{2,6},{3,7},{4,0},{5,1},{6,2},{7,3},{8,12},{9,13},{10,... | collective-permute-start | bytes 78344 | tf_op jit(solution)/shard_map/ppermute | solution.py:463
  5.1 4.1 %collective-permute-start.1 = (f32[3,4,544]{2,1,0:T(4,128)}, f32[3,4,544]{2,1,0:T(4,128)S(1)}, u32[]{:S(2)}, u32[]{:S(2)}) collective-permute-start(f32[3,4,544]{2,1,0:T(4,128)} %points_ref.3), channel_id=1, source_target_pairs={{0,2},{1,3},{2,0},{3,1},{4,6},{5,7},{6,4},{7,5},{8,10},{9,11},{10,... | collective-permute-start | bytes 78344 | tf_op jit(solution)/shard_map/ppermute | solution.py:463
  5.3 15.0 %collective-permute-start = (f32[3,4,544]{2,1,0:T(4,128)}, f32[3,4,544]{2,1,0:T(4,128)S(1)}, u32[]{:S(2)}, u32[]{:S(2)}) collective-permute-start(f32[3,4,544]{2,1,0:T(4,128)} %points_ref.3), channel_id=1, source_target_pairs={{0,1},{1,0},{2,3},{3,2},{4,5},{5,4},{6,7},{7,6},{8,9},{9,8},{10,11... | collective-permute-start | bytes 78344 | tf_op jit(solution)/shard_map/ppermute | solution.py:463
  6.7 13.6 %collective-permute-start.6 = (f32[3,4,544]{2,1,0:T(4,128)S(1)}, f32[3,4,544]{2,1,0:T(4,128)S(1)}, u32[]{:S(2)}, u32[]{:S(2)}) collective-permute-start(f32[3,4,544]{2,1,0:T(4,128)S(1)} %collective-permute-done.5.refs_6_), channel_id=1, source_target_pairs={{0,1},{1,0},{2,3},{3,2},{4,5},{5,4},{6,7},{7,6},{8,9},{9,8},{10,11... | collective-permute-start | bytes 78344 | tf_op jit(solution)/shard_map/ppermute | solution.py:463
  8.7 11.6 %collective-permute-start.4 = (f32[3,4,544]{2,1,0:T(4,128)S(1)}, f32[3,4,544]{2,1,0:T(4,128)S(1)}, u32[]{:S(2)}, u32[]{:S(2)}) collective-permute-start(f32[3,4,544]{2,1,0:T(4,128)S(1)} %collective-permute-done.3.refs_4_), channel_id=1, source_target_pairs={{0,1},{1,0},{2,3},{3,2},{4,5},{5,4},{6,7},{7,6},{8,9},{9,8},{10,11... | collective-permute-start | bytes 78344 | tf_op jit(solution)/shard_map/ppermute | solution.py:463
  9.2 11.1 %collective-permute-start.2 = (f32[3,4,544]{2,1,0:T(4,128)S(1)}, f32[3,4,544]{2,1,0:T(4,128)S(1)}, u32[]{:S(2)}, u32[]{:S(2)}) collective-permute-start(f32[3,4,544]{2,1,0:T(4,128)S(1)} %collective-permute-done.1.refs_2_), channel_id=1, source_target_pairs={{0,1},{1,0},{2,3},{3,2},{4,5},{5,4},{6,7},{7,6},{8,9},{9,8},{10,11... | collective-permute-start | bytes 78344 | tf_op jit(solution)/shard_map/ppermute | solution.py:463
  9.2 1.3 %copy-start = (f32[544,544]{1,0:T(8,128)S(1)}, f32[544,544]{1,0:T(8,128)}, u32[]{:S(2)}) copy-start(f32[544,544]{1,0:T(8,128)} %refs_0_.2) | copy-start | bytes 3551236
  10.6 1.0 %copy-start.1 = (f32[544,152]{0,1:T(8,128)S(1)}, f32[544,152]{0,1:T(8,128)}, u32[]{:S(2)}) copy-start(f32[544,152]{0,1:T(8,128)} %param.14) | copy-start | bytes 992260
  11.6 0.8 %copy-start.5 = (f32[3,4,544]{2,1,0:T(4,128)S(1)}, f32[3,4,544]{2,1,0:T(4,128)}, u32[]{:S(2)}) copy-start(f32[3,4,544]{2,1,0:T(4,128)} %points_ref.3) | copy-start | bytes 78340
  12.3 0.7 %copy-start.7 = (f32[3,544]{1,0:T(4,128)S(1)}, f32[3,544]{1,0:T(4,128)}, u32[]{:S(2)}) copy-start(f32[3,544]{1,0:T(4,128)} %refs_8_.3) | copy-start | bytes 19588
  13.0 7.3 %copy-start.6 = (f32[3,4,544]{2,1,0:T(4,128)S(1)}, f32[3,4,544]{2,1,0:T(4,128)}, u32[]{:S(2)}) copy-start(f32[3,4,544]{2,1,0:T(4,128)} %points_ref.3) | copy-start | bytes 78340
  13.0 7.3 %copy-start.8 = (f32[3,544]{1,0:T(4,128)S(1)}, f32[3,544]{1,0:T(4,128)}, u32[]{:S(2)}) copy-start(f32[3,544]{1,0:T(4,128)} %refs_8_.3) | copy-start | bytes 19588
  13.0 7.3 %copy-start.10 = (s32[1,2]{1,0:T(1,128)S(1)}, s32[1,2]{1,0:T(1,128)}, u32[]{:S(2)}) copy-start(s32[1,2]{1,0:T(1,128)} %target_ref.3) | copy-start | bytes 28
  13.0 7.3 %copy-start.11 = (s32[1,2]{1,0:T(1,128)S(1)}, s32[1,2]{1,0:T(1,128)}, u32[]{:S(2)}) copy-start(s32[1,2]{1,0:T(1,128)} %owner_ref.3) | copy-start | bytes 28
  13.0 7.3 %copy-start.12 = (s32[1,2]{1,0:T(1,128)S(1)}, s32[1,2]{1,0:T(1,128)}, u32[]{:S(2)}) copy-start(s32[1,2]{1,0:T(1,128)} %cell_ref.3) | copy-start | bytes 28
  14.6 12.4 %all-to-all-start = ((f32[32,4,128]{2,1,0:T(4,128)}), f32[32,4,128]{2,1,0:T(4,128)S(1)}, u32[]{:S(2)}, u32[]{:S(2)}) async-start(f32[32,4,128]{2,1,0:T(4,128)} %get-tuple-element.6), calls=%async_computation | async-start | bytes 131072 | tf_op jit(solution)/shard_map/all_to_all | solution.py:471
  20.3 6.7 %copy-start.3 = (f32[152,544]{1,0:T(8,128)S(1)}, f32[152,544]{1,0:T(8,128)}, u32[]{:S(2)}) copy-start(f32[152,544]{1,0:T(8,128)} %down_ref.3) | copy-start | bytes 992260
  20.4 6.7 %copy-start.4 = (f32[152,152]{1,0:T(8,128)S(1)}, f32[152,152]{1,0:T(8,128)}, u32[]{:S(2)}) copy-start(f32[152,152]{1,0:T(8,128)} %m2m_ref.3) | copy-start | bytes 277252
  20.4 6.7 %copy-start.9 = (f32[3,152]{1,0:T(4,128)S(1)}, f32[3,152]{1,0:T(4,128)}, u32[]{:S(2)}) copy-start(f32[3,152]{1,0:T(4,128)} %template_ref.3) | copy-start | bytes 5476
  23.5 11.8 %copy-start.2 = (f32[544,152]{0,1:T(8,128)S(1)}, f32[544,152]{0,1:T(8,128)}, u32[]{:S(2)}) copy-start(f32[544,152]{0,1:T(8,128)} %param.14) | copy-start | bytes 992260
  29.5 4.9 %collective-permute-start.12 = (f32[3,4,544]{2,1,0:T(4,128)S(1)}, f32[3,4,544]{2,1,0:T(4,128)S(1)}, u32[]{:S(2)}, u32[]{:S(2)}) collective-permute-start(f32[3,4,544]{2,1,0:T(4,128)S(1)} %get-tuple-element.9.points_ref.own_ref.refs_0_), channel_id=1, source_target_pairs={{0,6},{1,7},{2,4},{3,5},{4,2},{5,3},{6,0},{7,1},{8,14},{9,15},{10,... | collective-permute-start | bytes 78344 | tf_op jit(solution)/shard_map/ppermute | solution.py:463
  30.2 4.2 %collective-permute-start.10 = (f32[3,4,544]{2,1,0:T(4,128)S(1)}, f32[3,4,544]{2,1,0:T(4,128)S(1)}, u32[]{:S(2)}, u32[]{:S(2)}) collective-permute-start(f32[3,4,544]{2,1,0:T(4,128)S(1)} %get-tuple-element.9.points_ref.own_ref.refs_0_), channel_id=1, source_target_pairs={{0,4},{1,5},{2,6},{3,7},{4,0},{5,1},{6,2},{7,3},{8,12},{9,13},{10,... | collective-permute-start | bytes 78344 | tf_op jit(solution)/shard_map/ppermute | solution.py:463
  31.4 3.9 %collective-permute-start.8 = (f32[3,4,544]{2,1,0:T(4,128)S(1)}, f32[3,4,544]{2,1,0:T(4,128)S(1)}, u32[]{:S(2)}, u32[]{:S(2)}) collective-permute-start(f32[3,4,544]{2,1,0:T(4,128)S(1)} %get-tuple-element.9.points_ref.own_ref.refs_0_), channel_id=1, source_target_pairs={{0,2},{1,3},{2,0},{3,1},{4,6},{5,7},{6,4},{7,5},{8,10},{9,11},{10,... | collective-permute-start | bytes 78344 | tf_op jit(solution)/shard_map/ppermute | solution.py:463
  33.0 6.2 %collective-permute-start.7 = (f32[3,4,544]{2,1,0:T(4,128)S(1)}, f32[3,4,544]{2,1,0:T(4,128)S(1)}, u32[]{:S(2)}, u32[]{:S(2)}) collective-permute-start(f32[3,4,544]{2,1,0:T(4,128)S(1)} %get-tuple-element.9.points_ref.own_ref.refs_0_), channel_id=1, source_target_pairs={{0,1},{1,0},{2,3},{3,2},{4,5},{5,4},{6,7},{7,6},{8,9},{9,8},{10,11... | collective-permute-start | bytes 78344 | tf_op jit(solution)/shard_map/ppermute | solution.py:463
  34.5 4.8 %collective-permute-start.13 = (f32[3,4,544]{2,1,0:T(4,128)S(1)}, f32[3,4,544]{2,1,0:T(4,128)S(1)}, u32[]{:S(2)}, u32[]{:S(2)}) collective-permute-start(f32[3,4,544]{2,1,0:T(4,128)S(1)} %collective-permute-done.12.refs_6_), channel_id=1, source_target_pairs={{0,1},{1,0},{2,3},{3,2},{4,5},{5,4},{6,7},{7,6},{8,9},{9,8},{10,11... | collective-permute-start | bytes 78344 | tf_op jit(solution)/shard_map/ppermute | solution.py:463
  34.5 4.8 %collective-permute-start.11 = (f32[3,4,544]{2,1,0:T(4,128)S(1)}, f32[3,4,544]{2,1,0:T(4,128)S(1)}, u32[]{:S(2)}, u32[]{:S(2)}) collective-permute-start(f32[3,4,544]{2,1,0:T(4,128)S(1)} %collective-permute-done.10.refs_4_), channel_id=1, source_target_pairs={{0,1},{1,0},{2,3},{3,2},{4,5},{5,4},{6,7},{7,6},{8,9},{9,8},{10,11... | collective-permute-start | bytes 78344 | tf_op jit(solution)/shard_map/ppermute | solution.py:463
  35.3 4.0 %collective-permute-start.9 = (f32[3,4,544]{2,1,0:T(4,128)S(1)}, f32[3,4,544]{2,1,0:T(4,128)S(1)}, u32[]{:S(2)}, u32[]{:S(2)}) collective-permute-start(f32[3,4,544]{2,1,0:T(4,128)S(1)} %collective-permute-done.8.refs_2_), channel_id=1, source_target_pairs={{0,1},{1,0},{2,3},{3,2},{4,5},{5,4},{6,7},{7,6},{8,9},{9,8},{10,11... | collective-permute-start | bytes 78344 | tf_op jit(solution)/shard_map/ppermute | solution.py:463
  36.7 10.0 %all-to-all-start.1 = ((f32[32,4,128]{2,1,0:T(4,128)}), f32[32,4,128]{2,1,0:T(4,128)S(1)}, u32[]{:S(2)}, u32[]{:S(2)}) async-start(f32[32,4,128]{2,1,0:T(4,128)} %membrane.3), calls=%async_computation.1 | async-start | bytes 131072 | tf_op jit(solution)/shard_map/all_to_all | solution.py:471

commit v4 on v3

v4 whole, which is shorter than its diff:
```python
import functools

import jax
import jax.numpy as jnp
from jax import lax
from jax.experimental import pallas as pl
from jax.experimental.pallas import tpu as pltpu
from jax.sharding import PartitionSpec as P


NEAR = 2

EPSILON_SQ = 0.25
VISCOSITY = 0.039788735772973836
TIME_STEP = 0.1
SKALAK_HARDEN = 2.0
CHECK_RADIUS = 1.0
DEVICE_RADIUS = 1.5
GROUP_RADIUS = 6.0

LANES = 128
SUB = 8
BATCH = 3


def up8(n):
    return -(-n // SUB) * SUB


def split(a):
    high = a.astype(jnp.bfloat16)
    low = (a - high.astype(jnp.float32)).astype(jnp.bfloat16)
    return high, low


NN = (((1,), (0,)), ((), ()))
NT = (((1,), (1,)), ((), ()))


def dot3(a, b_parts, dims=NN):
    dot = functools.partial(
        lax.dot_general, dimension_numbers=dims, preferred_element_type=jnp.float32
    )
    rows = a.shape[0]
    first = a.astype(jnp.bfloat16).astype(jnp.float32)
    both = jnp.concatenate([first, a - first], axis=0).astype(jnp.bfloat16)
    high = dot(both, b_parts[0])
    return high[:rows] + (high[rows:] + dot(first.astype(jnp.bfloat16), b_parts[1]))


def harden(linear, stretch):
    return -linear * (1.0 + SKALAK_HARDEN * stretch / (1.0 + stretch))


def parts3(a):
    first = a.astype(jnp.bfloat16).astype(jnp.float32)
    rest = a - first
    second = rest.astype(jnp.bfloat16).astype(jnp.float32)
    return first, second, rest - second


def stack_left(a):
    first, second, third = parts3(a)
    return jnp.concatenate([first, first, first, second, second, third], axis=0)


def stack_right(a):
    first, second, third = parts3(a)
    return jnp.concatenate([first, second, third, first, second, first], axis=0)


def stack_pair(a):
    first, second, _ = parts3(a)
    return jnp.concatenate([first, second], axis=0).astype(jnp.bfloat16)


def rows8(rows):
    size = rows[0].shape[1]
    count = sum(row.shape[0] for row in rows)
    return jnp.concatenate(rows + [jnp.zeros((SUB - count, size), jnp.float32)], axis=0)


def square_of(place):
    return jnp.sum(place * place, axis=0, keepdims=True)


def target_rows(place):
    return rows8([place, square_of(place), jnp.ones_like(place[:1])])


def source_rows(place, force):
    near = rows8(
        [-2.0 * place, jnp.ones_like(place[:1]), square_of(place) + EPSILON_SQ]
    )
    along = rows8(
        [
            force,
            jnp.zeros_like(place[:1]),
            -jnp.sum(place * force, axis=0, keepdims=True),
        ]
    )
    return near, along


def weights(shifted, along):
    root = lax.rsqrt(jnp.maximum(shifted, EPSILON_SQ))
    inverse = root * root * root
    return split(root + EPSILON_SQ * inverse) + split(along * inverse)


def twice(a):
    return jnp.concatenate([a, a], axis=1)


def finish(place, direct, moment):
    direct = direct[:SUB] + direct[SUB:]
    moment = moment[:SUB] + moment[SUB:]
    return VISCOSITY * (direct[0:3] + place * moment[3:4] - moment[0:3])


def membrane_rows(points, rest_ref, rows_ref):
    cells = points[0].shape[0]
    rows_ref[...] = jnp.zeros_like(rows_ref)
    centers = []
    for k in range(3):
        mean = jnp.mean(points[k], axis=1, keepdims=True)
        rows_ref[SUB * k : SUB * k + cells, :] = points[k] - mean - rest_ref[k : k + 1, :]
        centers.append(jnp.mean(mean, axis=0, keepdims=True))
    return centers


def equivalent_rows(linear, up, flat_ref):
    parts = [linear[SUB * k : SUB * (k + 1)] for k in range(3)]
    stretch = parts[0] * parts[0] + parts[1] * parts[1] + parts[2] * parts[2]
    sums = [jnp.sum(harden(part, stretch), axis=0, keepdims=True) for part in parts]
    flat_ref[...] = jnp.zeros_like(flat_ref)
    flat_ref[:, : up.shape[0]] = dot3(rows8(sums), split(up), NT)


def pack(flat_ref, q, centers=()):
    tail = q - LANES
    ends = flat_ref[:, LANES:]
    last = ends[0:1]
    lane = lax.broadcasted_iota(jnp.int32, (1, LANES), 1)
    for k in range(1, 3):
        last = last + pltpu.roll(ends[k : k + 1], tail * k, axis=1)
    for k, center in enumerate(centers):
        last = jnp.where(lane == 3 * tail + k, center, last)
    return jnp.concatenate([flat_ref[0:3, :LANES], last], axis=0)


def ends_of(row, k, tail):
    lane = lax.broadcasted_iota(jnp.int32, (1, LANES), 1)
    moved = pltpu.roll(row, LANES - tail * k, axis=1) if k else row
    return jnp.where(lane < tail, moved, 0.0)


def first_kernel(points_ref, rest_ref, up_ref, stiffness_ref, out_ref, rows_ref, flat_ref):
    centers = membrane_rows([points_ref[k] for k in range(3)], rest_ref, rows_ref)
    linear = dot3(rows_ref[...], split(stiffness_ref[...]))
    equivalent_rows(linear, up_ref[...], flat_ref)
    message = pack(flat_ref, up_ref.shape[0], centers)
    out_ref[...] = jnp.broadcast_to(message[None], out_ref.shape)


def pick(block, row):
    rows = lax.broadcasted_iota(jnp.int32, (block.shape[0], 1), 0)
    return jnp.sum(jnp.where(rows == row, block, 0.0), axis=0, keepdims=True)


def gather(owner_ref, cell_ref, pool_refs, rows_ref, spread):
    me = lax.axis_index("dev")
    rows_ref[...] = jnp.zeros_like(rows_ref)
    for slot in range(NEAR):
        cell = cell_ref[0, slot]
        owner = owner_ref[0, slot]
        if spread:
            for mask, pool_ref in enumerate(pool_refs):

                @pl.when((owner ^ me) == mask)
                def _(pool_ref=pool_ref):
                    for k in range(3):
                        rows_ref[SUB * slot + k : SUB * slot + k + 1, :] = pick(pool_ref[k], cell)
        else:
            for k in range(3):
                rows_ref[SUB * slot + k : SUB * slot + k + 1, :] = pick(
                    pool_refs[0][owner, k], cell
                )


def near_sums(target_ref, count_ref, points_ref, rest_ref, stiffness, rows_ref, move_ref):
    cells, _ = points_ref.shape[1:]
    sources = rows_ref[...]
    move_ref[...] = jnp.zeros_like(move_ref)
    for slot in range(NEAR):
        own = sources[SUB * slot : SUB * slot + 3]
        mean = jnp.mean(own, axis=1, keepdims=True)
        move_ref[SUB * slot : SUB * slot + 3, :] = own - mean - rest_ref[...]
    linear = dot3(move_ref[...], stiffness)
    square = linear * linear
    dot = functools.partial(jnp.dot, preferred_element_type=jnp.float32)
    results = []
    for slot in range(NEAR):
        part = linear[SUB * slot : SUB * slot + 3]
        stretch = jnp.sum(square[SUB * slot : SUB * slot + 3], axis=0, keepdims=True)
        force = harden(part, stretch)
        aim = jnp.concatenate([pick(points_ref[k], target_ref[0, slot]) for k in range(3)], axis=0)
        center = jnp.mean(aim, axis=1, keepdims=True)
        aim = aim - center
        place = sources[SUB * slot : SUB * slot + 3] - center
        near, along = source_rows(place, force)
        near = jnp.transpose(stack_left(near)).astype(jnp.bfloat16)
        along = jnp.transpose(stack_left(along)).astype(jnp.bfloat16)
        right = stack_right(target_rows(aim)).astype(jnp.bfloat16)
        forces = stack_pair(rows8([force]))
        places = stack_pair(rows8([place, jnp.ones_like(place[:1])]))
        both = weights(dot(near, right), dot(along, right))
        direct = dot(twice(forces), jnp.concatenate(both[:2], axis=0))
        moment = dot(twice(places), jnp.concatenate(both[2:], axis=0))
        results.append(jnp.where(slot < count_ref[0], finish(aim, direct, moment), 0.0))
    rows = lax.broadcasted_iota(jnp.int32, (cells, 1), 0)
    return [
        sum(
            jnp.where(rows == target_ref[0, slot], results[slot][k : k + 1], 0.0)
            for slot in range(NEAR)
        )
        for k in range(3)
    ]


def near_kernel(target_ref, owner_ref, cell_ref, count_ref, points_ref, *refs, spread, move):
    pool_refs, (rest_ref, stiffness_ref, out_ref, rows_ref, move_ref) = refs[:-5], refs[-5:]
    gather(owner_ref, cell_ref, pool_refs, rows_ref, spread)
    stiffness = split(stiffness_ref[...])
    near = near_sums(target_ref, count_ref, points_ref, rest_ref, stiffness, rows_ref, move_ref)
    for k in range(3):
        out_ref[k] = points_ref[k] + TIME_STEP * near[k] if move else near[k]


def boxes(main, ends, center, template, radius, per_row):
    count = main[0].shape[0]
    tail_lanes = template[2]
    rows = []
    for k in range(3):
        place_main = center[k] + radius * template[0][k : k + 1]
        place_ends = jnp.where(tail_lanes, center[k] + radius * template[1][k : k + 1], 0.0)
        rows.append((place_main, place_ends))
    for k in range(3):
        rows.append((main[k], ends[k]))
    packed = []
    for whole, part in rows:
        turn = lax.broadcasted_iota(jnp.int32, (count, 1), 0) % per_row[0]
        shifted = jnp.where(turn == 0, part, 0.0)
        for i in range(1, per_row[0]):
            shifted += jnp.where(turn == i, pltpu.roll(part, per_row[1] * i, axis=1), 0.0)
        packed.append(
            [whole]
            + [
                jnp.sum(shifted[a : min(a + per_row[0], count)], axis=0, keepdims=True)
                for a in range(0, count, per_row[0])
            ]
        )
    return packed


def far_checks(
    told_ref, m2m_ref, template_ref, wide_ref, sums_ref, group_ref, source_ref, groups, devs
):
    q = template_ref.shape[1]
    tail = q - LANES
    per_row = (LANES // tail, tail)
    group = lax.axis_index("grp")
    dev = lax.axis_index("dev")
    tail_lanes = lax.broadcasted_iota(jnp.int32, (1, LANES), 1) < tail

    wide_ref[...] = jnp.zeros_like(wide_ref)
    wide_ref[0:3, :q] = template_ref[...]
    template = (wide_ref[:, :LANES], wide_ref[:, LANES:], tail_lanes)

    first = group * devs
    own_rows = [told_ref[pl.ds(first, devs), k, :] for k in range(4)]
    others = lax.broadcasted_iota(jnp.int32, (devs, 1), 0) != dev
    inner = boxes(
        [jnp.where(others, own_rows[k], 0.0) for k in range(3)],
        [jnp.where(others, ends_of(own_rows[3], k, tail), 0.0) for k in range(3)],
        [own_rows[3][:, 3 * tail + k : 3 * tail + k + 1] for k in range(3)],
        template,
        DEVICE_RADIUS,
        per_row,
    )

    span = up8(groups)
    sums_ref[...] = jnp.zeros_like(sums_ref)
    for h in range(groups):
        sums_ref[h] = jnp.sum(told_ref[h * devs : (h + 1) * devs, 0:4, :], axis=0)
    sum_rows = [sums_ref[:, k, :] for k in range(4)]
    for k in range(3):
        group_ref[span * k : span * (k + 1), :LANES] = sum_rows[k]
        group_ref[span * k : span * (k + 1), LANES:] = ends_of(sum_rows[3], k, tail)
    shifted = dot3(group_ref[:, :q], split(m2m_ref[...]))
    group_ref[:, :q] = shifted
    other_groups = lax.broadcasted_iota(jnp.int32, (span, 1), 0) != group
    outer = boxes(
        [
            jnp.where(other_groups, group_ref[span * k : span * (k + 1), :LANES], 0.0)
            for k in range(3)
        ],
        [
            jnp.where(other_groups, group_ref[span * k : span * (k + 1), LANES:], 0.0)
            for k in range(3)
        ],
        [sum_rows[3][:, 3 * tail + k : 3 * tail + k + 1] / devs for k in range(3)],
        template,
        GROUP_RADIUS,
        per_row,
    )
    source_ref[...] = jnp.zeros_like(source_ref)
    rows = 0
    center_row = told_ref[pl.ds(first + dev, 1), 3, :]
    centers = [center_row[:, 3 * tail + k : 3 * tail + k + 1] for k in range(3)]
    for part, count in ((inner, devs), (outer, groups)):
        ends = -(-count // per_row[0])
        for index in range(6):
            shift = centers[index] if index < 3 else 0.0
            source_ref[rows : rows + count, index, :] = part[index][0][:count] - shift
            for j in range(ends):
                at = rows + count + j
                source_ref[at : at + 1, index, :] = part[index][1 + j] - shift
        rows += count + ends
    tall = up8(up8(q) // 2) * 2
    targets = CHECK_RADIUS * wide_ref[0:3, :]
    left = jnp.transpose(stack_left(target_rows(targets)))[:tall].astype(jnp.bfloat16)
    targets = targets[:, :tall]
    contract = functools.partial(
        lax.dot_general,
        dimension_numbers=NT,
        preferred_element_type=jnp.float32,
    )
    dot = functools.partial(jnp.dot, preferred_element_type=jnp.float32)
    direct = jnp.zeros((2 * SUB, tall), jnp.float32)
    moment = jnp.zeros((2 * SUB, tall), jnp.float32)
    for row in range(0, source_ref.shape[0], BATCH):
        block = jnp.concatenate([source_ref[row + i] for i in range(BATCH)], axis=1)
        place = block[0:3]
        force = block[3:6]
        near, along = source_rows(place, force)
        both = weights(
            dot(left, stack_right(near).astype(jnp.bfloat16)),
            dot(left, stack_right(along).astype(jnp.bfloat16)),
        )
        forces = stack_pair(rows8([force]))
        places = stack_pair(rows8([place, jnp.ones_like(place[:1])]))
        direct += contract(twice(forces), jnp.concatenate(both[:2], axis=1))
        moment += contract(twice(places), jnp.concatenate(both[2:], axis=1))
    return finish(targets, direct, moment)[:, :q]


def surface_of(checks, down_ref):
    return dot3(rows8([checks]), split(down_ref[...]))


def turn_kernel(
    told_ref,
    partial_ref,
    m2m_ref,
    template_ref,
    down_ref,
    rest_ref,
    up_ref,
    stiffness_ref,
    points_ref,
    out_ref,
    *refs,
    groups,
    devs,
):
    rows_ref, flat_ref = refs[-2:]
    checks = far_checks(told_ref, m2m_ref, template_ref, *refs[:-2], groups, devs)
    surface = surface_of(checks, down_ref)
    points = [partial_ref[k] + TIME_STEP * surface[k : k + 1] for k in range(3)]
    for k in range(3):
        points_ref[k] = points[k]
    centers = membrane_rows(points, rest_ref, rows_ref)
    linear = dot3(rows_ref[...], split(stiffness_ref[...]))
    equivalent_rows(linear, up_ref[...], flat_ref)
    message = pack(flat_ref, up_ref.shape[0], centers)
    out_ref[...] = jnp.broadcast_to(message[None], out_ref.shape)


def last_kernel(
    told_ref,
    points_ref,
    near_ref,
    m2m_ref,
    template_ref,
    down_ref,
    points_out_ref,
    velocity_ref,
    *refs,
    groups,
    devs,
):
    checks = far_checks(told_ref, m2m_ref, template_ref, *refs, groups, devs)
    surface = surface_of(checks, down_ref)
    for k in range(3):
        velocity = surface[k : k + 1] + near_ref[k]
        velocity_ref[k] = velocity
        points_out_ref[k] = points_ref[k] + TIME_STEP * velocity


VMEM = pl.BlockSpec(memory_space=pltpu.VMEM)
SMEM = pl.BlockSpec(memory_space=pltpu.SMEM)


def float32(*shape):
    return jax.ShapeDtypeStruct(shape, jnp.float32)


def scratch(*shape):
    return pltpu.VMEM(shape, jnp.float32)


def call(kernel, in_specs, outs, scratch_shapes, gflop, mib=24):
    return pl.pallas_call(
        kernel,
        in_specs=in_specs,
        out_shape=tuple(outs),
        out_specs=(VMEM,) * len(outs),
        scratch_shapes=scratch_shapes,
        compiler_params=pltpu.CompilerParams(vmem_limit_bytes=mib * 2**20),
        cost_estimate=pl.CostEstimate(
            flops=gflop * 10**9, bytes_accessed=10**6, transcendentals=0
        ),
    )


def body(
    positions,
    rest_shape,
    stiffness,
    up_map,
    down_map,
    m2m,
    box_template,
    near_target,
    near_owner,
    near_cell,
    near_count,
):
    devs = lax.axis_size("dev")
    groups = lax.axis_size("grp")
    everyone = groups * devs
    cells, size = positions.shape[1:]
    q = up_map.shape[1]
    spread = devs == 8
    pools = 8 if spread else 1
    span = up8(groups)
    tail_boxes = LANES // (q - LANES)
    source_count = devs + groups + -(-devs // tail_boxes) + -(-groups // tail_boxes)
    cell_array = float32(3, cells, size)
    up_rows = up_map.T
    lists = (near_target, near_owner, near_cell, near_count)
    far_scratch = [
        scratch(SUB, 2 * LANES),
        scratch(span, 4, LANES),
        scratch(3 * span, 2 * LANES),
        scratch(-(-source_count // BATCH) * BATCH, SUB, LANES),
    ]
    near_scratch = [scratch(NEAR * SUB, size), scratch(NEAR * SUB, size)]
    membrane_scratch = [scratch(3 * SUB, size), scratch(SUB, 2 * LANES)]

    first = call(
        first_kernel, [VMEM] * 4, [float32(everyone, 4, LANES)], membrane_scratch, 1, mib=62
    )

    def near(points, pool, move):
        kernel = functools.partial(near_kernel, spread=spread, move=move)
        specs = [SMEM] * 4 + [VMEM] * (1 + pools + 2)
        run = call(kernel, specs, [cell_array], near_scratch, 4)
        return run(*lists, points, *pool, rest_shape, stiffness)[0]

    turn = call(
        functools.partial(turn_kernel, groups=groups, devs=devs),
        [VMEM] * 8,
        [cell_array, float32(everyone, 4, LANES)],
        far_scratch + membrane_scratch,
        3,
    )
    last = call(
        functools.partial(last_kernel, groups=groups, devs=devs),
        [VMEM] * 6,
        [cell_array, cell_array],
        far_scratch,
        3,
    )

    def to(array, mask):
        return lax.ppermute(array, "dev", [(j, j ^ mask) for j in range(devs)])

    def pool_of(array):
        if not spread:
            copies = jnp.broadcast_to(array[None], (devs,) + array.shape)
            return [lax.all_to_all(copies, "dev", 0, 0)]
        reached = {0: array}
        for mask in (6, 4, 2):
            reached[mask] = to(array, mask)
        reached[1] = to(array, 1)
        for mask in (2, 4, 6):
            reached[mask + 1] = to(reached[mask], 1)
        return [reached[mask] for mask in range(8)]

    def tell(message):
        return lax.all_to_all(message, ("grp", "dev"), 0, 0)

    pool = pool_of(positions)
    (message,) = first(positions, rest_shape, up_rows, stiffness)
    told = tell(message)
    partial = near(positions, pool, True)
    points, message = turn(
        told, partial, m2m, box_template, down_map, rest_shape, up_rows, stiffness
    )
    pool = pool_of(points)
    told = tell(message)
    close = near(points, pool, False)
    return last(told, points, close, m2m, box_template, down_map)


def solution(mesh):
    both = ("grp", "dev")
    return jax.shard_map(
        body,
        mesh=mesh,
        in_specs=(P(None, both, None),) + (P(),) * 6 + (P(both, None),) * 3 + (P(both),),
        out_specs=(P(None, both, None), P(None, both, None)),
        check_vma=False,
    )
```

time: 49.6 us -> 46.5 us (0.938)
  local copies, waits for them, and re-layouts: 3.84 us -> 0.05 us
  starting transfers between devices: 16.3 us -> 15.3 us
  Pallas kernels: 14 us -> 14.9 us
  waiting for transfers between devices: 13.6 us -> 14.5 us
    unnamed x26 -> x20, local copies, waits for them, and re-layouts: 3.84 us -> 0.05 us
    ppermute x14, waiting for transfers between devices: 5.76 us -> 6.75 us  [to(): return lax.ppermute(array, 'dev', [(j, j ^ mask) for j in range(devs)])]
    all_to_all x2, starting transfers between devices: 7.61 us -> 6.67 us  [tell(): return lax.all_to_all(message, ('grp', 'dev'), 0, 0)]
    pallas_call x6 -> x5, Pallas kernels: 14 us -> 14.9 us  [the longest x2 6.21 us: near(): return run(*lists, points, *pool, rest_shape, stiffness)[0]]
  transfers between devices with their start and end apart: 16 -> 16, of which waited for: 7 -> 7; matrix products, arithmetic and copies ran while one was open for 0% -> 0% of each run, Pallas kernels for 18% -> 20%
where the time goes in v4:
time: 46.5 us; the launch traced here: 46.2 us
  starting transfers between devices  15.3 us (33%)
  Pallas kernels  14.9 us (32%)
  waiting for transfers between devices  14.5 us (31%)
  between operations  1.5 us (3%)
    ppermute x14, starting transfers between devices, to(): return lax.ppermute(array, 'dev', [(j, j ^ mask) for j in range(devs)])  8.62 us
    all_to_all x2, waiting for transfers between devices, tell(): return lax.all_to_all(message, ('grp', 'dev'), 0, 0)  7.76 us
    ppermute x14, waiting for transfers between devices, to(): return lax.ppermute(array, 'dev', [(j, j ^ mask) for j in range(devs)])  6.75 us
    all_to_all x2, starting transfers between devices, tell(): return lax.all_to_all(message, ('grp', 'dev'), 0, 0)  6.67 us
    pallas_call x2, Pallas kernels, near(): return run(*lists, points, *pool, rest_shape, stiffness)[0]  6.21 us
    pallas_call x1, Pallas kernels, body(): turn(told, partial, m2m, box_template, down_map, rest_shape, up_rows, sti...  3.22 us
    pallas_call x1, Pallas kernels, body(): message, = first(positions, rest_shape, up_rows, stiffness)  2.95 us
    pallas_call x1, Pallas kernels, body(): return last(told, points, close, m2m, box_template, down_map)  2.5 us
  transfers between devices with their start and end apart: 16, of which 7 were waited for; matrix products, arithmetic and copies ran while one was open for 0% of the time, Pallas kernels for 20%

profile of v4, /device:TPU:0, one launch (start us, length us, event | category | flops | bytes accessed | tf_op | source)
XLA Modules:
  0.0 46.2 jit_solution(15782455434687169363)
XLA Ops:
  0.6 3.1 %collective-permute-start.3 = (f32[3,4,544]{2,1,0:T(4,128)}, f32[3,4,544]{2,1,0:T(4,128)S(1)}, u32[]{:S(2)}, u32[]{:S(2)}) collective-permute-start(f32[3,4,544]{2,1,0:T(4,128)} %refs_0_.1), channel_id=1, source_target_pairs={{0,4},{1,5},{2,6},{3,7},{4,0},{5,1},{6,2},{7,3},{8,12},{9,13},{10,... | collective-permute-start | bytes 78344 | tf_op jit(solution)/shard_map/ppermute | solution.py:498
  3.7 1.5 %collective-permute-start.1 = (f32[3,4,544]{2,1,0:T(4,128)}, f32[3,4,544]{2,1,0:T(4,128)S(1)}, u32[]{:S(2)}, u32[]{:S(2)}) collective-permute-start(f32[3,4,544]{2,1,0:T(4,128)} %refs_0_.1), channel_id=1, source_target_pairs={{0,2},{1,3},{2,0},{3,1},{4,6},{5,7},{6,4},{7,5},{8,10},{9,11},{10,... | collective-permute-start | bytes 78344 | tf_op jit(solution)/shard_map/ppermute | solution.py:498
  5.2 0.0 collective-permute-start.5
  5.2 0.0 collective-permute-start
  5.2 0.5 %collective-permute-done.3.refs_4_ = f32[3,4,544]{2,1,0:T(4,128)S(1)} collective-permute-done((f32[3,4,544]{2,1,0:T(4,128)}, f32[3,4,544]{2,1,0:T(4,128)S(1)}, u32[]{:S(2)}, u32[]{:S(2)}) %collective-permute-start.3) | collective-permute-done | bytes 26144 | tf_op jit(solution)/shard_map/ppermute | solution.py:498
  5.8 0.0 collective-permute-start.4
  5.8 2.1 %collective-permute-done.1.refs_2_ = f32[3,4,544]{2,1,0:T(4,128)S(1)} collective-permute-done((f32[3,4,544]{2,1,0:T(4,128)}, f32[3,4,544]{2,1,0:T(4,128)S(1)}, u32[]{:S(2)}, u32[]{:S(2)}) %collective-permute-start.1) | collective-permute-done | bytes 26144 | tf_op jit(solution)/shard_map/ppermute | solution.py:498
  7.9 0.0 collective-permute-start.2
  7.9 2.3 %collective-permute-done.5.refs_6_ = f32[3,4,544]{2,1,0:T(4,128)S(1)} collective-permute-done((f32[3,4,544]{2,1,0:T(4,128)}, f32[3,4,544]{2,1,0:T(4,128)S(1)}, u32[]{:S(2)}, u32[]{:S(2)}) %collective-permute-start.5) | collective-permute-done | bytes 26144 | tf_op jit(solution)/shard_map/ppermute | solution.py:498
  10.2 0.0 collective-permute-start.6
  10.2 0.0 copy-start
  10.2 0.0 copy-start.4
  10.2 0.0 copy-start.5
  10.2 0.0 copy-start.7
  10.2 0.0 copy-start.8
  10.2 0.0 copy-start.9
  10.2 2.9 %shard_map.122 = f32[32,4,128]{2,1,0:T(4,128)} custom-call(f32[3,4,544]{2,1,0:T(4,128)} %refs_0_.1, f32[3,544]{1,0:T(4,128)} %refs_8_.3, f32[152,544]{1,0:T(8,128)} %bitcast.1, f32[544,544]{1,0:T(8,128)} %refs_9_.3), custom_call_target="tpu_custom_call" | custom-call | flops 1000000000 | bytes 1000000 | tf_op jit(solution)/shard_map/pallas_call | solution.py:516
  13.2 4.1 %all-to-all-start = ((f32[32,4,128]{2,1,0:T(4,128)}), f32[32,4,128]{2,1,0:T(4,128)S(1)}, u32[]{:S(2)}, u32[]{:S(2)}) async-start(f32[32,4,128]{2,1,0:T(4,128)} %shard_map.122), calls=%async_computation | async-start | bytes 131072 | tf_op jit(solution)/shard_map/all_to_all | solution.py:513
  17.9 0.0 copy-start.1
  17.9 0.0 copy-start.2
  17.9 0.0 copy-start.3
  17.9 0.0 copy-start.6
  17.9 0.0 collective-permute-done.refs_1_
  18.0 0.0 collective-permute-done.4.refs_5_
  18.0 0.0 collective-permute-done.2.refs_3_
  18.0 0.0 collective-permute-done.6.refs_7_
  18.0 0.0 copy-done
  18.0 0.0 copy-done.4
  18.0 0.0 copy-done.5
  18.0 0.0 copy-done.7
  18.0 0.0 copy-done.8
  18.0 0.0 copy-done.9
  18.0 3.1 %shard_map.123.partial_ref = f32[3,4,544]{2,1,0:T(4,128)S(1)} custom-call(s32[1,2]{1,0:T(1,128)S(1)} %copy-done.7, s32[1,2]{1,0:T(1,128)S(1)} %copy-done.8, s32[1,2]{1,0:T(1,128)S(1)} %copy-done.9, s32[1]{0:T(128)S(6)} %copy.13.count_ref, f32[3,4,544]{2,1,0:T(4,128)S(1)} %copy-done.4, f32[3,4,544]{2,1,0:T(4,128)S(1)} %copy-done.4, ...), custom_call_target="tpu_custom_call" | custom-call | flops 4000000000 | bytes 1000000 | tf_op jit(solution)/shard_map/pallas_call | solution.py:480
  21.2 3.5 %all-to-all-done.told_ref = f32[32,4,128]{2,1,0:T(4,128)S(1)} async-done(((f32[32,4,128]{2,1,0:T(4,128)}), f32[32,4,128]{2,1,0:T(4,128)S(1)}, u32[]{:S(2)}, u32[]{:S(2)}) %all-to-all-start) | async-done | bytes 65568 | tf_op jit(solution)/shard_map/all_to_all | solution.py:513
  24.7 0.0 copy-done.1
  24.7 0.0 copy-done.2
  24.7 0.0 copy-done.3
  24.7 0.0 copy-done.6
  24.7 3.2 %shard_map.124 = (f32[3,4,544]{2,1,0:T(4,128)S(1)}, f32[32,4,128]{2,1,0:T(4,128)}) custom-call(f32[32,4,128]{2,1,0:T(4,128)S(1)} %all-to-all-done.told_ref, f32[3,4,544]{2,1,0:T(4,128)S(1)} %shard_map.123.partial_ref, f32[152,152]{1,0:T(8,128)S(1)} %copy-done.3, f32[3,152]{1,0:T(4,128)S(1)} %copy-done.6, f32[152,544]{1,0:T(8,128)S(1)} %copy-done.2, ...), custom_call_target="tpu_custom_call" | custom-call | flops 3000000000 | bytes 1000000 | tf_op jit(solution)/shard_map/pallas_call | solution.py:519
  27.9 0.7 %collective-permute-start.12 = (f32[3,4,544]{2,1,0:T(4,128)S(1)}, f32[3,4,544]{2,1,0:T(4,128)S(1)}, u32[]{:S(2)}, u32[]{:S(2)}) collective-permute-start(f32[3,4,544]{2,1,0:T(4,128)S(1)} %get-tuple-element.5.points_ref.refs_0_), channel_id=1, source_target_pairs={{0,6},{1,7},{2,4},{3,5},{4,2},{5,3},{6,0},{7,1},{8,14},{9,15},{10,... | collective-permute-start | bytes 78344 | tf_op jit(solution)/shard_map/ppermute | solution.py:498
  28.6 1.2 %collective-permute-start.10 = (f32[3,4,544]{2,1,0:T(4,128)S(1)}, f32[3,4,544]{2,1,0:T(4,128)S(1)}, u32[]{:S(2)}, u32[]{:S(2)}) collective-permute-start(f32[3,4,544]{2,1,0:T(4,128)S(1)} %get-tuple-element.5.points_ref.refs_0_), channel_id=1, source_target_pairs={{0,4},{1,5},{2,6},{3,7},{4,0},{5,1},{6,2},{7,3},{8,12},{9,13},{10,... | collective-permute-start | bytes 78344 | tf_op jit(solution)/shard_map/ppermute | solution.py:498
  29.8 1.6 %collective-permute-start.8 = (f32[3,4,544]{2,1,0:T(4,128)S(1)}, f32[3,4,544]{2,1,0:T(4,128)S(1)}, u32[]{:S(2)}, u32[]{:S(2)}) collective-permute-start(f32[3,4,544]{2,1,0:T(4,128)S(1)} %get-tuple-element.5.points_ref.refs_0_), channel_id=1, source_target_pairs={{0,2},{1,3},{2,0},{3,1},{4,6},{5,7},{6,4},{7,5},{8,10},{9,11},{10,... | collective-permute-start | bytes 78344 | tf_op jit(solution)/shard_map/ppermute | solution.py:498
  31.4 0.0 collective-permute-start.7
  31.4 1.4 %collective-permute-done.12.refs_6_ = f32[3,4,544]{2,1,0:T(4,128)S(1)} collective-permute-done((f32[3,4,544]{2,1,0:T(4,128)S(1)}, f32[3,4,544]{2,1,0:T(4,128)S(1)}, u32[]{:S(2)}, u32[]{:S(2)}) %collective-permute-start.12) | collective-permute-done | bytes 26144 | tf_op jit(solution)/shard_map/ppermute | solution.py:498
  32.8 0.0 collective-permute-start.13
  32.8 0.0 collective-permute-done.10.refs_4_
  32.8 0.5 %collective-permute-start.11 = (f32[3,4,544]{2,1,0:T(4,128)S(1)}, f32[3,4,544]{2,1,0:T(4,128)S(1)}, u32[]{:S(2)}, u32[]{:S(2)}) collective-permute-start(f32[3,4,544]{2,1,0:T(4,128)S(1)} %collective-permute-done.10.refs_4_), channel_id=1, source_target_pairs={{0,1},{1,0},{2,3},{3,2},{4,5},{5,4},{6,7},{7,6},{8,9},{9,8},{10,11... | collective-permute-start | bytes 78344 | tf_op jit(solution)/shard_map/ppermute | solution.py:498
  33.4 0.3 collective-permute-done.8.refs_2_
  33.7 0.0 collective-permute-start.9
  33.7 2.6 %all-to-all-start.1 = ((f32[32,4,128]{2,1,0:T(4,128)}), f32[32,4,128]{2,1,0:T(4,128)S(1)}, u32[]{:S(2)}, u32[]{:S(2)}) async-start(f32[32,4,128]{2,1,0:T(4,128)} %get-tuple-element.4), calls=%async_computation.1 | async-start | bytes 131072 | tf_op jit(solution)/shard_map/all_to_all | solution.py:513
  36.3 0.0 collective-permute-done.7.refs_1_
  36.3 0.0 collective-permute-done.13.refs_7_
  36.3 0.0 collective-permute-done.11.refs_5_
  36.3 0.0 collective-permute-done.9.refs_3_
  36.3 3.1 %shard_map.125.near_ref = f32[3,4,544]{2,1,0:T(4,128)S(1)} custom-call(s32[1,2]{1,0:T(1,128)S(1)} %copy-done.7, s32[1,2]{1,0:T(1,128)S(1)} %copy-done.8, s32[1,2]{1,0:T(1,128)S(1)} %copy-done.9, s32[1]{0:T(128)S(6)} %copy.13.count_ref, f32[3,4,544]{2,1,0:T(4,128)S(1)} %get-tuple-element.5.points_ref.refs_0_, ...), custom_call_target="tpu_custom_call" | custom-call | flops 4000000000 | bytes 1000000 | tf_op jit(solution)/shard_map/pallas_call | solution.py:480
  39.5 4.3 %all-to-all-done.1.told_ref = f32[32,4,128]{2,1,0:T(4,128)S(1)} async-done(((f32[32,4,128]{2,1,0:T(4,128)}), f32[32,4,128]{2,1,0:T(4,128)S(1)}, u32[]{:S(2)}, u32[]{:S(2)}) %all-to-all-start.1) | async-done | bytes 65568 | tf_op jit(solution)/shard_map/all_to_all | solution.py:513
  43.7 2.5 %shard_map.126 = (f32[3,4,544]{2,1,0:T(4,128)}, f32[3,4,544]{2,1,0:T(4,128)}) custom-call(f32[32,4,128]{2,1,0:T(4,128)S(1)} %all-to-all-done.1.told_ref, f32[3,4,544]{2,1,0:T(4,128)S(1)} %get-tuple-element.5.points_ref.refs_0_, f32[3,4,544]{2,1,0:T(4,128)S(1)} %shard_map.125.near_ref, f32[152,152]{1,0:T(8,128)S(1)} %copy-done.3, f32[3,152]{1,0:T(4,128)S(1)} %copy-done.6, ...), custom_call_target="tpu_custom_call" | custom-call | flops 3000000000 | bytes 1000000 | tf_op jit(solution)/shard_map/pallas_call | solution.py:525
Async XLA Ops:
  0.6 5.1 %collective-permute-start.3 = (f32[3,4,544]{2,1,0:T(4,128)}, f32[3,4,544]{2,1,0:T(4,128)S(1)}, u32[]{:S(2)}, u32[]{:S(2)}) collective-permute-start(f32[3,4,544]{2,1,0:T(4,128)} %refs_0_.1), channel_id=1, source_target_pairs={{0,4},{1,5},{2,6},{3,7},{4,0},{5,1},{6,2},{7,3},{8,12},{9,13},{10,... | collective-permute-start | bytes 78344 | tf_op jit(solution)/shard_map/ppermute | solution.py:498
  3.7 4.2 %collective-permute-start.1 = (f32[3,4,544]{2,1,0:T(4,128)}, f32[3,4,544]{2,1,0:T(4,128)S(1)}, u32[]{:S(2)}, u32[]{:S(2)}) collective-permute-start(f32[3,4,544]{2,1,0:T(4,128)} %refs_0_.1), channel_id=1, source_target_pairs={{0,2},{1,3},{2,0},{3,1},{4,6},{5,7},{6,4},{7,5},{8,10},{9,11},{10,... | collective-permute-start | bytes 78344 | tf_op jit(solution)/shard_map/ppermute | solution.py:498
  5.2 5.0 %collective-permute-start.5 = (f32[3,4,544]{2,1,0:T(4,128)}, f32[3,4,544]{2,1,0:T(4,128)S(1)}, u32[]{:S(2)}, u32[]{:S(2)}) collective-permute-start(f32[3,4,544]{2,1,0:T(4,128)} %refs_0_.1), channel_id=1, source_target_pairs={{0,6},{1,7},{2,4},{3,5},{4,2},{5,3},{6,0},{7,1},{8,14},{9,15},{10,... | collective-permute-start | bytes 78344 | tf_op jit(solution)/shard_map/ppermute | solution.py:498
  5.2 12.7 %collective-permute-start = (f32[3,4,544]{2,1,0:T(4,128)}, f32[3,4,544]{2,1,0:T(4,128)S(1)}, u32[]{:S(2)}, u32[]{:S(2)}) collective-permute-start(f32[3,4,544]{2,1,0:T(4,128)} %refs_0_.1), channel_id=1, source_target_pairs={{0,1},{1,0},{2,3},{3,2},{4,5},{5,4},{6,7},{7,6},{8,9},{9,8},{10,11... | collective-permute-start | bytes 78344 | tf_op jit(solution)/shard_map/ppermute | solution.py:498
  5.8 12.2 %collective-permute-start.4 = (f32[3,4,544]{2,1,0:T(4,128)S(1)}, f32[3,4,544]{2,1,0:T(4,128)S(1)}, u32[]{:S(2)}, u32[]{:S(2)}) collective-permute-start(f32[3,4,544]{2,1,0:T(4,128)S(1)} %collective-permute-done.3.refs_4_), channel_id=1, source_target_pairs={{0,1},{1,0},{2,3},{3,2},{4,5},{5,4},{6,7},{7,6},{8,9},{9,8},{10,11... | collective-permute-start | bytes 78344 | tf_op jit(solution)/shard_map/ppermute | solution.py:498
  7.9 10.1 %collective-permute-start.2 = (f32[3,4,544]{2,1,0:T(4,128)S(1)}, f32[3,4,544]{2,1,0:T(4,128)S(1)}, u32[]{:S(2)}, u32[]{:S(2)}) collective-permute-start(f32[3,4,544]{2,1,0:T(4,128)S(1)} %collective-permute-done.1.refs_2_), channel_id=1, source_target_pairs={{0,1},{1,0},{2,3},{3,2},{4,5},{5,4},{6,7},{7,6},{8,9},{9,8},{10,11... | collective-permute-start | bytes 78344 | tf_op jit(solution)/shard_map/ppermute | solution.py:498
  10.2 7.8 %collective-permute-start.6 = (f32[3,4,544]{2,1,0:T(4,128)S(1)}, f32[3,4,544]{2,1,0:T(4,128)S(1)}, u32[]{:S(2)}, u32[]{:S(2)}) collective-permute-start(f32[3,4,544]{2,1,0:T(4,128)S(1)} %collective-permute-done.5.refs_6_), channel_id=1, source_target_pairs={{0,1},{1,0},{2,3},{3,2},{4,5},{5,4},{6,7},{7,6},{8,9},{9,8},{10,11... | collective-permute-start | bytes 78344 | tf_op jit(solution)/shard_map/ppermute | solution.py:498
  10.2 7.8 %copy-start = (f32[544,544]{1,0:T(8,128)S(1)}, f32[544,544]{1,0:T(8,128)}, u32[]{:S(2)}) copy-start(f32[544,544]{1,0:T(8,128)} %refs_9_.3) | copy-start | bytes 3551236
  10.2 7.8 %copy-start.4 = (f32[3,4,544]{2,1,0:T(4,128)S(1)}, f32[3,4,544]{2,1,0:T(4,128)}, u32[]{:S(2)}) copy-start(f32[3,4,544]{2,1,0:T(4,128)} %refs_0_.1) | copy-start | bytes 78340
  10.2 7.8 %copy-start.5 = (f32[3,544]{1,0:T(4,128)S(1)}, f32[3,544]{1,0:T(4,128)}, u32[]{:S(2)}) copy-start(f32[3,544]{1,0:T(4,128)} %refs_8_.3) | copy-start | bytes 19588
  10.2 7.8 %copy-start.7 = (s32[1,2]{1,0:T(1,128)S(1)}, s32[1,2]{1,0:T(1,128)}, u32[]{:S(2)}) copy-start(s32[1,2]{1,0:T(1,128)} %target_ref.3) | copy-start | bytes 28
  10.2 7.8 %copy-start.8 = (s32[1,2]{1,0:T(1,128)S(1)}, s32[1,2]{1,0:T(1,128)}, u32[]{:S(2)}) copy-start(s32[1,2]{1,0:T(1,128)} %owner_ref.3) | copy-start | bytes 28
  10.2 7.8 %copy-start.9 = (s32[1,2]{1,0:T(1,128)S(1)}, s32[1,2]{1,0:T(1,128)}, u32[]{:S(2)}) copy-start(s32[1,2]{1,0:T(1,128)} %cell_ref.3) | copy-start | bytes 28
  13.2 11.5 %all-to-all-start = ((f32[32,4,128]{2,1,0:T(4,128)}), f32[32,4,128]{2,1,0:T(4,128)S(1)}, u32[]{:S(2)}, u32[]{:S(2)}) async-start(f32[32,4,128]{2,1,0:T(4,128)} %shard_map.122), calls=%async_computation | async-start | bytes 131072 | tf_op jit(solution)/shard_map/all_to_all | solution.py:513
  17.9 6.8 %copy-start.1 = (f32[544,152]{0,1:T(8,128)S(1)}, f32[544,152]{0,1:T(8,128)}, u32[]{:S(2)}) copy-start(f32[544,152]{0,1:T(8,128)} %param.14) | copy-start | bytes 992260
  17.9 6.8 %copy-start.2 = (f32[152,544]{1,0:T(8,128)S(1)}, f32[152,544]{1,0:T(8,128)}, u32[]{:S(2)}) copy-start(f32[152,544]{1,0:T(8,128)} %down_ref.3) | copy-start | bytes 992260
  17.9 6.7 %copy-start.3 = (f32[152,152]{1,0:T(8,128)S(1)}, f32[152,152]{1,0:T(8,128)}, u32[]{:S(2)}) copy-start(f32[152,152]{1,0:T(8,128)} %m2m_ref.3) | copy-start | bytes 277252
  17.9 6.7 %copy-start.6 = (f32[3,152]{1,0:T(4,128)S(1)}, f32[3,152]{1,0:T(4,128)}, u32[]{:S(2)}) copy-start(f32[3,152]{1,0:T(4,128)} %template_ref.3) | copy-start | bytes 5476
  27.9 4.9 %collective-permute-start.12 = (f32[3,4,544]{2,1,0:T(4,128)S(1)}, f32[3,4,544]{2,1,0:T(4,128)S(1)}, u32[]{:S(2)}, u32[]{:S(2)}) collective-permute-start(f32[3,4,544]{2,1,0:T(4,128)S(1)} %get-tuple-element.5.points_ref.refs_0_), channel_id=1, source_target_pairs={{0,6},{1,7},{2,4},{3,5},{4,2},{5,3},{6,0},{7,1},{8,14},{9,15},{10,... | collective-permute-start | bytes 78344 | tf_op jit(solution)/shard_map/ppermute | solution.py:498
  28.6 4.2 %collective-permute-start.10 = (f32[3,4,544]{2,1,0:T(4,128)S(1)}, f32[3,4,544]{2,1,0:T(4,128)S(1)}, u32[]{:S(2)}, u32[]{:S(2)}) collective-permute-start(f32[3,4,544]{2,1,0:T(4,128)S(1)} %get-tuple-element.5.points_ref.refs_0_), channel_id=1, source_target_pairs={{0,4},{1,5},{2,6},{3,7},{4,0},{5,1},{6,2},{7,3},{8,12},{9,13},{10,... | collective-permute-start | bytes 78344 | tf_op jit(solution)/shard_map/ppermute | solution.py:498
  29.8 3.9 %collective-permute-start.8 = (f32[3,4,544]{2,1,0:T(4,128)S(1)}, f32[3,4,544]{2,1,0:T(4,128)S(1)}, u32[]{:S(2)}, u32[]{:S(2)}) collective-permute-start(f32[3,4,544]{2,1,0:T(4,128)S(1)} %get-tuple-element.5.points_ref.refs_0_), channel_id=1, source_target_pairs={{0,2},{1,3},{2,0},{3,1},{4,6},{5,7},{6,4},{7,5},{8,10},{9,11},{10,... | collective-permute-start | bytes 78344 | tf_op jit(solution)/shard_map/ppermute | solution.py:498
  31.4 4.9 %collective-permute-start.7 = (f32[3,4,544]{2,1,0:T(4,128)S(1)}, f32[3,4,544]{2,1,0:T(4,128)S(1)}, u32[]{:S(2)}, u32[]{:S(2)}) collective-permute-start(f32[3,4,544]{2,1,0:T(4,128)S(1)} %get-tuple-element.5.points_ref.refs_0_), channel_id=1, source_target_pairs={{0,1},{1,0},{2,3},{3,2},{4,5},{5,4},{6,7},{7,6},{8,9},{9,8},{10,11... | collective-permute-start | bytes 78344 | tf_op jit(solution)/shard_map/ppermute | solution.py:498
  32.8 3.5 %collective-permute-start.13 = (f32[3,4,544]{2,1,0:T(4,128)S(1)}, f32[3,4,544]{2,1,0:T(4,128)S(1)}, u32[]{:S(2)}, u32[]{:S(2)}) collective-permute-start(f32[3,4,544]{2,1,0:T(4,128)S(1)} %collective-permute-done.12.refs_6_), channel_id=1, source_target_pairs={{0,1},{1,0},{2,3},{3,2},{4,5},{5,4},{6,7},{7,6},{8,9},{9,8},{10,11... | collective-permute-start | bytes 78344 | tf_op jit(solution)/shard_map/ppermute | solution.py:498
  32.8 3.5 %collective-permute-start.11 = (f32[3,4,544]{2,1,0:T(4,128)S(1)}, f32[3,4,544]{2,1,0:T(4,128)S(1)}, u32[]{:S(2)}, u32[]{:S(2)}) collective-permute-start(f32[3,4,544]{2,1,0:T(4,128)S(1)} %collective-permute-done.10.refs_4_), channel_id=1, source_target_pairs={{0,1},{1,0},{2,3},{3,2},{4,5},{5,4},{6,7},{7,6},{8,9},{9,8},{10,11... | collective-permute-start | bytes 78344 | tf_op jit(solution)/shard_map/ppermute | solution.py:498
  33.7 2.6 %collective-permute-start.9 = (f32[3,4,544]{2,1,0:T(4,128)S(1)}, f32[3,4,544]{2,1,0:T(4,128)S(1)}, u32[]{:S(2)}, u32[]{:S(2)}) collective-permute-start(f32[3,4,544]{2,1,0:T(4,128)S(1)} %collective-permute-done.8.refs_2_), channel_id=1, source_target_pairs={{0,1},{1,0},{2,3},{3,2},{4,5},{5,4},{6,7},{7,6},{8,9},{9,8},{10,11... | collective-permute-start | bytes 78344 | tf_op jit(solution)/shard_map/ppermute | solution.py:498
  33.7 10.0 %all-to-all-start.1 = ((f32[32,4,128]{2,1,0:T(4,128)}), f32[32,4,128]{2,1,0:T(4,128)S(1)}, u32[]{:S(2)}, u32[]{:S(2)}) async-start(f32[32,4,128]{2,1,0:T(4,128)} %get-tuple-element.4), calls=%async_computation.1 | async-start | bytes 131072 | tf_op jit(solution)/shard_map/all_to_all | solution.py:513

commit v5 on v4

--- a/solution.py
+++ b/solution.py
@@ -155,11 +155,17 @@
     return jnp.where(lane < tail, moved, 0.0)
 
 
-def first_kernel(points_ref, rest_ref, up_ref, stiffness_ref, out_ref, rows_ref, flat_ref):
+def blank_kernel(out_ref):
+    out_ref[...] = jnp.zeros_like(out_ref)
+
+
+def first_kernel(
+    blank_ref, points_ref, rest_ref, up_ref, stiffness_ref, out_ref, rows_ref, flat_ref
+):
     centers = membrane_rows([points_ref[k] for k in range(3)], rest_ref, rows_ref)
     linear = dot3(rows_ref[...], split(stiffness_ref[...]))
     equivalent_rows(linear, up_ref[...], flat_ref)
-    message = pack(flat_ref, up_ref.shape[0], centers)
+    message = pack(flat_ref, up_ref.shape[0], centers) + blank_ref[0:4, :]
     out_ref[...] = jnp.broadcast_to(message[None], out_ref.shape)
 
 
@@ -469,9 +475,8 @@
     near_scratch = [scratch(NEAR * SUB, size), scratch(NEAR * SUB, size)]
     membrane_scratch = [scratch(3 * SUB, size), scratch(SUB, 2 * LANES)]
 
-    first = call(
-        first_kernel, [VMEM] * 4, [float32(everyone, 4, LANES)], membrane_scratch, 1, mib=62
-    )
+    first = call(first_kernel, [VMEM] * 5, [float32(everyone, 4, LANES)], membrane_scratch, 1)
+    blank = call(blank_kernel, [], [float32(SUB, LANES)], [], 40)
 
     def near(points, pool, move):
         kernel = functools.partial(near_kernel, spread=spread, move=move)
@@ -512,8 +517,9 @@
     def tell(message):
         return lax.all_to_all(message, ("grp", "dev"), 0, 0)
 
+    (empty,) = blank()
     pool = pool_of(positions)
-    (message,) = first(positions, rest_shape, up_rows, stiffness)
+    (message,) = first(empty, positions, rest_shape, up_rows, stiffness)
     told = tell(message)
     partial = near(positions, pool, True)
     points, message = turn(

time: 46.5 us -> 45 us (0.968)
  Pallas kernels: 14.9 us -> 13.3 us
    pallas_call x1 -> x2, Pallas kernels: 2.95 us -> 1.35 us  [the longest x1 1.35 us: body(): message, = first(empty, positions, rest_shape, up_rows, stiffness)]
  transfers between devices with their start and end apart: 16 -> 16, of which waited for: 7 -> 7; matrix products, arithmetic and copies ran while one was open for 0% -> 0% of each run, Pallas kernels for 20% -> 17%
where the time goes in v5:
time: 45 us; the launch traced here: 44.7 us
  starting transfers between devices  15.3 us (34%)
  waiting for transfers between devices  14.6 us (32%)
  Pallas kernels  13.3 us (30%)
  between operations  1.5 us (3%)
    ppermute x14, starting transfers between devices, to(): return lax.ppermute(array, 'dev', [(j, j ^ mask) for j in range(devs)])  8.62 us
    all_to_all x2, waiting for transfers between devices, tell(): return lax.all_to_all(message, ('grp', 'dev'), 0, 0)  7.81 us
    ppermute x14, waiting for transfers between devices, to(): return lax.ppermute(array, 'dev', [(j, j ^ mask) for j in range(devs)])  6.75 us
    all_to_all x2, starting transfers between devices, tell(): return lax.all_to_all(message, ('grp', 'dev'), 0, 0)  6.72 us
    pallas_call x2, Pallas kernels, near(): return run(*lists, points, *pool, rest_shape, stiffness)[0]  6.21 us
    pallas_call x1, Pallas kernels, body(): turn(told, partial, m2m, box_template, down_map, rest_shape, up_rows, sti...  3.22 us
    pallas_call x1, Pallas kernels, body(): return last(told, points, close, m2m, box_template, down_map)  2.5 us
    pallas_call x1, Pallas kernels, body(): message, = first(empty, positions, rest_shape, up_rows, stiffness)  1.35 us
  transfers between devices with their start and end apart: 16, of which 7 were waited for; matrix products, arithmetic and copies ran while one was open for 0% of the time, Pallas kernels for 17%

profile of v5, /device:TPU:0, one launch (start us, length us, event | category | flops | bytes accessed | tf_op | source)
XLA Modules:
  0.0 44.7 jit_solution(9634147670474578082)
XLA Ops:
  0.6 0.0 copy-start.4
  0.6 0.0 copy-start
  0.7 0.0 copy-start.5
  0.7 0.0 copy-start.1
  0.7 3.1 %collective-permute-start.3 = (f32[3,4,544]{2,1,0:T(4,128)}, f32[3,4,544]{2,1,0:T(4,128)S(1)}, u32[]{:S(2)}, u32[]{:S(2)}) collective-permute-start(f32[3,4,544]{2,1,0:T(4,128)} %refs_0_.1), channel_id=1, source_target_pairs={{0,4},{1,5},{2,6},{3,7},{4,0},{5,1},{6,2},{7,3},{8,12},{9,13},{10,... | collective-permute-start | bytes 78344 | tf_op jit(solution)/shard_map/ppermute | solution.py:503
  3.7 1.5 %collective-permute-start.1 = (f32[3,4,544]{2,1,0:T(4,128)}, f32[3,4,544]{2,1,0:T(4,128)S(1)}, u32[]{:S(2)}, u32[]{:S(2)}) collective-permute-start(f32[3,4,544]{2,1,0:T(4,128)} %refs_0_.1), channel_id=1, source_target_pairs={{0,2},{1,3},{2,0},{3,1},{4,6},{5,7},{6,4},{7,5},{8,10},{9,11},{10,... | collective-permute-start | bytes 78344 | tf_op jit(solution)/shard_map/ppermute | solution.py:503
  5.2 0.0 collective-permute-start
  5.2 0.0 collective-permute-start.5
  5.3 0.5 %collective-permute-done.3.refs_4_ = f32[3,4,544]{2,1,0:T(4,128)S(1)} collective-permute-done((f32[3,4,544]{2,1,0:T(4,128)}, f32[3,4,544]{2,1,0:T(4,128)S(1)}, u32[]{:S(2)}, u32[]{:S(2)}) %collective-permute-start.3) | collective-permute-done | bytes 26144 | tf_op jit(solution)/shard_map/ppermute | solution.py:503
  5.8 0.0 collective-permute-start.4
  5.8 2.0 %collective-permute-done.1.refs_2_ = f32[3,4,544]{2,1,0:T(4,128)S(1)} collective-permute-done((f32[3,4,544]{2,1,0:T(4,128)}, f32[3,4,544]{2,1,0:T(4,128)S(1)}, u32[]{:S(2)}, u32[]{:S(2)}) %collective-permute-start.1) | collective-permute-done | bytes 26144 | tf_op jit(solution)/shard_map/ppermute | solution.py:503
  7.8 0.0 collective-permute-start.2
  7.8 2.4 %collective-permute-done.5.refs_6_ = f32[3,4,544]{2,1,0:T(4,128)S(1)} collective-permute-done((f32[3,4,544]{2,1,0:T(4,128)}, f32[3,4,544]{2,1,0:T(4,128)S(1)}, u32[]{:S(2)}, u32[]{:S(2)}) %collective-permute-start.5) | collective-permute-done | bytes 26144 | tf_op jit(solution)/shard_map/ppermute | solution.py:503
  10.2 0.0 collective-permute-start.6
  10.2 0.0 copy-done.4
  10.2 0.0 copy-done
  10.2 0.0 copy-done.5
  10.2 0.0 copy-done.1
  10.3 0.0 copy-start.7
  10.3 0.0 copy-start.8
  10.3 0.0 copy-start.9
  10.3 1.4 %shard_map.123 = f32[32,4,128]{2,1,0:T(4,128)} custom-call(f32[8,128]{1,0:T(8,128)S(1)} %shard_map.122.blank_ref, f32[3,4,544]{2,1,0:T(4,128)S(1)} %copy-done.4, f32[3,544]{1,0:T(4,128)S(1)} %copy-done.5, f32[152,544]{1,0:T(8,128)S(1)} %bitcast.1, f32[544,544]{1,0:T(8,128)S(1)} %copy-done), custom_call_target="tpu_custom_call" | custom-call | flops 1000000000 | bytes 1000000 | tf_op jit(solution)/shard_map/pallas_call | solution.py:522
  11.6 4.2 %all-to-all-start = ((f32[32,4,128]{2,1,0:T(4,128)}), f32[32,4,128]{2,1,0:T(4,128)S(1)}, u32[]{:S(2)}, u32[]{:S(2)}) async-start(f32[32,4,128]{2,1,0:T(4,128)} %shard_map.123), calls=%async_computation | async-start | bytes 131072 | tf_op jit(solution)/shard_map/all_to_all | solution.py:518
  16.5 0.0 copy-start.2
  16.5 0.0 copy-start.3
  16.5 0.0 copy-start.6
  16.5 0.0 collective-permute-done.refs_1_
  16.5 0.0 collective-permute-done.4.refs_5_
  16.5 0.0 collective-permute-done.2.refs_3_
  16.5 0.0 collective-permute-done.6.refs_7_
  16.5 0.0 copy-done.7
  16.5 0.0 copy-done.8
  16.6 0.0 copy-done.9
  16.6 3.1 %shard_map.124.partial_ref = f32[3,4,544]{2,1,0:T(4,128)S(1)} custom-call(s32[1,2]{1,0:T(1,128)S(1)} %copy-done.7, s32[1,2]{1,0:T(1,128)S(1)} %copy-done.8, s32[1,2]{1,0:T(1,128)S(1)} %copy-done.9, s32[1]{0:T(128)S(6)} %copy.13.count_ref, f32[3,4,544]{2,1,0:T(4,128)S(1)} %copy-done.4, f32[3,4,544]{2,1,0:T(4,128)S(1)} %copy-done.4, ...), custom_call_target="tpu_custom_call" | custom-call | flops 4000000000 | bytes 1000000 | tf_op jit(solution)/shard_map/pallas_call | solution.py:485
  19.7 3.5 %all-to-all-done.told_ref = f32[32,4,128]{2,1,0:T(4,128)S(1)} async-done(((f32[32,4,128]{2,1,0:T(4,128)}), f32[32,4,128]{2,1,0:T(4,128)S(1)}, u32[]{:S(2)}, u32[]{:S(2)}) %all-to-all-start) | async-done | bytes 65568 | tf_op jit(solution)/shard_map/all_to_all | solution.py:518
  23.2 0.0 copy-done.2
  23.2 0.0 copy-done.3
  23.2 0.0 copy-done.6
  23.2 3.2 %shard_map.125 = (f32[3,4,544]{2,1,0:T(4,128)S(1)}, f32[32,4,128]{2,1,0:T(4,128)}) custom-call(f32[32,4,128]{2,1,0:T(4,128)S(1)} %all-to-all-done.told_ref, f32[3,4,544]{2,1,0:T(4,128)S(1)} %shard_map.124.partial_ref, f32[152,152]{1,0:T(8,128)S(1)} %copy-done.3, f32[3,152]{1,0:T(4,128)S(1)} %copy-done.6, f32[152,544]{1,0:T(8,128)S(1)} %copy-done.2, ...), custom_call_target="tpu_custom_call" | custom-call | flops 3000000000 | bytes 1000000 | tf_op jit(solution)/shard_map/pallas_call | solution.py:525
  26.5 0.7 %collective-permute-start.12 = (f32[3,4,544]{2,1,0:T(4,128)S(1)}, f32[3,4,544]{2,1,0:T(4,128)S(1)}, u32[]{:S(2)}, u32[]{:S(2)}) collective-permute-start(f32[3,4,544]{2,1,0:T(4,128)S(1)} %get-tuple-element.5.points_ref.refs_0_), channel_id=1, source_target_pairs={{0,6},{1,7},{2,4},{3,5},{4,2},{5,3},{6,0},{7,1},{8,14},{9,15},{10,... | collective-permute-start | bytes 78344 | tf_op jit(solution)/shard_map/ppermute | solution.py:503
  27.2 1.2 %collective-permute-start.10 = (f32[3,4,544]{2,1,0:T(4,128)S(1)}, f32[3,4,544]{2,1,0:T(4,128)S(1)}, u32[]{:S(2)}, u32[]{:S(2)}) collective-permute-start(f32[3,4,544]{2,1,0:T(4,128)S(1)} %get-tuple-element.5.points_ref.refs_0_), channel_id=1, source_target_pairs={{0,4},{1,5},{2,6},{3,7},{4,0},{5,1},{6,2},{7,3},{8,12},{9,13},{10,... | collective-permute-start | bytes 78344 | tf_op jit(solution)/shard_map/ppermute | solution.py:503
  28.4 1.6 %collective-permute-start.8 = (f32[3,4,544]{2,1,0:T(4,128)S(1)}, f32[3,4,544]{2,1,0:T(4,128)S(1)}, u32[]{:S(2)}, u32[]{:S(2)}) collective-permute-start(f32[3,4,544]{2,1,0:T(4,128)S(1)} %get-tuple-element.5.points_ref.refs_0_), channel_id=1, source_target_pairs={{0,2},{1,3},{2,0},{3,1},{4,6},{5,7},{6,4},{7,5},{8,10},{9,11},{10,... | collective-permute-start | bytes 78344 | tf_op jit(solution)/shard_map/ppermute | solution.py:503
  29.9 0.0 collective-permute-start.7
  29.9 1.4 %collective-permute-done.12.refs_6_ = f32[3,4,544]{2,1,0:T(4,128)S(1)} collective-permute-done((f32[3,4,544]{2,1,0:T(4,128)S(1)}, f32[3,4,544]{2,1,0:T(4,128)S(1)}, u32[]{:S(2)}, u32[]{:S(2)}) %collective-permute-start.12) | collective-permute-done | bytes 26144 | tf_op jit(solution)/shard_map/ppermute | solution.py:503
  31.4 0.0 collective-permute-start.13
  31.4 0.0 collective-permute-done.10.refs_4_
  31.4 0.5 %collective-permute-start.11 = (f32[3,4,544]{2,1,0:T(4,128)S(1)}, f32[3,4,544]{2,1,0:T(4,128)S(1)}, u32[]{:S(2)}, u32[]{:S(2)}) collective-permute-start(f32[3,4,544]{2,1,0:T(4,128)S(1)} %collective-permute-done.10.refs_4_), channel_id=1, source_target_pairs={{0,1},{1,0},{2,3},{3,2},{4,5},{5,4},{6,7},{7,6},{8,9},{9,8},{10,11... | collective-permute-start | bytes 78344 | tf_op jit(solution)/shard_map/ppermute | solution.py:503
  31.9 0.3 collective-permute-done.8.refs_2_
  32.2 0.0 collective-permute-start.9
  32.2 2.6 %all-to-all-start.1 = ((f32[32,4,128]{2,1,0:T(4,128)}), f32[32,4,128]{2,1,0:T(4,128)S(1)}, u32[]{:S(2)}, u32[]{:S(2)}) async-start(f32[32,4,128]{2,1,0:T(4,128)} %get-tuple-element.4), calls=%async_computation.1 | async-start | bytes 131072 | tf_op jit(solution)/shard_map/all_to_all | solution.py:518
  34.8 0.0 collective-permute-done.7.refs_1_
  34.8 0.0 collective-permute-done.13.refs_7_
  34.8 0.0 collective-permute-done.11.refs_5_
  34.9 0.0 collective-permute-done.9.refs_3_
  34.9 3.1 %shard_map.126.near_ref = f32[3,4,544]{2,1,0:T(4,128)S(1)} custom-call(s32[1,2]{1,0:T(1,128)S(1)} %copy-done.7, s32[1,2]{1,0:T(1,128)S(1)} %copy-done.8, s32[1,2]{1,0:T(1,128)S(1)} %copy-done.9, s32[1]{0:T(128)S(6)} %copy.13.count_ref, f32[3,4,544]{2,1,0:T(4,128)S(1)} %get-tuple-element.5.points_ref.refs_0_, ...), custom_call_target="tpu_custom_call" | custom-call | flops 4000000000 | bytes 1000000 | tf_op jit(solution)/shard_map/pallas_call | solution.py:485
  38.0 4.3 %all-to-all-done.1.told_ref = f32[32,4,128]{2,1,0:T(4,128)S(1)} async-done(((f32[32,4,128]{2,1,0:T(4,128)}), f32[32,4,128]{2,1,0:T(4,128)S(1)}, u32[]{:S(2)}, u32[]{:S(2)}) %all-to-all-start.1) | async-done | bytes 65568 | tf_op jit(solution)/shard_map/all_to_all | solution.py:518
  42.2 2.5 %shard_map.127 = (f32[3,4,544]{2,1,0:T(4,128)}, f32[3,4,544]{2,1,0:T(4,128)}) custom-call(f32[32,4,128]{2,1,0:T(4,128)S(1)} %all-to-all-done.1.told_ref, f32[3,4,544]{2,1,0:T(4,128)S(1)} %get-tuple-element.5.points_ref.refs_0_, f32[3,4,544]{2,1,0:T(4,128)S(1)} %shard_map.126.near_ref, f32[152,152]{1,0:T(8,128)S(1)} %copy-done.3, f32[3,152]{1,0:T(4,128)S(1)} %copy-done.6, ...), custom_call_target="tpu_custom_call" | custom-call | flops 3000000000 | bytes 1000000 | tf_op jit(solution)/shard_map/pallas_call | solution.py:531
  (1 shorter events, 0.0 us)
Async XLA Ops:
  0.6 9.6 %copy-start.4 = (f32[3,4,544]{2,1,0:T(4,128)S(1)}, f32[3,4,544]{2,1,0:T(4,128)}, u32[]{:S(2)}) copy-start(f32[3,4,544]{2,1,0:T(4,128)} %refs_0_.1) | copy-start | bytes 78340
  0.6 9.6 %copy-start = (f32[544,544]{1,0:T(8,128)S(1)}, f32[544,544]{1,0:T(8,128)}, u32[]{:S(2)}) copy-start(f32[544,544]{1,0:T(8,128)} %refs_9_.3) | copy-start | bytes 3551236
  0.7 9.6 %copy-start.5 = (f32[3,544]{1,0:T(4,128)S(1)}, f32[3,544]{1,0:T(4,128)}, u32[]{:S(2)}) copy-start(f32[3,544]{1,0:T(4,128)} %refs_8_.3) | copy-start | bytes 19588
  0.7 9.6 %copy-start.1 = (f32[544,152]{0,1:T(8,128)S(1)}, f32[544,152]{0,1:T(8,128)}, u32[]{:S(2)}) copy-start(f32[544,152]{0,1:T(8,128)} %param.14) | copy-start | bytes 992260
  0.7 5.1 %collective-permute-start.3 = (f32[3,4,544]{2,1,0:T(4,128)}, f32[3,4,544]{2,1,0:T(4,128)S(1)}, u32[]{:S(2)}, u32[]{:S(2)}) collective-permute-start(f32[3,4,544]{2,1,0:T(4,128)} %refs_0_.1), channel_id=1, source_target_pairs={{0,4},{1,5},{2,6},{3,7},{4,0},{5,1},{6,2},{7,3},{8,12},{9,13},{10,... | collective-permute-start | bytes 78344 | tf_op jit(solution)/shard_map/ppermute | solution.py:503
  3.7 4.1 %collective-permute-start.1 = (f32[3,4,544]{2,1,0:T(4,128)}, f32[3,4,544]{2,1,0:T(4,128)S(1)}, u32[]{:S(2)}, u32[]{:S(2)}) collective-permute-start(f32[3,4,544]{2,1,0:T(4,128)} %refs_0_.1), channel_id=1, source_target_pairs={{0,2},{1,3},{2,0},{3,1},{4,6},{5,7},{6,4},{7,5},{8,10},{9,11},{10,... | collective-permute-start | bytes 78344 | tf_op jit(solution)/shard_map/ppermute | solution.py:503
  5.2 11.3 %collective-permute-start = (f32[3,4,544]{2,1,0:T(4,128)}, f32[3,4,544]{2,1,0:T(4,128)S(1)}, u32[]{:S(2)}, u32[]{:S(2)}) collective-permute-start(f32[3,4,544]{2,1,0:T(4,128)} %refs_0_.1), channel_id=1, source_target_pairs={{0,1},{1,0},{2,3},{3,2},{4,5},{5,4},{6,7},{7,6},{8,9},{9,8},{10,11... | collective-permute-start | bytes 78344 | tf_op jit(solution)/shard_map/ppermute | solution.py:503
  5.2 5.0 %collective-permute-start.5 = (f32[3,4,544]{2,1,0:T(4,128)}, f32[3,4,544]{2,1,0:T(4,128)S(1)}, u32[]{:S(2)}, u32[]{:S(2)}) collective-permute-start(f32[3,4,544]{2,1,0:T(4,128)} %refs_0_.1), channel_id=1, source_target_pairs={{0,6},{1,7},{2,4},{3,5},{4,2},{5,3},{6,0},{7,1},{8,14},{9,15},{10,... | collective-permute-start | bytes 78344 | tf_op jit(solution)/shard_map/ppermute | solution.py:503
  5.8 10.7 %collective-permute-start.4 = (f32[3,4,544]{2,1,0:T(4,128)S(1)}, f32[3,4,544]{2,1,0:T(4,128)S(1)}, u32[]{:S(2)}, u32[]{:S(2)}) collective-permute-start(f32[3,4,544]{2,1,0:T(4,128)S(1)} %collective-permute-done.3.refs_4_), channel_id=1, source_target_pairs={{0,1},{1,0},{2,3},{3,2},{4,5},{5,4},{6,7},{7,6},{8,9},{9,8},{10,11... | collective-permute-start | bytes 78344 | tf_op jit(solution)/shard_map/ppermute | solution.py:503
  7.8 8.7 %collective-permute-start.2 = (f32[3,4,544]{2,1,0:T(4,128)S(1)}, f32[3,4,544]{2,1,0:T(4,128)S(1)}, u32[]{:S(2)}, u32[]{:S(2)}) collective-permute-start(f32[3,4,544]{2,1,0:T(4,128)S(1)} %collective-permute-done.1.refs_2_), channel_id=1, source_target_pairs={{0,1},{1,0},{2,3},{3,2},{4,5},{5,4},{6,7},{7,6},{8,9},{9,8},{10,11... | collective-permute-start | bytes 78344 | tf_op jit(solution)/shard_map/ppermute | solution.py:503
  10.2 6.3 %collective-permute-start.6 = (f32[3,4,544]{2,1,0:T(4,128)S(1)}, f32[3,4,544]{2,1,0:T(4,128)S(1)}, u32[]{:S(2)}, u32[]{:S(2)}) collective-permute-start(f32[3,4,544]{2,1,0:T(4,128)S(1)} %collective-permute-done.5.refs_6_), channel_id=1, source_target_pairs={{0,1},{1,0},{2,3},{3,2},{4,5},{5,4},{6,7},{7,6},{8,9},{9,8},{10,11... | collective-permute-start | bytes 78344 | tf_op jit(solution)/shard_map/ppermute | solution.py:503
  10.3 6.3 %copy-start.7 = (s32[1,2]{1,0:T(1,128)S(1)}, s32[1,2]{1,0:T(1,128)}, u32[]{:S(2)}) copy-start(s32[1,2]{1,0:T(1,128)} %target_ref.3) | copy-start | bytes 28
  10.3 6.3 %copy-start.8 = (s32[1,2]{1,0:T(1,128)S(1)}, s32[1,2]{1,0:T(1,128)}, u32[]{:S(2)}) copy-start(s32[1,2]{1,0:T(1,128)} %owner_ref.3) | copy-start | bytes 28
  10.3 6.3 %copy-start.9 = (s32[1,2]{1,0:T(1,128)S(1)}, s32[1,2]{1,0:T(1,128)}, u32[]{:S(2)}) copy-start(s32[1,2]{1,0:T(1,128)} %cell_ref.3) | copy-start | bytes 28
  11.6 11.6 %all-to-all-start = ((f32[32,4,128]{2,1,0:T(4,128)}), f32[32,4,128]{2,1,0:T(4,128)S(1)}, u32[]{:S(2)}, u32[]{:S(2)}) async-start(f32[32,4,128]{2,1,0:T(4,128)} %shard_map.123), calls=%async_computation | async-start | bytes 131072 | tf_op jit(solution)/shard_map/all_to_all | solution.py:518
  16.5 6.8 %copy-start.2 = (f32[152,544]{1,0:T(8,128)S(1)}, f32[152,544]{1,0:T(8,128)}, u32[]{:S(2)}) copy-start(f32[152,544]{1,0:T(8,128)} %down_ref.3) | copy-start | bytes 992260
  16.5 6.8 %copy-start.3 = (f32[152,152]{1,0:T(8,128)S(1)}, f32[152,152]{1,0:T(8,128)}, u32[]{:S(2)}) copy-start(f32[152,152]{1,0:T(8,128)} %m2m_ref.3) | copy-start | bytes 277252
  16.5 6.7 %copy-start.6 = (f32[3,152]{1,0:T(4,128)S(1)}, f32[3,152]{1,0:T(4,128)}, u32[]{:S(2)}) copy-start(f32[3,152]{1,0:T(4,128)} %template_ref.3) | copy-start | bytes 5476
  26.5 4.9 %collective-permute-start.12 = (f32[3,4,544]{2,1,0:T(4,128)S(1)}, f32[3,4,544]{2,1,0:T(4,128)S(1)}, u32[]{:S(2)}, u32[]{:S(2)}) collective-permute-start(f32[3,4,544]{2,1,0:T(4,128)S(1)} %get-tuple-element.5.points_ref.refs_0_), channel_id=1, source_target_pairs={{0,6},{1,7},{2,4},{3,5},{4,2},{5,3},{6,0},{7,1},{8,14},{9,15},{10,... | collective-permute-start | bytes 78344 | tf_op jit(solution)/shard_map/ppermute | solution.py:503
  27.2 4.2 %collective-permute-start.10 = (f32[3,4,544]{2,1,0:T(4,128)S(1)}, f32[3,4,544]{2,1,0:T(4,128)S(1)}, u32[]{:S(2)}, u32[]{:S(2)}) collective-permute-start(f32[3,4,544]{2,1,0:T(4,128)S(1)} %get-tuple-element.5.points_ref.refs_0_), channel_id=1, source_target_pairs={{0,4},{1,5},{2,6},{3,7},{4,0},{5,1},{6,2},{7,3},{8,12},{9,13},{10,... | collective-permute-start | bytes 78344 | tf_op jit(solution)/shard_map/ppermute | solution.py:503
  28.4 3.9 %collective-permute-start.8 = (f32[3,4,544]{2,1,0:T(4,128)S(1)}, f32[3,4,544]{2,1,0:T(4,128)S(1)}, u32[]{:S(2)}, u32[]{:S(2)}) collective-permute-start(f32[3,4,544]{2,1,0:T(4,128)S(1)} %get-tuple-element.5.points_ref.refs_0_), channel_id=1, source_target_pairs={{0,2},{1,3},{2,0},{3,1},{4,6},{5,7},{6,4},{7,5},{8,10},{9,11},{10,... | collective-permute-start | bytes 78344 | tf_op jit(solution)/shard_map/ppermute | solution.py:503
  29.9 4.9 %collective-permute-start.7 = (f32[3,4,544]{2,1,0:T(4,128)S(1)}, f32[3,4,544]{2,1,0:T(4,128)S(1)}, u32[]{:S(2)}, u32[]{:S(2)}) collective-permute-start(f32[3,4,544]{2,1,0:T(4,128)S(1)} %get-tuple-element.5.points_ref.refs_0_), channel_id=1, source_target_pairs={{0,1},{1,0},{2,3},{3,2},{4,5},{5,4},{6,7},{7,6},{8,9},{9,8},{10,11... | collective-permute-start | bytes 78344 | tf_op jit(solution)/shard_map/ppermute | solution.py:503
  31.4 3.4 %collective-permute-start.13 = (f32[3,4,544]{2,1,0:T(4,128)S(1)}, f32[3,4,544]{2,1,0:T(4,128)S(1)}, u32[]{:S(2)}, u32[]{:S(2)}) collective-permute-start(f32[3,4,544]{2,1,0:T(4,128)S(1)} %collective-permute-done.12.refs_6_), channel_id=1, source_target_pairs={{0,1},{1,0},{2,3},{3,2},{4,5},{5,4},{6,7},{7,6},{8,9},{9,8},{10,11... | collective-permute-start | bytes 78344 | tf_op jit(solution)/shard_map/ppermute | solution.py:503
  31.4 3.5 %collective-permute-start.11 = (f32[3,4,544]{2,1,0:T(4,128)S(1)}, f32[3,4,544]{2,1,0:T(4,128)S(1)}, u32[]{:S(2)}, u32[]{:S(2)}) collective-permute-start(f32[3,4,544]{2,1,0:T(4,128)S(1)} %collective-permute-done.10.refs_4_), channel_id=1, source_target_pairs={{0,1},{1,0},{2,3},{3,2},{4,5},{5,4},{6,7},{7,6},{8,9},{9,8},{10,11... | collective-permute-start | bytes 78344 | tf_op jit(solution)/shard_map/ppermute | solution.py:503
  32.2 2.6 %collective-permute-start.9 = (f32[3,4,544]{2,1,0:T(4,128)S(1)}, f32[3,4,544]{2,1,0:T(4,128)S(1)}, u32[]{:S(2)}, u32[]{:S(2)}) collective-permute-start(f32[3,4,544]{2,1,0:T(4,128)S(1)} %collective-permute-done.8.refs_2_), channel_id=1, source_target_pairs={{0,1},{1,0},{2,3},{3,2},{4,5},{5,4},{6,7},{7,6},{8,9},{9,8},{10,11... | collective-permute-start | bytes 78344 | tf_op jit(solution)/shard_map/ppermute | solution.py:503
  32.2 10.0 %all-to-all-start.1 = ((f32[32,4,128]{2,1,0:T(4,128)}), f32[32,4,128]{2,1,0:T(4,128)S(1)}, u32[]{:S(2)}, u32[]{:S(2)}) async-start(f32[32,4,128]{2,1,0:T(4,128)} %get-tuple-element.4), calls=%async_computation.1 | async-start | bytes 131072 | tf_op jit(solution)/shard_map/all_to_all | solution.py:518

commit v6 on v5

--- a/solution.py
+++ b/solution.py
@@ -20,7 +20,10 @@
 
 LANES = 128
 SUB = 8
-BATCH = 3
+BATCH = 1
+WIDTH = 128
+LAG = 1
+LEAD = 2
 
 
 def up8(n):
@@ -195,7 +198,7 @@
 
 
 def near_sums(target_ref, count_ref, points_ref, rest_ref, stiffness, rows_ref, move_ref):
-    cells, _ = points_ref.shape[1:]
+    cells, size = points_ref.shape[1:]
     sources = rows_ref[...]
     move_ref[...] = jnp.zeros_like(move_ref)
     for slot in range(NEAR):
@@ -205,7 +208,7 @@
     linear = dot3(move_ref[...], stiffness)
     square = linear * linear
     dot = functools.partial(jnp.dot, preferred_element_type=jnp.float32)
-    results = []
+    opened = []
     for slot in range(NEAR):
         part = linear[SUB * slot : SUB * slot + 3]
         stretch = jnp.sum(square[SUB * slot : SUB * slot + 3], axis=0, keepdims=True)
@@ -214,16 +217,32 @@
         center = jnp.mean(aim, axis=1, keepdims=True)
         aim = aim - center
         place = sources[SUB * slot : SUB * slot + 3] - center
-        near, along = source_rows(place, force)
-        near = jnp.transpose(stack_left(near)).astype(jnp.bfloat16)
-        along = jnp.transpose(stack_left(along)).astype(jnp.bfloat16)
+        near, along = (
+            jnp.transpose(stack_left(rows)).astype(jnp.bfloat16)
+            for rows in source_rows(place, force)
+        )
         right = stack_right(target_rows(aim)).astype(jnp.bfloat16)
-        forces = stack_pair(rows8([force]))
-        places = stack_pair(rows8([place, jnp.ones_like(place[:1])]))
-        both = weights(dot(near, right), dot(along, right))
-        direct = dot(twice(forces), jnp.concatenate(both[:2], axis=0))
-        moment = dot(twice(places), jnp.concatenate(both[2:], axis=0))
-        results.append(jnp.where(slot < count_ref[0], finish(aim, direct, moment), 0.0))
+        forces = twice(stack_pair(rows8([force])))
+        places = twice(stack_pair(rows8([place, jnp.ones_like(place[:1])])))
+        for lane in range(0, size, WIDTH):
+            part = slice(lane, min(lane + WIDTH, size))
+            opened.append((slot, aim[:, part], near, along, right[:, part], forces, places))
+    pairs = {}
+    results = [[] for _ in range(NEAR)]
+    for step in range(len(opened) + 1):
+        if step < len(opened):
+            _, _, near, along, right, _, _ = opened[step]
+            pairs[step] = dot(near, right), dot(along, right)
+        if step:
+            slot, aim, _, _, _, forces, places = opened[step - 1]
+            both = weights(*pairs.pop(step - 1))
+            direct = dot(forces, jnp.concatenate(both[:2], axis=0))
+            moment = dot(places, jnp.concatenate(both[2:], axis=0))
+            results[slot].append(finish(aim, direct, moment))
+    results = [
+        jnp.where(slot < count_ref[0], jnp.concatenate(results[slot], axis=1), 0.0)
+        for slot in range(NEAR)
+    ]
     rows = lax.broadcasted_iota(jnp.int32, (cells, 1), 0)
     return [
         sum(
@@ -345,19 +364,27 @@
     dot = functools.partial(jnp.dot, preferred_element_type=jnp.float32)
     direct = jnp.zeros((2 * SUB, tall), jnp.float32)
     moment = jnp.zeros((2 * SUB, tall), jnp.float32)
-    for row in range(0, source_ref.shape[0], BATCH):
-        block = jnp.concatenate([source_ref[row + i] for i in range(BATCH)], axis=1)
-        place = block[0:3]
-        force = block[3:6]
-        near, along = source_rows(place, force)
-        both = weights(
-            dot(left, stack_right(near).astype(jnp.bfloat16)),
-            dot(left, stack_right(along).astype(jnp.bfloat16)),
-        )
-        forces = stack_pair(rows8([force]))
-        places = stack_pair(rows8([place, jnp.ones_like(place[:1])]))
-        direct += contract(twice(forces), jnp.concatenate(both[:2], axis=1))
-        moment += contract(twice(places), jnp.concatenate(both[2:], axis=1))
+    count = source_ref.shape[0] // BATCH
+    opened, weighed = {}, {}
+    for step in range(count + LAG + LEAD):
+        if step < count:
+            block = jnp.concatenate(
+                [source_ref[step * BATCH + i] for i in range(BATCH)], axis=1
+            )
+            place, force = block[0:3], block[3:6]
+            opened[step] = place, force, *(
+                dot(left, stack_right(rows).astype(jnp.bfloat16))
+                for rows in source_rows(place, force)
+            )
+        if 0 <= step - LEAD < count:
+            place, force, *pair = opened.pop(step - LEAD)
+            weighed[step - LEAD] = place, force, weights(*pair)
+        if 0 <= step - LEAD - LAG < count:
+            place, force, both = weighed.pop(step - LEAD - LAG)
+            forces = stack_pair(rows8([force]))
+            places = stack_pair(rows8([place, jnp.ones_like(place[:1])]))
+            direct += contract(twice(forces), jnp.concatenate(both[:2], axis=1))
+            moment += contract(twice(places), jnp.concatenate(both[2:], axis=1))
     return finish(targets, direct, moment)[:, :q]
 
 

time: 45 us -> 44.3 us (0.984)
  Pallas kernels: 13.3 us -> 12.4 us
where the time goes in v6:
time: 44.3 us; the launch traced here: 44.1 us
  starting transfers between devices  15.3 us (35%)
  waiting for transfers between devices  14.8 us (33%)
  Pallas kernels  12.4 us (28%)
  between operations  1.51 us (3%)
    ppermute x14, starting transfers between devices, to(): return lax.ppermute(array, 'dev', [(j, j ^ mask) for j in range(devs)])  8.62 us
    all_to_all x2, waiting for transfers between devices, tell(): return lax.all_to_all(message, ('grp', 'dev'), 0, 0)  8.04 us
    ppermute x14, waiting for transfers between devices, to(): return lax.ppermute(array, 'dev', [(j, j ^ mask) for j in range(devs)])  6.75 us
    all_to_all x2, starting transfers between devices, tell(): return lax.all_to_all(message, ('grp', 'dev'), 0, 0)  6.72 us
    pallas_call x2, Pallas kernels, near(): return run(*lists, points, *pool, rest_shape, stiffness)[0]  5.97 us
    pallas_call x1, Pallas kernels, body(): turn(told, partial, m2m, box_template, down_map, rest_shape, up_rows, sti...  2.88 us
    pallas_call x1, Pallas kernels, body(): return last(told, points, close, m2m, box_template, down_map)  2.17 us
    pallas_call x1, Pallas kernels, body(): message, = first(empty, positions, rest_shape, up_rows, stiffness)  1.35 us
  transfers between devices with their start and end apart: 16, of which 7 were waited for; matrix products, arithmetic and copies ran while one was open for 0% of the time, Pallas kernels for 17%

profile of v6, /device:TPU:0, one launch (start us, length us, event | category | flops | bytes accessed | tf_op | source)
XLA Modules:
  0.0 44.1 jit_solution(11811583485422496026)
XLA Ops:
  0.6 0.0 copy-start.4
  0.6 0.0 copy-start
  0.7 0.0 copy-start.5
  0.7 0.0 copy-start.1
  0.7 3.1 %collective-permute-start.3 = (f32[3,4,544]{2,1,0:T(4,128)}, f32[3,4,544]{2,1,0:T(4,128)S(1)}, u32[]{:S(2)}, u32[]{:S(2)}) collective-permute-start(f32[3,4,544]{2,1,0:T(4,128)} %refs_0_.1), channel_id=1, source_target_pairs={{0,4},{1,5},{2,6},{3,7},{4,0},{5,1},{6,2},{7,3},{8,12},{9,13},{10,... | collective-permute-start | bytes 78344 | tf_op jit(solution)/shard_map/ppermute | solution.py:530
  3.7 1.5 %collective-permute-start.1 = (f32[3,4,544]{2,1,0:T(4,128)}, f32[3,4,544]{2,1,0:T(4,128)S(1)}, u32[]{:S(2)}, u32[]{:S(2)}) collective-permute-start(f32[3,4,544]{2,1,0:T(4,128)} %refs_0_.1), channel_id=1, source_target_pairs={{0,2},{1,3},{2,0},{3,1},{4,6},{5,7},{6,4},{7,5},{8,10},{9,11},{10,... | collective-permute-start | bytes 78344 | tf_op jit(solution)/shard_map/ppermute | solution.py:530
  5.2 0.0 collective-permute-start
  5.2 0.0 collective-permute-start.5
  5.3 0.5 %collective-permute-done.3.refs_4_ = f32[3,4,544]{2,1,0:T(4,128)S(1)} collective-permute-done((f32[3,4,544]{2,1,0:T(4,128)}, f32[3,4,544]{2,1,0:T(4,128)S(1)}, u32[]{:S(2)}, u32[]{:S(2)}) %collective-permute-start.3) | collective-permute-done | bytes 26144 | tf_op jit(solution)/shard_map/ppermute | solution.py:530
  5.8 0.0 collective-permute-start.4
  5.8 2.0 %collective-permute-done.1.refs_2_ = f32[3,4,544]{2,1,0:T(4,128)S(1)} collective-permute-done((f32[3,4,544]{2,1,0:T(4,128)}, f32[3,4,544]{2,1,0:T(4,128)S(1)}, u32[]{:S(2)}, u32[]{:S(2)}) %collective-permute-start.1) | collective-permute-done | bytes 26144 | tf_op jit(solution)/shard_map/ppermute | solution.py:530
  7.8 0.0 collective-permute-start.2
  7.8 2.4 %collective-permute-done.5.refs_6_ = f32[3,4,544]{2,1,0:T(4,128)S(1)} collective-permute-done((f32[3,4,544]{2,1,0:T(4,128)}, f32[3,4,544]{2,1,0:T(4,128)S(1)}, u32[]{:S(2)}, u32[]{:S(2)}) %collective-permute-start.5) | collective-permute-done | bytes 26144 | tf_op jit(solution)/shard_map/ppermute | solution.py:530
  10.2 0.0 collective-permute-start.6
  10.2 0.0 copy-done.4
  10.2 0.0 copy-done
  10.2 0.0 copy-done.5
  10.2 0.0 copy-done.1
  10.3 0.0 copy-start.7
  10.3 0.0 copy-start.8
  10.3 0.0 copy-start.9
  10.3 1.4 %shard_map.123 = f32[32,4,128]{2,1,0:T(4,128)} custom-call(f32[8,128]{1,0:T(8,128)S(1)} %shard_map.122.blank_ref, f32[3,4,544]{2,1,0:T(4,128)S(1)} %copy-done.4, f32[3,544]{1,0:T(4,128)S(1)} %copy-done.5, f32[152,544]{1,0:T(8,128)S(1)} %bitcast.1, f32[544,544]{1,0:T(8,128)S(1)} %copy-done), custom_call_target="tpu_custom_call" | custom-call | flops 1000000000 | bytes 1000000 | tf_op jit(solution)/shard_map/pallas_call | solution.py:549
  11.6 4.2 %all-to-all-start = ((f32[32,4,128]{2,1,0:T(4,128)}), f32[32,4,128]{2,1,0:T(4,128)S(1)}, u32[]{:S(2)}, u32[]{:S(2)}) async-start(f32[32,4,128]{2,1,0:T(4,128)} %shard_map.123), calls=%async_computation | async-start | bytes 131072 | tf_op jit(solution)/shard_map/all_to_all | solution.py:545
  16.5 0.0 copy-start.2
  16.5 0.0 copy-start.3
  16.5 0.0 copy-start.6
  16.5 0.0 collective-permute-done.refs_1_
  16.5 0.0 collective-permute-done.4.refs_5_
  16.5 0.0 collective-permute-done.2.refs_3_
  16.5 0.0 collective-permute-done.6.refs_7_
  16.5 0.0 copy-done.7
  16.5 0.0 copy-done.8
  16.6 0.0 copy-done.9
  16.6 3.0 %shard_map.124.partial_ref = f32[3,4,544]{2,1,0:T(4,128)S(1)} custom-call(s32[1,2]{1,0:T(1,128)S(1)} %copy-done.7, s32[1,2]{1,0:T(1,128)S(1)} %copy-done.8, s32[1,2]{1,0:T(1,128)S(1)} %copy-done.9, s32[1]{0:T(128)S(6)} %copy.13.count_ref, f32[3,4,544]{2,1,0:T(4,128)S(1)} %copy-done.4, f32[3,4,544]{2,1,0:T(4,128)S(1)} %copy-done.4, ...), custom_call_target="tpu_custom_call" | custom-call | flops 4000000000 | bytes 1000000 | tf_op jit(solution)/shard_map/pallas_call | solution.py:512
  19.6 3.7 %all-to-all-done.told_ref = f32[32,4,128]{2,1,0:T(4,128)S(1)} async-done(((f32[32,4,128]{2,1,0:T(4,128)}), f32[32,4,128]{2,1,0:T(4,128)S(1)}, u32[]{:S(2)}, u32[]{:S(2)}) %all-to-all-start) | async-done | bytes 65568 | tf_op jit(solution)/shard_map/all_to_all | solution.py:545
  23.2 0.0 copy-done.2
  23.2 0.0 copy-done.3
  23.2 0.0 copy-done.6
  23.2 2.9 %shard_map.125 = (f32[3,4,544]{2,1,0:T(4,128)S(1)}, f32[32,4,128]{2,1,0:T(4,128)}) custom-call(f32[32,4,128]{2,1,0:T(4,128)S(1)} %all-to-all-done.told_ref, f32[3,4,544]{2,1,0:T(4,128)S(1)} %shard_map.124.partial_ref, f32[152,152]{1,0:T(8,128)S(1)} %copy-done.3, f32[3,152]{1,0:T(4,128)S(1)} %copy-done.6, f32[152,544]{1,0:T(8,128)S(1)} %copy-done.2, ...), custom_call_target="tpu_custom_call" | custom-call | flops 3000000000 | bytes 1000000 | tf_op jit(solution)/shard_map/pallas_call | solution.py:552
  26.1 0.7 %collective-permute-start.12 = (f32[3,4,544]{2,1,0:T(4,128)S(1)}, f32[3,4,544]{2,1,0:T(4,128)S(1)}, u32[]{:S(2)}, u32[]{:S(2)}) collective-permute-start(f32[3,4,544]{2,1,0:T(4,128)S(1)} %get-tuple-element.5.points_ref.refs_0_), channel_id=1, source_target_pairs={{0,6},{1,7},{2,4},{3,5},{4,2},{5,3},{6,0},{7,1},{8,14},{9,15},{10,... | collective-permute-start | bytes 78344 | tf_op jit(solution)/shard_map/ppermute | solution.py:530
  26.8 1.2 %collective-permute-start.10 = (f32[3,4,544]{2,1,0:T(4,128)S(1)}, f32[3,4,544]{2,1,0:T(4,128)S(1)}, u32[]{:S(2)}, u32[]{:S(2)}) collective-permute-start(f32[3,4,544]{2,1,0:T(4,128)S(1)} %get-tuple-element.5.points_ref.refs_0_), channel_id=1, source_target_pairs={{0,4},{1,5},{2,6},{3,7},{4,0},{5,1},{6,2},{7,3},{8,12},{9,13},{10,... | collective-permute-start | bytes 78344 | tf_op jit(solution)/shard_map/ppermute | solution.py:530
  28.0 1.6 %collective-permute-start.8 = (f32[3,4,544]{2,1,0:T(4,128)S(1)}, f32[3,4,544]{2,1,0:T(4,128)S(1)}, u32[]{:S(2)}, u32[]{:S(2)}) collective-permute-start(f32[3,4,544]{2,1,0:T(4,128)S(1)} %get-tuple-element.5.points_ref.refs_0_), channel_id=1, source_target_pairs={{0,2},{1,3},{2,0},{3,1},{4,6},{5,7},{6,4},{7,5},{8,10},{9,11},{10,... | collective-permute-start | bytes 78344 | tf_op jit(solution)/shard_map/ppermute | solution.py:530
  29.6 0.0 collective-permute-start.7
  29.6 1.4 %collective-permute-done.12.refs_6_ = f32[3,4,544]{2,1,0:T(4,128)S(1)} collective-permute-done((f32[3,4,544]{2,1,0:T(4,128)S(1)}, f32[3,4,544]{2,1,0:T(4,128)S(1)}, u32[]{:S(2)}, u32[]{:S(2)}) %collective-permute-start.12) | collective-permute-done | bytes 26144 | tf_op jit(solution)/shard_map/ppermute | solution.py:530
  31.0 0.0 collective-permute-start.13
  31.1 0.0 collective-permute-done.10.refs_4_
  31.1 0.5 %collective-permute-start.11 = (f32[3,4,544]{2,1,0:T(4,128)S(1)}, f32[3,4,544]{2,1,0:T(4,128)S(1)}, u32[]{:S(2)}, u32[]{:S(2)}) collective-permute-start(f32[3,4,544]{2,1,0:T(4,128)S(1)} %collective-permute-done.10.refs_4_), channel_id=1, source_target_pairs={{0,1},{1,0},{2,3},{3,2},{4,5},{5,4},{6,7},{7,6},{8,9},{9,8},{10,11... | collective-permute-start | bytes 78344 | tf_op jit(solution)/shard_map/ppermute | solution.py:530
  31.6 0.3 collective-permute-done.8.refs_2_
  31.9 0.0 collective-permute-start.9
  31.9 2.6 %all-to-all-start.1 = ((f32[32,4,128]{2,1,0:T(4,128)}), f32[32,4,128]{2,1,0:T(4,128)S(1)}, u32[]{:S(2)}, u32[]{:S(2)}) async-start(f32[32,4,128]{2,1,0:T(4,128)} %get-tuple-element.4), calls=%async_computation.1 | async-start | bytes 131072 | tf_op jit(solution)/shard_map/all_to_all | solution.py:545
  34.5 0.0 collective-permute-done.7.refs_1_
  34.5 0.0 collective-permute-done.13.refs_7_
  34.5 0.0 collective-permute-done.11.refs_5_
  34.5 0.0 collective-permute-done.9.refs_3_
  34.5 3.0 %shard_map.126.near_ref = f32[3,4,544]{2,1,0:T(4,128)S(1)} custom-call(s32[1,2]{1,0:T(1,128)S(1)} %copy-done.7, s32[1,2]{1,0:T(1,128)S(1)} %copy-done.8, s32[1,2]{1,0:T(1,128)S(1)} %copy-done.9, s32[1]{0:T(128)S(6)} %copy.13.count_ref, f32[3,4,544]{2,1,0:T(4,128)S(1)} %get-tuple-element.5.points_ref.refs_0_, ...), custom_call_target="tpu_custom_call" | custom-call | flops 4000000000 | bytes 1000000 | tf_op jit(solution)/shard_map/pallas_call | solution.py:512
  37.5 4.4 %all-to-all-done.1.told_ref = f32[32,4,128]{2,1,0:T(4,128)S(1)} async-done(((f32[32,4,128]{2,1,0:T(4,128)}), f32[32,4,128]{2,1,0:T(4,128)S(1)}, u32[]{:S(2)}, u32[]{:S(2)}) %all-to-all-start.1) | async-done | bytes 65568 | tf_op jit(solution)/shard_map/all_to_all | solution.py:545
  41.9 2.2 %shard_map.127 = (f32[3,4,544]{2,1,0:T(4,128)}, f32[3,4,544]{2,1,0:T(4,128)}) custom-call(f32[32,4,128]{2,1,0:T(4,128)S(1)} %all-to-all-done.1.told_ref, f32[3,4,544]{2,1,0:T(4,128)S(1)} %get-tuple-element.5.points_ref.refs_0_, f32[3,4,544]{2,1,0:T(4,128)S(1)} %shard_map.126.near_ref, f32[152,152]{1,0:T(8,128)S(1)} %copy-done.3, f32[3,152]{1,0:T(4,128)S(1)} %copy-done.6, ...), custom_call_target="tpu_custom_call" | custom-call | flops 3000000000 | bytes 1000000 | tf_op jit(solution)/shard_map/pallas_call | solution.py:558
  (1 shorter events, 0.0 us)
Async XLA Ops:
  0.6 9.6 %copy-start.4 = (f32[3,4,544]{2,1,0:T(4,128)S(1)}, f32[3,4,544]{2,1,0:T(4,128)}, u32[]{:S(2)}) copy-start(f32[3,4,544]{2,1,0:T(4,128)} %refs_0_.1) | copy-start | bytes 78340
  0.6 9.6 %copy-start = (f32[544,544]{1,0:T(8,128)S(1)}, f32[544,544]{1,0:T(8,128)}, u32[]{:S(2)}) copy-start(f32[544,544]{1,0:T(8,128)} %refs_9_.3) | copy-start | bytes 3551236
  0.7 9.6 %copy-start.5 = (f32[3,544]{1,0:T(4,128)S(1)}, f32[3,544]{1,0:T(4,128)}, u32[]{:S(2)}) copy-start(f32[3,544]{1,0:T(4,128)} %refs_8_.3) | copy-start | bytes 19588
  0.7 9.6 %copy-start.1 = (f32[544,152]{0,1:T(8,128)S(1)}, f32[544,152]{0,1:T(8,128)}, u32[]{:S(2)}) copy-start(f32[544,152]{0,1:T(8,128)} %param.14) | copy-start | bytes 992260
  0.7 5.1 %collective-permute-start.3 = (f32[3,4,544]{2,1,0:T(4,128)}, f32[3,4,544]{2,1,0:T(4,128)S(1)}, u32[]{:S(2)}, u32[]{:S(2)}) collective-permute-start(f32[3,4,544]{2,1,0:T(4,128)} %refs_0_.1), channel_id=1, source_target_pairs={{0,4},{1,5},{2,6},{3,7},{4,0},{5,1},{6,2},{7,3},{8,12},{9,13},{10,... | collective-permute-start | bytes 78344 | tf_op jit(solution)/shard_map/ppermute | solution.py:530
  3.7 4.1 %collective-permute-start.1 = (f32[3,4,544]{2,1,0:T(4,128)}, f32[3,4,544]{2,1,0:T(4,128)S(1)}, u32[]{:S(2)}, u32[]{:S(2)}) collective-permute-start(f32[3,4,544]{2,1,0:T(4,128)} %refs_0_.1), channel_id=1, source_target_pairs={{0,2},{1,3},{2,0},{3,1},{4,6},{5,7},{6,4},{7,5},{8,10},{9,11},{10,... | collective-permute-start | bytes 78344 | tf_op jit(solution)/shard_map/ppermute | solution.py:530
  5.2 11.3 %collective-permute-start = (f32[3,4,544]{2,1,0:T(4,128)}, f32[3,4,544]{2,1,0:T(4,128)S(1)}, u32[]{:S(2)}, u32[]{:S(2)}) collective-permute-start(f32[3,4,544]{2,1,0:T(4,128)} %refs_0_.1), channel_id=1, source_target_pairs={{0,1},{1,0},{2,3},{3,2},{4,5},{5,4},{6,7},{7,6},{8,9},{9,8},{10,11... | collective-permute-start | bytes 78344 | tf_op jit(solution)/shard_map/ppermute | solution.py:530
  5.2 5.0 %collective-permute-start.5 = (f32[3,4,544]{2,1,0:T(4,128)}, f32[3,4,544]{2,1,0:T(4,128)S(1)}, u32[]{:S(2)}, u32[]{:S(2)}) collective-permute-start(f32[3,4,544]{2,1,0:T(4,128)} %refs_0_.1), channel_id=1, source_target_pairs={{0,6},{1,7},{2,4},{3,5},{4,2},{5,3},{6,0},{7,1},{8,14},{9,15},{10,... | collective-permute-start | bytes 78344 | tf_op jit(solution)/shard_map/ppermute | solution.py:530
  5.8 10.7 %collective-permute-start.4 = (f32[3,4,544]{2,1,0:T(4,128)S(1)}, f32[3,4,544]{2,1,0:T(4,128)S(1)}, u32[]{:S(2)}, u32[]{:S(2)}) collective-permute-start(f32[3,4,544]{2,1,0:T(4,128)S(1)} %collective-permute-done.3.refs_4_), channel_id=1, source_target_pairs={{0,1},{1,0},{2,3},{3,2},{4,5},{5,4},{6,7},{7,6},{8,9},{9,8},{10,11... | collective-permute-start | bytes 78344 | tf_op jit(solution)/shard_map/ppermute | solution.py:530
  7.8 8.7 %collective-permute-start.2 = (f32[3,4,544]{2,1,0:T(4,128)S(1)}, f32[3,4,544]{2,1,0:T(4,128)S(1)}, u32[]{:S(2)}, u32[]{:S(2)}) collective-permute-start(f32[3,4,544]{2,1,0:T(4,128)S(1)} %collective-permute-done.1.refs_2_), channel_id=1, source_target_pairs={{0,1},{1,0},{2,3},{3,2},{4,5},{5,4},{6,7},{7,6},{8,9},{9,8},{10,11... | collective-permute-start | bytes 78344 | tf_op jit(solution)/shard_map/ppermute | solution.py:530
  10.2 6.3 %collective-permute-start.6 = (f32[3,4,544]{2,1,0:T(4,128)S(1)}, f32[3,4,544]{2,1,0:T(4,128)S(1)}, u32[]{:S(2)}, u32[]{:S(2)}) collective-permute-start(f32[3,4,544]{2,1,0:T(4,128)S(1)} %collective-permute-done.5.refs_6_), channel_id=1, source_target_pairs={{0,1},{1,0},{2,3},{3,2},{4,5},{5,4},{6,7},{7,6},{8,9},{9,8},{10,11... | collective-permute-start | bytes 78344 | tf_op jit(solution)/shard_map/ppermute | solution.py:530
  10.3 6.3 %copy-start.7 = (s32[1,2]{1,0:T(1,128)S(1)}, s32[1,2]{1,0:T(1,128)}, u32[]{:S(2)}) copy-start(s32[1,2]{1,0:T(1,128)} %target_ref.3) | copy-start | bytes 28
  10.3 6.3 %copy-start.8 = (s32[1,2]{1,0:T(1,128)S(1)}, s32[1,2]{1,0:T(1,128)}, u32[]{:S(2)}) copy-start(s32[1,2]{1,0:T(1,128)} %owner_ref.3) | copy-start | bytes 28
  10.3 6.3 %copy-start.9 = (s32[1,2]{1,0:T(1,128)S(1)}, s32[1,2]{1,0:T(1,128)}, u32[]{:S(2)}) copy-start(s32[1,2]{1,0:T(1,128)} %cell_ref.3) | copy-start | bytes 28
  11.6 11.6 %all-to-all-start = ((f32[32,4,128]{2,1,0:T(4,128)}), f32[32,4,128]{2,1,0:T(4,128)S(1)}, u32[]{:S(2)}, u32[]{:S(2)}) async-start(f32[32,4,128]{2,1,0:T(4,128)} %shard_map.123), calls=%async_computation | async-start | bytes 131072 | tf_op jit(solution)/shard_map/all_to_all | solution.py:545
  16.5 6.8 %copy-start.2 = (f32[152,544]{1,0:T(8,128)S(1)}, f32[152,544]{1,0:T(8,128)}, u32[]{:S(2)}) copy-start(f32[152,544]{1,0:T(8,128)} %down_ref.3) | copy-start | bytes 992260
  16.5 6.8 %copy-start.3 = (f32[152,152]{1,0:T(8,128)S(1)}, f32[152,152]{1,0:T(8,128)}, u32[]{:S(2)}) copy-start(f32[152,152]{1,0:T(8,128)} %m2m_ref.3) | copy-start | bytes 277252
  16.5 6.7 %copy-start.6 = (f32[3,152]{1,0:T(4,128)S(1)}, f32[3,152]{1,0:T(4,128)}, u32[]{:S(2)}) copy-start(f32[3,152]{1,0:T(4,128)} %template_ref.3) | copy-start | bytes 5476
  26.1 4.9 %collective-permute-start.12 = (f32[3,4,544]{2,1,0:T(4,128)S(1)}, f32[3,4,544]{2,1,0:T(4,128)S(1)}, u32[]{:S(2)}, u32[]{:S(2)}) collective-permute-start(f32[3,4,544]{2,1,0:T(4,128)S(1)} %get-tuple-element.5.points_ref.refs_0_), channel_id=1, source_target_pairs={{0,6},{1,7},{2,4},{3,5},{4,2},{5,3},{6,0},{7,1},{8,14},{9,15},{10,... | collective-permute-start | bytes 78344 | tf_op jit(solution)/shard_map/ppermute | solution.py:530
  26.8 4.2 %collective-permute-start.10 = (f32[3,4,544]{2,1,0:T(4,128)S(1)}, f32[3,4,544]{2,1,0:T(4,128)S(1)}, u32[]{:S(2)}, u32[]{:S(2)}) collective-permute-start(f32[3,4,544]{2,1,0:T(4,128)S(1)} %get-tuple-element.5.points_ref.refs_0_), channel_id=1, source_target_pairs={{0,4},{1,5},{2,6},{3,7},{4,0},{5,1},{6,2},{7,3},{8,12},{9,13},{10,... | collective-permute-start | bytes 78344 | tf_op jit(solution)/shard_map/ppermute | solution.py:530
  28.0 3.9 %collective-permute-start.8 = (f32[3,4,544]{2,1,0:T(4,128)S(1)}, f32[3,4,544]{2,1,0:T(4,128)S(1)}, u32[]{:S(2)}, u32[]{:S(2)}) collective-permute-start(f32[3,4,544]{2,1,0:T(4,128)S(1)} %get-tuple-element.5.points_ref.refs_0_), channel_id=1, source_target_pairs={{0,2},{1,3},{2,0},{3,1},{4,6},{5,7},{6,4},{7,5},{8,10},{9,11},{10,... | collective-permute-start | bytes 78344 | tf_op jit(solution)/shard_map/ppermute | solution.py:530
  29.6 4.9 %collective-permute-start.7 = (f32[3,4,544]{2,1,0:T(4,128)S(1)}, f32[3,4,544]{2,1,0:T(4,128)S(1)}, u32[]{:S(2)}, u32[]{:S(2)}) collective-permute-start(f32[3,4,544]{2,1,0:T(4,128)S(1)} %get-tuple-element.5.points_ref.refs_0_), channel_id=1, source_target_pairs={{0,1},{1,0},{2,3},{3,2},{4,5},{5,4},{6,7},{7,6},{8,9},{9,8},{10,11... | collective-permute-start | bytes 78344 | tf_op jit(solution)/shard_map/ppermute | solution.py:530
  31.0 3.4 %collective-permute-start.13 = (f32[3,4,544]{2,1,0:T(4,128)S(1)}, f32[3,4,544]{2,1,0:T(4,128)S(1)}, u32[]{:S(2)}, u32[]{:S(2)}) collective-permute-start(f32[3,4,544]{2,1,0:T(4,128)S(1)} %collective-permute-done.12.refs_6_), channel_id=1, source_target_pairs={{0,1},{1,0},{2,3},{3,2},{4,5},{5,4},{6,7},{7,6},{8,9},{9,8},{10,11... | collective-permute-start | bytes 78344 | tf_op jit(solution)/shard_map/ppermute | solution.py:530
  31.1 3.4 %collective-permute-start.11 = (f32[3,4,544]{2,1,0:T(4,128)S(1)}, f32[3,4,544]{2,1,0:T(4,128)S(1)}, u32[]{:S(2)}, u32[]{:S(2)}) collective-permute-start(f32[3,4,544]{2,1,0:T(4,128)S(1)} %collective-permute-done.10.refs_4_), channel_id=1, source_target_pairs={{0,1},{1,0},{2,3},{3,2},{4,5},{5,4},{6,7},{7,6},{8,9},{9,8},{10,11... | collective-permute-start | bytes 78344 | tf_op jit(solution)/shard_map/ppermute | solution.py:530
  31.9 2.6 %collective-permute-start.9 = (f32[3,4,544]{2,1,0:T(4,128)S(1)}, f32[3,4,544]{2,1,0:T(4,128)S(1)}, u32[]{:S(2)}, u32[]{:S(2)}) collective-permute-start(f32[3,4,544]{2,1,0:T(4,128)S(1)} %collective-permute-done.8.refs_2_), channel_id=1, source_target_pairs={{0,1},{1,0},{2,3},{3,2},{4,5},{5,4},{6,7},{7,6},{8,9},{9,8},{10,11... | collective-permute-start | bytes 78344 | tf_op jit(solution)/shard_map/ppermute | solution.py:530
  31.9 10.0 %all-to-all-start.1 = ((f32[32,4,128]{2,1,0:T(4,128)}), f32[32,4,128]{2,1,0:T(4,128)S(1)}, u32[]{:S(2)}, u32[]{:S(2)}) async-start(f32[32,4,128]{2,1,0:T(4,128)} %get-tuple-element.4), calls=%async_computation.1 | async-start | bytes 131072 | tf_op jit(solution)/shard_map/all_to_all | solution.py:545

commit v7 on v6

--- a/solution.py
+++ b/solution.py
@@ -20,10 +20,10 @@
 
 LANES = 128
 SUB = 8
-BATCH = 1
+BATCH = 2
 WIDTH = 128
 LAG = 1
-LEAD = 2
+LEAD = 1
 
 
 def up8(n):
@@ -184,12 +184,12 @@
         cell = cell_ref[0, slot]
         owner = owner_ref[0, slot]
         if spread:
-            for mask, pool_ref in enumerate(pool_refs):
-
-                @pl.when((owner ^ me) == mask)
-                def _(pool_ref=pool_ref):
-                    for k in range(3):
-                        rows_ref[SUB * slot + k : SUB * slot + k + 1, :] = pick(pool_ref[k], cell)
+            place = owner ^ me
+            for k in range(3):
+                chosen = pool_refs[0][k]
+                for mask in range(1, len(pool_refs)):
+                    chosen = jnp.where(place == mask, pool_refs[mask][k], chosen)
+                rows_ref[SUB * slot + k : SUB * slot + k + 1, :] = pick(chosen, cell)
         else:
             for k in range(3):
                 rows_ref[SUB * slot + k : SUB * slot + k + 1, :] = pick(

time: 44.3 us -> 44.3 us (level)
  transfers between devices with their start and end apart: 16 -> 16, of which waited for: 7 -> 7; matrix products, arithmetic and copies ran while one was open for 0% -> 0% of each run, Pallas kernels for 17% -> 16%
where the time goes in v7:
time: 44.3 us; the launch traced here: 44.1 us
  starting transfers between devices  15.3 us (35%)
  waiting for transfers between devices  14.9 us (34%)
  Pallas kernels  12.2 us (28%)
  between operations  1.51 us (3%)
    ppermute x14, starting transfers between devices, to(): return lax.ppermute(array, 'dev', [(j, j ^ mask) for j in range(devs)])  8.62 us
    all_to_all x2, waiting for transfers between devices, tell(): return lax.all_to_all(message, ('grp', 'dev'), 0, 0)  8.16 us
    ppermute x14, waiting for transfers between devices, to(): return lax.ppermute(array, 'dev', [(j, j ^ mask) for j in range(devs)])  6.74 us
    all_to_all x2, starting transfers between devices, tell(): return lax.all_to_all(message, ('grp', 'dev'), 0, 0)  6.72 us
    pallas_call x2, Pallas kernels, near(): return run(*lists, points, *pool, rest_shape, stiffness)[0]  5.85 us
    pallas_call x1, Pallas kernels, body(): turn(told, partial, m2m, box_template, down_map, rest_shape, up_rows, sti...  2.88 us
    pallas_call x1, Pallas kernels, body(): return last(told, points, close, m2m, box_template, down_map)  2.17 us
    pallas_call x1, Pallas kernels, body(): message, = first(empty, positions, rest_shape, up_rows, stiffness)  1.35 us
  transfers between devices with their start and end apart: 16, of which 7 were waited for; matrix products, arithmetic and copies ran while one was open for 0% of the time, Pallas kernels for 16%

profile of v7, /device:TPU:0, one launch (start us, length us, event | category | flops | bytes accessed | tf_op | source)
XLA Modules:
  0.0 44.1 jit_solution(15679818691414952015)
XLA Ops:
  0.6 0.0 copy-start.4
  0.6 0.0 copy-start
  0.7 0.0 copy-start.5
  0.7 0.0 copy-start.1
  0.7 3.1 %collective-permute-start.3 = (f32[3,4,544]{2,1,0:T(4,128)}, f32[3,4,544]{2,1,0:T(4,128)S(1)}, u32[]{:S(2)}, u32[]{:S(2)}) collective-permute-start(f32[3,4,544]{2,1,0:T(4,128)} %refs_0_.1), channel_id=1, source_target_pairs={{0,4},{1,5},{2,6},{3,7},{4,0},{5,1},{6,2},{7,3},{8,12},{9,13},{10,... | collective-permute-start | bytes 78344 | tf_op jit(solution)/shard_map/ppermute | solution.py:530
  3.7 1.5 %collective-permute-start.1 = (f32[3,4,544]{2,1,0:T(4,128)}, f32[3,4,544]{2,1,0:T(4,128)S(1)}, u32[]{:S(2)}, u32[]{:S(2)}) collective-permute-start(f32[3,4,544]{2,1,0:T(4,128)} %refs_0_.1), channel_id=1, source_target_pairs={{0,2},{1,3},{2,0},{3,1},{4,6},{5,7},{6,4},{7,5},{8,10},{9,11},{10,... | collective-permute-start | bytes 78344 | tf_op jit(solution)/shard_map/ppermute | solution.py:530
  5.2 0.0 collective-permute-start
  5.2 0.0 collective-permute-start.5
  5.3 0.5 %collective-permute-done.3.refs_4_ = f32[3,4,544]{2,1,0:T(4,128)S(1)} collective-permute-done((f32[3,4,544]{2,1,0:T(4,128)}, f32[3,4,544]{2,1,0:T(4,128)S(1)}, u32[]{:S(2)}, u32[]{:S(2)}) %collective-permute-start.3) | collective-permute-done | bytes 26144 | tf_op jit(solution)/shard_map/ppermute | solution.py:530
  5.8 0.0 collective-permute-start.4
  5.8 2.0 %collective-permute-done.1.refs_2_ = f32[3,4,544]{2,1,0:T(4,128)S(1)} collective-permute-done((f32[3,4,544]{2,1,0:T(4,128)}, f32[3,4,544]{2,1,0:T(4,128)S(1)}, u32[]{:S(2)}, u32[]{:S(2)}) %collective-permute-start.1) | collective-permute-done | bytes 26144 | tf_op jit(solution)/shard_map/ppermute | solution.py:530
  7.8 0.0 collective-permute-start.2
  7.8 2.4 %collective-permute-done.5.refs_6_ = f32[3,4,544]{2,1,0:T(4,128)S(1)} collective-permute-done((f32[3,4,544]{2,1,0:T(4,128)}, f32[3,4,544]{2,1,0:T(4,128)S(1)}, u32[]{:S(2)}, u32[]{:S(2)}) %collective-permute-start.5) | collective-permute-done | bytes 26144 | tf_op jit(solution)/shard_map/ppermute | solution.py:530
  10.2 0.0 collective-permute-start.6
  10.2 0.0 copy-done.4
  10.2 0.0 copy-done
  10.2 0.0 copy-done.5
  10.2 0.0 copy-done.1
  10.3 0.0 copy-start.7
  10.3 0.0 copy-start.8
  10.3 0.0 copy-start.9
  10.3 1.4 %shard_map.123 = f32[32,4,128]{2,1,0:T(4,128)} custom-call(f32[8,128]{1,0:T(8,128)S(1)} %shard_map.122.blank_ref, f32[3,4,544]{2,1,0:T(4,128)S(1)} %copy-done.4, f32[3,544]{1,0:T(4,128)S(1)} %copy-done.5, f32[152,544]{1,0:T(8,128)S(1)} %bitcast.1, f32[544,544]{1,0:T(8,128)S(1)} %copy-done), custom_call_target="tpu_custom_call" | custom-call | flops 1000000000 | bytes 1000000 | tf_op jit(solution)/shard_map/pallas_call | solution.py:549
  11.6 4.2 %all-to-all-start = ((f32[32,4,128]{2,1,0:T(4,128)}), f32[32,4,128]{2,1,0:T(4,128)S(1)}, u32[]{:S(2)}, u32[]{:S(2)}) async-start(f32[32,4,128]{2,1,0:T(4,128)} %shard_map.123), calls=%async_computation | async-start | bytes 131072 | tf_op jit(solution)/shard_map/all_to_all | solution.py:545
  16.5 0.0 copy-start.2
  16.5 0.0 copy-start.3
  16.5 0.0 copy-start.6
  16.5 0.0 collective-permute-done.refs_1_
  16.5 0.0 collective-permute-done.4.refs_5_
  16.5 0.0 collective-permute-done.2.refs_3_
  16.5 0.0 collective-permute-done.6.refs_7_
  16.5 0.0 copy-done.7
  16.5 0.0 copy-done.8
  16.6 0.0 copy-done.9
  16.6 2.9 %shard_map.124.partial_ref = f32[3,4,544]{2,1,0:T(4,128)S(1)} custom-call(s32[1,2]{1,0:T(1,128)S(1)} %copy-done.7, s32[1,2]{1,0:T(1,128)S(1)} %copy-done.8, s32[1,2]{1,0:T(1,128)S(1)} %copy-done.9, s32[1]{0:T(128)S(6)} %copy.13.count_ref, f32[3,4,544]{2,1,0:T(4,128)S(1)} %copy-done.4, f32[3,4,544]{2,1,0:T(4,128)S(1)} %copy-done.4, ...), custom_call_target="tpu_custom_call" | custom-call | flops 4000000000 | bytes 1000000 | tf_op jit(solution)/shard_map/pallas_call | solution.py:512
  19.5 3.7 %all-to-all-done.told_ref = f32[32,4,128]{2,1,0:T(4,128)S(1)} async-done(((f32[32,4,128]{2,1,0:T(4,128)}), f32[32,4,128]{2,1,0:T(4,128)S(1)}, u32[]{:S(2)}, u32[]{:S(2)}) %all-to-all-start) | async-done | bytes 65568 | tf_op jit(solution)/shard_map/all_to_all | solution.py:545
  23.2 0.0 copy-done.2
  23.2 0.0 copy-done.3
  23.2 0.0 copy-done.6
  23.2 2.9 %shard_map.125 = (f32[3,4,544]{2,1,0:T(4,128)S(1)}, f32[32,4,128]{2,1,0:T(4,128)}) custom-call(f32[32,4,128]{2,1,0:T(4,128)S(1)} %all-to-all-done.told_ref, f32[3,4,544]{2,1,0:T(4,128)S(1)} %shard_map.124.partial_ref, f32[152,152]{1,0:T(8,128)S(1)} %copy-done.3, f32[3,152]{1,0:T(4,128)S(1)} %copy-done.6, f32[152,544]{1,0:T(8,128)S(1)} %copy-done.2, ...), custom_call_target="tpu_custom_call" | custom-call | flops 3000000000 | bytes 1000000 | tf_op jit(solution)/shard_map/pallas_call | solution.py:552
  26.1 0.7 %collective-permute-start.12 = (f32[3,4,544]{2,1,0:T(4,128)S(1)}, f32[3,4,544]{2,1,0:T(4,128)S(1)}, u32[]{:S(2)}, u32[]{:S(2)}) collective-permute-start(f32[3,4,544]{2,1,0:T(4,128)S(1)} %get-tuple-element.5.points_ref.refs_0_), channel_id=1, source_target_pairs={{0,6},{1,7},{2,4},{3,5},{4,2},{5,3},{6,0},{7,1},{8,14},{9,15},{10,... | collective-permute-start | bytes 78344 | tf_op jit(solution)/shard_map/ppermute | solution.py:530
  26.8 1.2 %collective-permute-start.10 = (f32[3,4,544]{2,1,0:T(4,128)S(1)}, f32[3,4,544]{2,1,0:T(4,128)S(1)}, u32[]{:S(2)}, u32[]{:S(2)}) collective-permute-start(f32[3,4,544]{2,1,0:T(4,128)S(1)} %get-tuple-element.5.points_ref.refs_0_), channel_id=1, source_target_pairs={{0,4},{1,5},{2,6},{3,7},{4,0},{5,1},{6,2},{7,3},{8,12},{9,13},{10,... | collective-permute-start | bytes 78344 | tf_op jit(solution)/shard_map/ppermute | solution.py:530
  28.0 1.6 %collective-permute-start.8 = (f32[3,4,544]{2,1,0:T(4,128)S(1)}, f32[3,4,544]{2,1,0:T(4,128)S(1)}, u32[]{:S(2)}, u32[]{:S(2)}) collective-permute-start(f32[3,4,544]{2,1,0:T(4,128)S(1)} %get-tuple-element.5.points_ref.refs_0_), channel_id=1, source_target_pairs={{0,2},{1,3},{2,0},{3,1},{4,6},{5,7},{6,4},{7,5},{8,10},{9,11},{10,... | collective-permute-start | bytes 78344 | tf_op jit(solution)/shard_map/ppermute | solution.py:530
  29.6 0.0 collective-permute-start.7
  29.6 1.4 %collective-permute-done.12.refs_6_ = f32[3,4,544]{2,1,0:T(4,128)S(1)} collective-permute-done((f32[3,4,544]{2,1,0:T(4,128)S(1)}, f32[3,4,544]{2,1,0:T(4,128)S(1)}, u32[]{:S(2)}, u32[]{:S(2)}) %collective-permute-start.12) | collective-permute-done | bytes 26144 | tf_op jit(solution)/shard_map/ppermute | solution.py:530
  31.1 0.0 collective-permute-start.13
  31.1 0.0 collective-permute-done.10.refs_4_
  31.1 0.5 %collective-permute-start.11 = (f32[3,4,544]{2,1,0:T(4,128)S(1)}, f32[3,4,544]{2,1,0:T(4,128)S(1)}, u32[]{:S(2)}, u32[]{:S(2)}) collective-permute-start(f32[3,4,544]{2,1,0:T(4,128)S(1)} %collective-permute-done.10.refs_4_), channel_id=1, source_target_pairs={{0,1},{1,0},{2,3},{3,2},{4,5},{5,4},{6,7},{7,6},{8,9},{9,8},{10,11... | collective-permute-start | bytes 78344 | tf_op jit(solution)/shard_map/ppermute | solution.py:530
  31.6 0.3 collective-permute-done.8.refs_2_
  31.9 0.0 collective-permute-start.9
  31.9 2.6 %all-to-all-start.1 = ((f32[32,4,128]{2,1,0:T(4,128)}), f32[32,4,128]{2,1,0:T(4,128)S(1)}, u32[]{:S(2)}, u32[]{:S(2)}) async-start(f32[32,4,128]{2,1,0:T(4,128)} %get-tuple-element.4), calls=%async_computation.1 | async-start | bytes 131072 | tf_op jit(solution)/shard_map/all_to_all | solution.py:545
  34.5 0.0 collective-permute-done.7.refs_1_
  34.5 0.0 collective-permute-done.13.refs_7_
  34.5 0.0 collective-permute-done.11.refs_5_
  34.5 0.0 collective-permute-done.9.refs_3_
  34.5 2.9 %shard_map.126.near_ref = f32[3,4,544]{2,1,0:T(4,128)S(1)} custom-call(s32[1,2]{1,0:T(1,128)S(1)} %copy-done.7, s32[1,2]{1,0:T(1,128)S(1)} %copy-done.8, s32[1,2]{1,0:T(1,128)S(1)} %copy-done.9, s32[1]{0:T(128)S(6)} %copy.13.count_ref, f32[3,4,544]{2,1,0:T(4,128)S(1)} %get-tuple-element.5.points_ref.refs_0_, ...), custom_call_target="tpu_custom_call" | custom-call | flops 4000000000 | bytes 1000000 | tf_op jit(solution)/shard_map/pallas_call | solution.py:512
  37.4 4.4 %all-to-all-done.1.told_ref = f32[32,4,128]{2,1,0:T(4,128)S(1)} async-done(((f32[32,4,128]{2,1,0:T(4,128)}), f32[32,4,128]{2,1,0:T(4,128)S(1)}, u32[]{:S(2)}, u32[]{:S(2)}) %all-to-all-start.1) | async-done | bytes 65568 | tf_op jit(solution)/shard_map/all_to_all | solution.py:545
  41.9 2.2 %shard_map.127 = (f32[3,4,544]{2,1,0:T(4,128)}, f32[3,4,544]{2,1,0:T(4,128)}) custom-call(f32[32,4,128]{2,1,0:T(4,128)S(1)} %all-to-all-done.1.told_ref, f32[3,4,544]{2,1,0:T(4,128)S(1)} %get-tuple-element.5.points_ref.refs_0_, f32[3,4,544]{2,1,0:T(4,128)S(1)} %shard_map.126.near_ref, f32[152,152]{1,0:T(8,128)S(1)} %copy-done.3, f32[3,152]{1,0:T(4,128)S(1)} %copy-done.6, ...), custom_call_target="tpu_custom_call" | custom-call | flops 3000000000 | bytes 1000000 | tf_op jit(solution)/shard_map/pallas_call | solution.py:558
  (1 shorter events, 0.0 us)
Async XLA Ops:
  0.6 9.6 %copy-start.4 = (f32[3,4,544]{2,1,0:T(4,128)S(1)}, f32[3,4,544]{2,1,0:T(4,128)}, u32[]{:S(2)}) copy-start(f32[3,4,544]{2,1,0:T(4,128)} %refs_0_.1) | copy-start | bytes 78340
  0.6 9.6 %copy-start = (f32[544,544]{1,0:T(8,128)S(1)}, f32[544,544]{1,0:T(8,128)}, u32[]{:S(2)}) copy-start(f32[544,544]{1,0:T(8,128)} %refs_9_.3) | copy-start | bytes 3551236
  0.7 9.6 %copy-start.5 = (f32[3,544]{1,0:T(4,128)S(1)}, f32[3,544]{1,0:T(4,128)}, u32[]{:S(2)}) copy-start(f32[3,544]{1,0:T(4,128)} %refs_8_.3) | copy-start | bytes 19588
  0.7 9.6 %copy-start.1 = (f32[544,152]{0,1:T(8,128)S(1)}, f32[544,152]{0,1:T(8,128)}, u32[]{:S(2)}) copy-start(f32[544,152]{0,1:T(8,128)} %param.14) | copy-start | bytes 992260
  0.7 5.1 %collective-permute-start.3 = (f32[3,4,544]{2,1,0:T(4,128)}, f32[3,4,544]{2,1,0:T(4,128)S(1)}, u32[]{:S(2)}, u32[]{:S(2)}) collective-permute-start(f32[3,4,544]{2,1,0:T(4,128)} %refs_0_.1), channel_id=1, source_target_pairs={{0,4},{1,5},{2,6},{3,7},{4,0},{5,1},{6,2},{7,3},{8,12},{9,13},{10,... | collective-permute-start | bytes 78344 | tf_op jit(solution)/shard_map/ppermute | solution.py:530
  3.7 4.1 %collective-permute-start.1 = (f32[3,4,544]{2,1,0:T(4,128)}, f32[3,4,544]{2,1,0:T(4,128)S(1)}, u32[]{:S(2)}, u32[]{:S(2)}) collective-permute-start(f32[3,4,544]{2,1,0:T(4,128)} %refs_0_.1), channel_id=1, source_target_pairs={{0,2},{1,3},{2,0},{3,1},{4,6},{5,7},{6,4},{7,5},{8,10},{9,11},{10,... | collective-permute-start | bytes 78344 | tf_op jit(solution)/shard_map/ppermute | solution.py:530
  5.2 11.3 %collective-permute-start = (f32[3,4,544]{2,1,0:T(4,128)}, f32[3,4,544]{2,1,0:T(4,128)S(1)}, u32[]{:S(2)}, u32[]{:S(2)}) collective-permute-start(f32[3,4,544]{2,1,0:T(4,128)} %refs_0_.1), channel_id=1, source_target_pairs={{0,1},{1,0},{2,3},{3,2},{4,5},{5,4},{6,7},{7,6},{8,9},{9,8},{10,11... | collective-permute-start | bytes 78344 | tf_op jit(solution)/shard_map/ppermute | solution.py:530
  5.2 5.0 %collective-permute-start.5 = (f32[3,4,544]{2,1,0:T(4,128)}, f32[3,4,544]{2,1,0:T(4,128)S(1)}, u32[]{:S(2)}, u32[]{:S(2)}) collective-permute-start(f32[3,4,544]{2,1,0:T(4,128)} %refs_0_.1), channel_id=1, source_target_pairs={{0,6},{1,7},{2,4},{3,5},{4,2},{5,3},{6,0},{7,1},{8,14},{9,15},{10,... | collective-permute-start | bytes 78344 | tf_op jit(solution)/shard_map/ppermute | solution.py:530
  5.8 10.7 %collective-permute-start.4 = (f32[3,4,544]{2,1,0:T(4,128)S(1)}, f32[3,4,544]{2,1,0:T(4,128)S(1)}, u32[]{:S(2)}, u32[]{:S(2)}) collective-permute-start(f32[3,4,544]{2,1,0:T(4,128)S(1)} %collective-permute-done.3.refs_4_), channel_id=1, source_target_pairs={{0,1},{1,0},{2,3},{3,2},{4,5},{5,4},{6,7},{7,6},{8,9},{9,8},{10,11... | collective-permute-start | bytes 78344 | tf_op jit(solution)/shard_map/ppermute | solution.py:530
  7.8 8.7 %collective-permute-start.2 = (f32[3,4,544]{2,1,0:T(4,128)S(1)}, f32[3,4,544]{2,1,0:T(4,128)S(1)}, u32[]{:S(2)}, u32[]{:S(2)}) collective-permute-start(f32[3,4,544]{2,1,0:T(4,128)S(1)} %collective-permute-done.1.refs_2_), channel_id=1, source_target_pairs={{0,1},{1,0},{2,3},{3,2},{4,5},{5,4},{6,7},{7,6},{8,9},{9,8},{10,11... | collective-permute-start | bytes 78344 | tf_op jit(solution)/shard_map/ppermute | solution.py:530
  10.2 6.3 %collective-permute-start.6 = (f32[3,4,544]{2,1,0:T(4,128)S(1)}, f32[3,4,544]{2,1,0:T(4,128)S(1)}, u32[]{:S(2)}, u32[]{:S(2)}) collective-permute-start(f32[3,4,544]{2,1,0:T(4,128)S(1)} %collective-permute-done.5.refs_6_), channel_id=1, source_target_pairs={{0,1},{1,0},{2,3},{3,2},{4,5},{5,4},{6,7},{7,6},{8,9},{9,8},{10,11... | collective-permute-start | bytes 78344 | tf_op jit(solution)/shard_map/ppermute | solution.py:530
  10.3 6.3 %copy-start.7 = (s32[1,2]{1,0:T(1,128)S(1)}, s32[1,2]{1,0:T(1,128)}, u32[]{:S(2)}) copy-start(s32[1,2]{1,0:T(1,128)} %target_ref.3) | copy-start | bytes 28
  10.3 6.3 %copy-start.8 = (s32[1,2]{1,0:T(1,128)S(1)}, s32[1,2]{1,0:T(1,128)}, u32[]{:S(2)}) copy-start(s32[1,2]{1,0:T(1,128)} %owner_ref.3) | copy-start | bytes 28
  10.3 6.3 %copy-start.9 = (s32[1,2]{1,0:T(1,128)S(1)}, s32[1,2]{1,0:T(1,128)}, u32[]{:S(2)}) copy-start(s32[1,2]{1,0:T(1,128)} %cell_ref.3) | copy-start | bytes 28
  11.6 11.6 %all-to-all-start = ((f32[32,4,128]{2,1,0:T(4,128)}), f32[32,4,128]{2,1,0:T(4,128)S(1)}, u32[]{:S(2)}, u32[]{:S(2)}) async-start(f32[32,4,128]{2,1,0:T(4,128)} %shard_map.123), calls=%async_computation | async-start | bytes 131072 | tf_op jit(solution)/shard_map/all_to_all | solution.py:545
  16.5 6.8 %copy-start.2 = (f32[152,544]{1,0:T(8,128)S(1)}, f32[152,544]{1,0:T(8,128)}, u32[]{:S(2)}) copy-start(f32[152,544]{1,0:T(8,128)} %down_ref.3) | copy-start | bytes 992260
  16.5 6.8 %copy-start.3 = (f32[152,152]{1,0:T(8,128)S(1)}, f32[152,152]{1,0:T(8,128)}, u32[]{:S(2)}) copy-start(f32[152,152]{1,0:T(8,128)} %m2m_ref.3) | copy-start | bytes 277252
  16.5 6.7 %copy-start.6 = (f32[3,152]{1,0:T(4,128)S(1)}, f32[3,152]{1,0:T(4,128)}, u32[]{:S(2)}) copy-start(f32[3,152]{1,0:T(4,128)} %template_ref.3) | copy-start | bytes 5476
  26.1 4.9 %collective-permute-start.12 = (f32[3,4,544]{2,1,0:T(4,128)S(1)}, f32[3,4,544]{2,1,0:T(4,128)S(1)}, u32[]{:S(2)}, u32[]{:S(2)}) collective-permute-start(f32[3,4,544]{2,1,0:T(4,128)S(1)} %get-tuple-element.5.points_ref.refs_0_), channel_id=1, source_target_pairs={{0,6},{1,7},{2,4},{3,5},{4,2},{5,3},{6,0},{7,1},{8,14},{9,15},{10,... | collective-permute-start | bytes 78344 | tf_op jit(solution)/shard_map/ppermute | solution.py:530
  26.8 4.2 %collective-permute-start.10 = (f32[3,4,544]{2,1,0:T(4,128)S(1)}, f32[3,4,544]{2,1,0:T(4,128)S(1)}, u32[]{:S(2)}, u32[]{:S(2)}) collective-permute-start(f32[3,4,544]{2,1,0:T(4,128)S(1)} %get-tuple-element.5.points_ref.refs_0_), channel_id=1, source_target_pairs={{0,4},{1,5},{2,6},{3,7},{4,0},{5,1},{6,2},{7,3},{8,12},{9,13},{10,... | collective-permute-start | bytes 78344 | tf_op jit(solution)/shard_map/ppermute | solution.py:530
  28.0 3.9 %collective-permute-start.8 = (f32[3,4,544]{2,1,0:T(4,128)S(1)}, f32[3,4,544]{2,1,0:T(4,128)S(1)}, u32[]{:S(2)}, u32[]{:S(2)}) collective-permute-start(f32[3,4,544]{2,1,0:T(4,128)S(1)} %get-tuple-element.5.points_ref.refs_0_), channel_id=1, source_target_pairs={{0,2},{1,3},{2,0},{3,1},{4,6},{5,7},{6,4},{7,5},{8,10},{9,11},{10,... | collective-permute-start | bytes 78344 | tf_op jit(solution)/shard_map/ppermute | solution.py:530
  29.6 4.9 %collective-permute-start.7 = (f32[3,4,544]{2,1,0:T(4,128)S(1)}, f32[3,4,544]{2,1,0:T(4,128)S(1)}, u32[]{:S(2)}, u32[]{:S(2)}) collective-permute-start(f32[3,4,544]{2,1,0:T(4,128)S(1)} %get-tuple-element.5.points_ref.refs_0_), channel_id=1, source_target_pairs={{0,1},{1,0},{2,3},{3,2},{4,5},{5,4},{6,7},{7,6},{8,9},{9,8},{10,11... | collective-permute-start | bytes 78344 | tf_op jit(solution)/shard_map/ppermute | solution.py:530
  31.1 3.4 %collective-permute-start.13 = (f32[3,4,544]{2,1,0:T(4,128)S(1)}, f32[3,4,544]{2,1,0:T(4,128)S(1)}, u32[]{:S(2)}, u32[]{:S(2)}) collective-permute-start(f32[3,4,544]{2,1,0:T(4,128)S(1)} %collective-permute-done.12.refs_6_), channel_id=1, source_target_pairs={{0,1},{1,0},{2,3},{3,2},{4,5},{5,4},{6,7},{7,6},{8,9},{9,8},{10,11... | collective-permute-start | bytes 78344 | tf_op jit(solution)/shard_map/ppermute | solution.py:530
  31.1 3.4 %collective-permute-start.11 = (f32[3,4,544]{2,1,0:T(4,128)S(1)}, f32[3,4,544]{2,1,0:T(4,128)S(1)}, u32[]{:S(2)}, u32[]{:S(2)}) collective-permute-start(f32[3,4,544]{2,1,0:T(4,128)S(1)} %collective-permute-done.10.refs_4_), channel_id=1, source_target_pairs={{0,1},{1,0},{2,3},{3,2},{4,5},{5,4},{6,7},{7,6},{8,9},{9,8},{10,11... | collective-permute-start | bytes 78344 | tf_op jit(solution)/shard_map/ppermute | solution.py:530
  31.9 2.6 %collective-permute-start.9 = (f32[3,4,544]{2,1,0:T(4,128)S(1)}, f32[3,4,544]{2,1,0:T(4,128)S(1)}, u32[]{:S(2)}, u32[]{:S(2)}) collective-permute-start(f32[3,4,544]{2,1,0:T(4,128)S(1)} %collective-permute-done.8.refs_2_), channel_id=1, source_target_pairs={{0,1},{1,0},{2,3},{3,2},{4,5},{5,4},{6,7},{7,6},{8,9},{9,8},{10,11... | collective-permute-start | bytes 78344 | tf_op jit(solution)/shard_map/ppermute | solution.py:530
  31.9 10.0 %all-to-all-start.1 = ((f32[32,4,128]{2,1,0:T(4,128)}), f32[32,4,128]{2,1,0:T(4,128)S(1)}, u32[]{:S(2)}, u32[]{:S(2)}) async-start(f32[32,4,128]{2,1,0:T(4,128)} %get-tuple-element.4), calls=%async_computation.1 | async-start | bytes 131072 | tf_op jit(solution)/shard_map/all_to_all | solution.py:545
